TPU v7x, 128 devices: a whole 4x4x4 slice. The times are simulated.
128 devices in a mesh: row: 8 (over y, core), col: 16 (over z, x).
Axes of the slice: x: 4, y: 4, z: 4, core: 2. Of those that a mesh axis runs over, the one named last changes fastest.
Arguments:
- shot_boxes: int32 [4, 8, 16384], P(None, 'row', 'col'), may hold values from 0 to 512, as said below
- block_counts: int32 [8, 16], P('row'), may hold values from 1 to 8, 64 in all within a row
- tail_shots: int32 [8, 16], P('row'), may hold values from 1 to 128
- doses: float32 [8, 16384], P('row', 'col'), may hold values from 0.5 to 1.5
- pixel_gain: float32 [4096, 8192], P('row', 'col'), may hold values from 0.6 to 1.6
Outputs:
- corrected: float32 [8, 16384], P('row', 'col')
- exposure: float32 [8, 16384], P('row', 'col')
Inputs may be any that keep to these rules, and one draw needn't show every extreme that they name: `shot_boxes`: every shot has 8 <= x1 - x0 <= 64 and 8 <= y1 - y0 <= 64, inside its tile of 512 pixels. `block_counts`: in every tile row the block counts sum to exactly 64, and some tile of the row has 8.
All inputs are finite; a program needn't handle non-finite values.
Results may differ from a plain program's by a relative error of at most 0.0003.
Values sent between devices are 32-bit elements; how exact they have to be, the bound alone decides.
No kernel may reach another device: no remote copies, remote signals or barrier semaphores. Data moves between devices by JAX's collectives and lax.ppermute only.
A program may use at most 64 MiB of HBM per device.

v0:
```python
import math

import jax
import jax.numpy as jnp
from jax import lax
from jax.sharding import PartitionSpec as P

TILE = 512
CG = 128
BLK = 128
ITERS = 3
CELL = 4
BETA = 16
REACH = 32


FORWARD_RANGE = 4.0
BACK_RATIO = 0.75
TARGET_LEVEL = 1.0
EXACT_MODE = lax.Precision.HIGHEST


def with_halo(block, sides, width):
    for axis, dim in sides:
        count = lax.axis_size(axis)
        forward = [(i, i + 1) for i in range(count - 1)]
        backward = [(target, source) for source, target in forward]
        low = lax.ppermute(
            lax.slice_in_dim(block, block.shape[dim] - width, None, axis=dim), axis, forward
        )
        high = lax.ppermute(lax.slice_in_dim(block, 0, width, axis=dim), axis, backward)
        block = jnp.concatenate([low, block, high], axis=dim)
    return block


def edge_term(doubled, low_edge, high_edge):
    middle = doubled.astype(jnp.float32)[None, :] * 0.5
    low_side = low_edge.astype(jnp.float32)[:, None]
    high_side = high_edge.astype(jnp.float32)[:, None]
    return 0.5 * (
        jax.scipy.special.erf((middle - low_side) / FORWARD_RANGE)
        - jax.scipy.special.erf((middle - high_side) / FORWARD_RANGE)
    )


def pair_kernel(sources, centres):
    return edge_term(centres[0], sources[0], sources[2]) * edge_term(
        centres[1], sources[1], sources[3]
    )


def intersection(low_edge, high_edge):
    cell_edges = jnp.arange(CG, dtype=jnp.int32) * CELL
    covered = jnp.minimum(high_edge[:, None], cell_edges[None, :] + CELL) - jnp.maximum(
        low_edge[:, None], cell_edges[None, :]
    )
    return jnp.maximum(covered, 0).astype(jnp.float32) / CELL


def spread(distance):
    scaled = distance.astype(jnp.float32) / BETA
    inside = jnp.abs(distance) <= REACH
    return jnp.where(inside, jnp.exp(-scaled * scaled) / (math.sqrt(math.pi) * BETA), 0.0)


def body(shot_boxes, block_counts, tail_shots, doses, pixel_gain):
    shot_box = shot_boxes[:, 0, :]
    slot_count = shot_box.shape[1]
    col_count = lax.axis_size("col")
    col_index = lax.axis_index("col")
    peer_ids = jnp.arange(col_count, dtype=jnp.int32)
    blocks_row = block_counts[0]
    totals = (blocks_row - 1) * BLK + tail_shots[0]
    my_total = jnp.sum(jnp.where(peer_ids == col_index, totals, 0))
    is_live = jnp.arange(slot_count, dtype=jnp.int32) < my_total
    shot_dose = jnp.where(is_live, doses[0], 0.0)
    centres = jnp.stack([shot_box[0] + shot_box[2], shot_box[1] + shot_box[3]])
    cell_ids = centres[1] // (2 * CELL) * CG + centres[0] // (2 * CELL)
    pixel_ids = centres[1] // 2 * TILE + centres[0] // 2
    sensitive = pixel_gain.reshape(-1)[pixel_ids]
    across = intersection(shot_box[0], shot_box[2])
    downward = intersection(shot_box[1], shot_box[3])
    kernel = pair_kernel(shot_box, centres)
    local_cells = jnp.arange(CG, dtype=jnp.int32)
    padded_cells = jnp.arange(CG + 2 * REACH, dtype=jnp.int32)
    band_weights = spread(local_cells[:, None] + REACH - padded_cells[None, :])
    exposure = jnp.zeros_like(shot_dose)
    for sweep in range(ITERS):
        forward = jnp.dot(shot_dose, kernel, precision=EXACT_MODE)
        coarse = jnp.dot(downward.T, shot_dose[:, None] * across, precision=EXACT_MODE)
        tall_map = with_halo(coarse, (("row", 0),), REACH)
        blurred = jnp.dot(band_weights, tall_map, precision=EXACT_MODE)
        broad_map = with_halo(blurred, (("col", 1),), REACH)
        background = jnp.dot(broad_map, band_weights.T, precision=EXACT_MODE)
        sampled = background.reshape(-1)[cell_ids]
        exposure = sensitive * (forward + BACK_RATIO * sampled) / (1.0 + BACK_RATIO)
        shot_dose = jnp.where(
            is_live, shot_dose * TARGET_LEVEL / jnp.where(is_live, exposure, 1.0), 0.0
        )
    return (shot_dose[None, :], jnp.where(is_live, exposure, 0.0)[None, :])


def solution(mesh):
    placed = (
        P(None, "row", "col"),
        P("row", None),
        P("row", None),
        P("row", "col"),
        P("row", "col"),
    )
    return jax.shard_map(
        body,
        mesh=mesh,
        in_specs=placed,
        out_specs=(P("row", "col"), P("row", "col")),
        check_vma=False,
    )
```

profile of v0, /device:TPU:62, one launch (start us, length us, event | category | flops | bytes accessed | tf_op | source)
XLA Modules:
  0.0 97.2 jit_solution(5653501333357320513)
XLA Ops:
  0.6 0.0 copy-start.1
  0.7 0.7 fusion.163
  1.4 1.4 %fusion.113 = s32[]{:T(128)} fusion(s32[1,16]{1,0:T(1,128)} %param.7, s32[1,16]{1,0:T(1,128)} %param.6, s32[]{:T(128)S(6)} %axis_index.12), kind=kLoop, calls=%fused_computation.152 | loop fusion | flops 95 | bytes 136 | tf_op jit(solution)/shard_map/reduce_sum | solution.py:74
  2.8 1.4 %broadcast_multiply_fusion.2 = (f32[1024]{0:T(1024)S(1)}, f32[1024]{0:T(1024)S(1)}) fusion(f32[1024]{0:T(1024)} %bitcast.89, s32[]{:T(128)} %fusion.113), kind=kLoop, calls=%fused_computation.150 | loop fusion | flops 3072 | bytes 12292 | tf_op jit(solution)/shard_map/mul | solution.py:90
  4.2 1.8 %fusion.7 = f32[128,128]{1,0:T(8,128)S(1)} fusion(f32[1024]{0:T(1024)S(1)} %get-tuple-element.6, s32[1024]{0:T(1024)S(1)} %bitcast.64, s32[1024]{0:T(1024)S(1)} %bitcast.79, s32[128]{0:T(128)S(1)} %get-tuple-element.30, s32[1024]{0:T(1024)S(1)} %bitcast.74, s32[128]{0:T(128)S(1)} %get-tuple-element.31, s32[1024]{0:T(1024)S(1)} %bitcast.69), kind=kOutput, calls=%fused_computation.17 | convolution fusion | flops 202899456 | bytes 87040 | tf_op jit(solution)/shard_map/dot_general | solution.py:90
  6.0 2.1 %collective-permute-start.1 = (f32[32,128]{1,0:T(8,128)S(1)}, f32[32,128]{1,0:T(8,128)S(1)}, u32[]{:S(2)}, u32[]{:S(2)}) collective-permute-start(f32[32,128]{1,0:T(8,128)S(1)} %get-tuple-element.19), channel_id=1, source_target_pairs={{16,0},{32,16},{48,32},{64,48},{80,64},{96,80},{112,96},{17,1},{33... | collective-permute-start | bytes 49160 | tf_op jit(solution)/shard_map/ppermute | solution.py:31
  8.1 2.2 %collective-permute-start = (f32[32,128]{1,0:T(8,128)S(1)}, f32[32,128]{1,0:T(8,128)S(1)}, u32[]{:S(2)}, u32[]{:S(2)}) collective-permute-start(f32[32,128]{1,0:T(8,128)S(1)} %get-tuple-element.18), channel_id=1, source_target_pairs={{0,16},{16,32},{32,48},{48,64},{64,80},{80,96},{96,112},{1,17},{17... | collective-permute-start | bytes 49160 | tf_op jit(solution)/shard_map/ppermute | solution.py:28
  10.3 0.0 copy-done.1
  10.3 0.1 compare_select_fusion
  10.5 0.0 copy-start
  10.5 4.4 %fusion.2 = f32[1,1024]{1,0:T(1,128)S(1)} fusion(f32[1024,1]{0,1:T(1,128)S(1)} %bitcast.84, f32[1024]{0:T(1024)S(1)} %convert_element_type.66, f32[1024]{0:T(1024)S(1)} %convert_element_type.65, f32[1024]{0:T(1024)S(1)} %get-tuple-element.28, f32[1024]{0:T(1024)S(1)} %convert_element_type.63, f32[1024]{0:T(1024)S(1)} %convert_element_type.62, ...), kind=kOutput, calls=%fused_computation.12 | convolution fusion | flops 26214400 | bytes 32768 | tf_op jit(solution)/shard_map/dot_general | solution.py:89
  14.9 0.0 collective-permute-done.1
  14.9 0.0 collective-permute-done
  15.0 0.5 fusion.49
  15.4 2.7 %collective-permute-start.3 = (f32[128,32]{0,1:T(8,128)S(1)}, f32[128,32]{0,1:T(8,128)S(1)}, u32[]{:S(2)}, u32[]{:S(2)}) collective-permute-start(f32[128,32]{0,1:T(8,128)S(1)} %get-tuple-element.17), channel_id=1, source_target_pairs={{1,0},{2,1},{3,2},{4,3},{5,4},{6,5},{7,6},{8,7},{9,8},{10,9},{11,1... | collective-permute-start | bytes 49160 | tf_op jit(solution)/shard_map/ppermute | solution.py:31
  18.2 5.2 %collective-permute-start.2 = (f32[128,32]{0,1:T(8,128)S(1)}, f32[128,32]{0,1:T(8,128)S(1)}, u32[]{:S(2)}, u32[]{:S(2)}) collective-permute-start(f32[128,32]{0,1:T(8,128)S(1)} %get-tuple-element.16), channel_id=1, source_target_pairs={{0,1},{1,2},{2,3},{3,4},{4,5},{5,6},{6,7},{7,8},{8,9},{9,10},{10,1... | collective-permute-start | bytes 49160 | tf_op jit(solution)/shard_map/ppermute | solution.py:28
  23.4 0.0 copy-done
  23.4 0.3 copy.7
  23.7 6.2 %gather_fusion = f32[1024]{0:T(1024)S(1)} fusion(f32[262144]{0:T(1024)S(1)} %bitcast.62, s32[1024]{0:T(1024)S(1)} %broadcast_clamp_fusion.1), kind=kCustom, calls=%fused_computation | custom fusion | bytes 12288 | tf_op jit(solution)/shard_map/gather | solution.py:80
  29.9 0.0 collective-permute-done.3
  29.9 0.0 collective-permute-done.2
  29.9 0.5 convolution_bitcast_fusion.2
  30.4 6.2 %gather_fusion.1 = f32[1024]{0:T(1024)S(1)} fusion(f32[16384]{0:T(1024)S(1)} %convolution_bitcast_fusion.2, s32[1024]{0:T(1024)S(1)} %broadcast_clamp_fusion), kind=kCustom, calls=%fused_computation.1 | custom fusion | bytes 12288 | tf_op jit(solution)/shard_map/gather | solution.py:95
  36.5 0.7 broadcast_multiply_fusion.1
  37.2 1.8 %fusion.5 = f32[128,128]{1,0:T(8,128)S(1)} fusion(f32[1024]{0:T(1024)S(1)} %get-tuple-element.4, s32[1024]{0:T(1024)S(1)} %bitcast.67, s32[1024]{0:T(1024)S(1)} %bitcast.82, s32[128]{0:T(128)S(1)} %get-tuple-element.30, s32[1024]{0:T(1024)S(1)} %bitcast.77, s32[128]{0:T(128)S(1)} %get-tuple-element.31, s32[1024]{0:T(1024)S(1)} %bitcast.72), kind=kOutput, calls=%fused_computation.15 | convolution fusion | flops 202899456 | bytes 87040 | tf_op jit(solution)/shard_map/dot_general | solution.py:90
  39.0 2.8 %collective-permute-start.5 = (f32[32,128]{1,0:T(8,128)S(1)}, f32[32,128]{1,0:T(8,128)S(1)}, u32[]{:S(2)}, u32[]{:S(2)}) collective-permute-start(f32[32,128]{1,0:T(8,128)S(1)} %get-tuple-element.15), channel_id=1, source_target_pairs={{16,0},{32,16},{48,32},{64,48},{80,64},{96,80},{112,96},{17,1},{33... | collective-permute-start | bytes 49160 | tf_op jit(solution)/shard_map/ppermute | solution.py:31
  41.8 1.9 %collective-permute-start.4 = (f32[32,128]{1,0:T(8,128)S(1)}, f32[32,128]{1,0:T(8,128)S(1)}, u32[]{:S(2)}, u32[]{:S(2)}) collective-permute-start(f32[32,128]{1,0:T(8,128)S(1)} %get-tuple-element.14), channel_id=1, source_target_pairs={{0,16},{16,32},{32,48},{48,64},{64,80},{80,96},{96,112},{1,17},{17... | collective-permute-start | bytes 49160 | tf_op jit(solution)/shard_map/ppermute | solution.py:28
  43.7 0.0 collective-permute-done.5
  43.7 3.1 %collective-permute-done.4 = f32[32,128]{1,0:T(8,128)S(1)} collective-permute-done((f32[32,128]{1,0:T(8,128)S(1)}, f32[32,128]{1,0:T(8,128)S(1)}, u32[]{:S(2)}, u32[]{:S(2)}) %collective-permute-start.4) | collective-permute-done | bytes 16416 | tf_op jit(solution)/shard_map/ppermute | solution.py:28
  46.9 0.5 fusion.46
  47.4 1.9 %collective-permute-start.7 = (f32[128,32]{0,1:T(8,128)S(1)}, f32[128,32]{0,1:T(8,128)S(1)}, u32[]{:S(2)}, u32[]{:S(2)}) collective-permute-start(f32[128,32]{0,1:T(8,128)S(1)} %get-tuple-element.13), channel_id=1, source_target_pairs={{1,0},{2,1},{3,2},{4,3},{5,4},{6,5},{7,6},{8,7},{9,8},{10,9},{11,1... | collective-permute-start | bytes 49160 | tf_op jit(solution)/shard_map/ppermute | solution.py:31
  49.3 6.2 %collective-permute-start.6 = (f32[128,32]{0,1:T(8,128)S(1)}, f32[128,32]{0,1:T(8,128)S(1)}, u32[]{:S(2)}, u32[]{:S(2)}) collective-permute-start(f32[128,32]{0,1:T(8,128)S(1)} %get-tuple-element.12), channel_id=1, source_target_pairs={{0,1},{1,2},{2,3},{3,4},{4,5},{5,6},{6,7},{7,8},{8,9},{9,10},{10,1... | collective-permute-start | bytes 49160 | tf_op jit(solution)/shard_map/ppermute | solution.py:28
  55.5 4.4 %fusion.1 = f32[1,1024]{1,0:T(1,128)S(1)} fusion(f32[1024,1]{0,1:T(1,128)S(1)} %bitcast.86, f32[1024]{0:T(1024)S(1)} %convert_element_type.66, f32[1024]{0:T(1024)S(1)} %convert_element_type.65, f32[1024]{0:T(1024)S(1)} %get-tuple-element.28, f32[1024]{0:T(1024)S(1)} %convert_element_type.63, f32[1024]{0:T(1024)S(1)} %convert_element_type.62, ...), kind=kOutput, calls=%fused_computation.11 | convolution fusion | flops 26214400 | bytes 32768 | tf_op jit(solution)/shard_map/dot_general | solution.py:89
  59.9 0.0 collective-permute-done.7
  59.9 0.0 collective-permute-done.6
  60.0 0.5 convolution_bitcast_fusion.1
  60.4 6.2 %gather_fusion.2 = f32[1024]{0:T(1024)S(1)} fusion(f32[16384]{0:T(1024)S(1)} %convolution_bitcast_fusion.1, s32[1024]{0:T(1024)S(1)} %broadcast_clamp_fusion), kind=kCustom, calls=%fused_computation.2 | custom fusion | bytes 12288 | tf_op jit(solution)/shard_map/gather | solution.py:95
  66.6 0.7 broadcast_multiply_fusion
  67.3 1.8 %fusion.3 = f32[128,128]{1,0:T(8,128)S(1)} fusion(f32[1024]{0:T(1024)S(1)} %get-tuple-element.2, s32[1024]{0:T(1024)S(1)} %bitcast.68, s32[1024]{0:T(1024)S(1)} %bitcast.83, s32[128]{0:T(128)S(1)} %get-tuple-element.30, s32[1024]{0:T(1024)S(1)} %bitcast.78, s32[128]{0:T(128)S(1)} %get-tuple-element.31, s32[1024]{0:T(1024)S(1)} %bitcast.73), kind=kOutput, calls=%fused_computation.13 | convolution fusion | flops 202899456 | bytes 87040 | tf_op jit(solution)/shard_map/dot_general | solution.py:90
  69.1 1.9 %collective-permute-start.9 = (f32[32,128]{1,0:T(8,128)S(1)}, f32[32,128]{1,0:T(8,128)S(1)}, u32[]{:S(2)}, u32[]{:S(2)}) collective-permute-start(f32[32,128]{1,0:T(8,128)S(1)} %get-tuple-element.11), channel_id=1, source_target_pairs={{16,0},{32,16},{48,32},{64,48},{80,64},{96,80},{112,96},{17,1},{33... | collective-permute-start | bytes 49160 | tf_op jit(solution)/shard_map/ppermute | solution.py:31
  71.0 2.4 %collective-permute-start.8 = (f32[32,128]{1,0:T(8,128)S(1)}, f32[32,128]{1,0:T(8,128)S(1)}, u32[]{:S(2)}, u32[]{:S(2)}) collective-permute-start(f32[32,128]{1,0:T(8,128)S(1)} %get-tuple-element.10), channel_id=1, source_target_pairs={{0,16},{16,32},{32,48},{48,64},{64,80},{80,96},{96,112},{1,17},{17... | collective-permute-start | bytes 49160 | tf_op jit(solution)/shard_map/ppermute | solution.py:28
  73.4 0.0 collective-permute-done.9
  73.4 2.6 %collective-permute-done.8 = f32[32,128]{1,0:T(8,128)S(1)} collective-permute-done((f32[32,128]{1,0:T(8,128)S(1)}, f32[32,128]{1,0:T(8,128)S(1)}, u32[]{:S(2)}, u32[]{:S(2)}) %collective-permute-start.8) | collective-permute-done | bytes 16416 | tf_op jit(solution)/shard_map/ppermute | solution.py:28
  76.1 0.5 fusion.43
  76.6 1.9 %collective-permute-start.11 = (f32[128,32]{0,1:T(8,128)S(1)}, f32[128,32]{0,1:T(8,128)S(1)}, u32[]{:S(2)}, u32[]{:S(2)}) collective-permute-start(f32[128,32]{0,1:T(8,128)S(1)} %get-tuple-element.9), channel_id=1, source_target_pairs={{1,0},{2,1},{3,2},{4,3},{5,4},{6,5},{7,6},{8,7},{9,8},{10,9},{11,1... | collective-permute-start | bytes 49160 | tf_op jit(solution)/shard_map/ppermute | solution.py:31
  78.5 6.3 %collective-permute-start.10 = (f32[128,32]{0,1:T(8,128)S(1)}, f32[128,32]{0,1:T(8,128)S(1)}, u32[]{:S(2)}, u32[]{:S(2)}) collective-permute-start(f32[128,32]{0,1:T(8,128)S(1)} %get-tuple-element.8), channel_id=1, source_target_pairs={{0,1},{1,2},{2,3},{3,4},{4,5},{5,6},{6,7},{7,8},{8,9},{9,10},{10,1... | collective-permute-start | bytes 49160 | tf_op jit(solution)/shard_map/ppermute | solution.py:28
  84.8 4.4 %fusion = f32[1,1024]{1,0:T(1,128)S(1)} fusion(f32[1024,1]{0,1:T(1,128)S(1)} %bitcast.85, f32[1024]{0:T(1024)S(1)} %convert_element_type.66, f32[1024]{0:T(1024)S(1)} %convert_element_type.65, f32[1024]{0:T(1024)S(1)} %get-tuple-element.28, f32[1024]{0:T(1024)S(1)} %convert_element_type.63, f32[1024]{0:T(1024)S(1)} %convert_element_type.62, ...), kind=kOutput, calls=%fused_computation.10 | convolution fusion | flops 26214400 | bytes 32768 | tf_op jit(solution)/shard_map/dot_general | solution.py:89
  89.2 0.0 collective-permute-done.11
  89.2 0.0 collective-permute-done.10
  89.2 0.5 convolution_bitcast_fusion
  89.7 6.2 %gather_fusion.3 = f32[1024]{0:T(1024)S(1)} fusion(f32[16384]{0:T(1024)S(1)} %convolution_bitcast_fusion, s32[1024]{0:T(1024)S(1)} %broadcast_clamp_fusion), kind=kCustom, calls=%fused_computation.3 | custom fusion | bytes 12288 | tf_op jit(solution)/shard_map/gather | solution.py:95
  95.9 1.3 %fusion.111 = (f32[1024]{0:T(1024)}, f32[1024]{0:T(1024)}) fusion(s32[]{:T(128)} %fusion.113, f32[1024]{0:T(1024)S(1)} %gather_fusion, f32[1024]{0:T(1024)S(1)} %bitcast.91, f32[1024]{0:T(1024)S(1)} %gather_fusion.3, f32[1024]{0:T(1024)S(1)} %get-tuple-element.3), kind=kLoop, calls=%fused_computation.144 | loop fusion | flops 9216 | bytes 24580 | tf_op jit(solution)/shard_map/jit(_where)/select_n | solution.py:100
  (15 shorter events, 0.1 us)
Async XLA Ops:
  0.6 9.7 %copy-start.1 = (s32[4,1,1024]{2,1,0:T(1,128)S(1)}, s32[4,1,1024]{2,1,0:T(1,128)}, u32[]{:S(2)}) copy-start(s32[4,1,1024]{2,1,0:T(1,128)} %param.5) | copy-start | bytes 49156
  6.0 9.0 %collective-permute-start.1 = (f32[32,128]{1,0:T(8,128)S(1)}, f32[32,128]{1,0:T(8,128)S(1)}, u32[]{:S(2)}, u32[]{:S(2)}) collective-permute-start(f32[32,128]{1,0:T(8,128)S(1)} %get-tuple-element.19), channel_id=1, source_target_pairs={{16,0},{32,16},{48,32},{64,48},{80,64},{96,80},{112,96},{17,1},{33... | collective-permute-start | bytes 49160 | tf_op jit(solution)/shard_map/ppermute | solution.py:31
  8.1 6.9 %collective-permute-start = (f32[32,128]{1,0:T(8,128)S(1)}, f32[32,128]{1,0:T(8,128)S(1)}, u32[]{:S(2)}, u32[]{:S(2)}) collective-permute-start(f32[32,128]{1,0:T(8,128)S(1)} %get-tuple-element.18), channel_id=1, source_target_pairs={{0,16},{16,32},{32,48},{48,64},{64,80},{80,96},{96,112},{1,17},{17... | collective-permute-start | bytes 49160 | tf_op jit(solution)/shard_map/ppermute | solution.py:28
  10.5 13.0 %copy-start = (f32[512,512]{1,0:T(8,128)S(1)}, f32[512,512]{1,0:T(8,128)}, u32[]{:S(2)}) copy-start(f32[512,512]{1,0:T(8,128)} %param.9) | copy-start | bytes 3145732
  15.4 14.4 %collective-permute-start.3 = (f32[128,32]{0,1:T(8,128)S(1)}, f32[128,32]{0,1:T(8,128)S(1)}, u32[]{:S(2)}, u32[]{:S(2)}) collective-permute-start(f32[128,32]{0,1:T(8,128)S(1)} %get-tuple-element.17), channel_id=1, source_target_pairs={{1,0},{2,1},{3,2},{4,3},{5,4},{6,5},{7,6},{8,7},{9,8},{10,9},{11,1... | collective-permute-start | bytes 49160 | tf_op jit(solution)/shard_map/ppermute | solution.py:31
  18.2 11.7 %collective-permute-start.2 = (f32[128,32]{0,1:T(8,128)S(1)}, f32[128,32]{0,1:T(8,128)S(1)}, u32[]{:S(2)}, u32[]{:S(2)}) collective-permute-start(f32[128,32]{0,1:T(8,128)S(1)} %get-tuple-element.16), channel_id=1, source_target_pairs={{0,1},{1,2},{2,3},{3,4},{4,5},{5,6},{6,7},{7,8},{8,9},{9,10},{10,1... | collective-permute-start | bytes 49160 | tf_op jit(solution)/shard_map/ppermute | solution.py:28
  39.0 4.7 %collective-permute-start.5 = (f32[32,128]{1,0:T(8,128)S(1)}, f32[32,128]{1,0:T(8,128)S(1)}, u32[]{:S(2)}, u32[]{:S(2)}) collective-permute-start(f32[32,128]{1,0:T(8,128)S(1)} %get-tuple-element.15), channel_id=1, source_target_pairs={{16,0},{32,16},{48,32},{64,48},{80,64},{96,80},{112,96},{17,1},{33... | collective-permute-start | bytes 49160 | tf_op jit(solution)/shard_map/ppermute | solution.py:31
  41.8 5.1 %collective-permute-start.4 = (f32[32,128]{1,0:T(8,128)S(1)}, f32[32,128]{1,0:T(8,128)S(1)}, u32[]{:S(2)}, u32[]{:S(2)}) collective-permute-start(f32[32,128]{1,0:T(8,128)S(1)} %get-tuple-element.14), channel_id=1, source_target_pairs={{0,16},{16,32},{32,48},{48,64},{64,80},{80,96},{96,112},{1,17},{17... | collective-permute-start | bytes 49160 | tf_op jit(solution)/shard_map/ppermute | solution.py:28
  47.4 12.6 %collective-permute-start.7 = (f32[128,32]{0,1:T(8,128)S(1)}, f32[128,32]{0,1:T(8,128)S(1)}, u32[]{:S(2)}, u32[]{:S(2)}) collective-permute-start(f32[128,32]{0,1:T(8,128)S(1)} %get-tuple-element.13), channel_id=1, source_target_pairs={{1,0},{2,1},{3,2},{4,3},{5,4},{6,5},{7,6},{8,7},{9,8},{10,9},{11,1... | collective-permute-start | bytes 49160 | tf_op jit(solution)/shard_map/ppermute | solution.py:31
  49.3 10.7 %collective-permute-start.6 = (f32[128,32]{0,1:T(8,128)S(1)}, f32[128,32]{0,1:T(8,128)S(1)}, u32[]{:S(2)}, u32[]{:S(2)}) collective-permute-start(f32[128,32]{0,1:T(8,128)S(1)} %get-tuple-element.12), channel_id=1, source_target_pairs={{0,1},{1,2},{2,3},{3,4},{4,5},{5,6},{6,7},{7,8},{8,9},{9,10},{10,1... | collective-permute-start | bytes 49160 | tf_op jit(solution)/shard_map/ppermute | solution.py:28
  69.1 4.3 %collective-permute-start.9 = (f32[32,128]{1,0:T(8,128)S(1)}, f32[32,128]{1,0:T(8,128)S(1)}, u32[]{:S(2)}, u32[]{:S(2)}) collective-permute-start(f32[32,128]{1,0:T(8,128)S(1)} %get-tuple-element.11), channel_id=1, source_target_pairs={{16,0},{32,16},{48,32},{64,48},{80,64},{96,80},{112,96},{17,1},{33... | collective-permute-start | bytes 49160 | tf_op jit(solution)/shard_map/ppermute | solution.py:31
  71.0 5.1 %collective-permute-start.8 = (f32[32,128]{1,0:T(8,128)S(1)}, f32[32,128]{1,0:T(8,128)S(1)}, u32[]{:S(2)}, u32[]{:S(2)}) collective-permute-start(f32[32,128]{1,0:T(8,128)S(1)} %get-tuple-element.10), channel_id=1, source_target_pairs={{0,16},{16,32},{32,48},{48,64},{64,80},{80,96},{96,112},{1,17},{17... | collective-permute-start | bytes 49160 | tf_op jit(solution)/shard_map/ppermute | solution.py:28
  76.6 12.6 %collective-permute-start.11 = (f32[128,32]{0,1:T(8,128)S(1)}, f32[128,32]{0,1:T(8,128)S(1)}, u32[]{:S(2)}, u32[]{:S(2)}) collective-permute-start(f32[128,32]{0,1:T(8,128)S(1)} %get-tuple-element.9), channel_id=1, source_target_pairs={{1,0},{2,1},{3,2},{4,3},{5,4},{6,5},{7,6},{8,7},{9,8},{10,9},{11,1... | collective-permute-start | bytes 49160 | tf_op jit(solution)/shard_map/ppermute | solution.py:31
  78.5 10.7 %collective-permute-start.10 = (f32[128,32]{0,1:T(8,128)S(1)}, f32[128,32]{0,1:T(8,128)S(1)}, u32[]{:S(2)}, u32[]{:S(2)}) collective-permute-start(f32[128,32]{0,1:T(8,128)S(1)} %get-tuple-element.8), channel_id=1, source_target_pairs={{0,1},{1,2},{2,3},{3,4},{4,5},{5,6},{6,7},{7,8},{8,9},{9,10},{10,1... | collective-permute-start | bytes 49160 | tf_op jit(solution)/shard_map/ppermute | solution.py:28
where the time goes:
time: 97.7 us; the launch traced here: 97.2 us
  starting transfers between devices  37.6 us (38%)
  local copies, waits for them, and re-layouts  25.7 us (26%)
  matrix products  21.5 us (22%)
  waiting for transfers between devices  5.79 us (6%)
  other arithmetic  5.59 us (6%)
  between operations  1.05 us (1%)
    ppermute x6, starting transfers between devices, with_halo(): lax.ppermute(lax.slice_in_dim(block, block.shape[dim] - width, None, axis...  24.2 us
    gather x3, local copies, waits for them, and re-layouts, body(): sampled = background.reshape(-1)[cell_ids]  18.5 us
    ppermute x6, starting transfers between devices, with_halo(): lax.ppermute(lax.slice_in_dim(block, 0, width, axis=dim), axis, backward)  13.4 us
    dot_general x3, matrix products, body(): forward = jnp.dot(shot_dose, kernel, precision=EXACT_MODE)  13.3 us
    gather x1, local copies, waits for them, and re-layouts, body(): sensitive = pixel_gain.reshape(-1)[pixel_ids]  6.15 us
    ppermute x6, waiting for transfers between devices, with_halo(): lax.ppermute(lax.slice_in_dim(block, block.shape[dim] - width, None, axis...  5.78 us
    dot_general x3, matrix products, body(): jnp.dot(downward.T, shot_dose[:, None] * across, precision=EXACT_MODE)  5.3 us
    mul x3, other arithmetic, body(): shot_dose[:, None] * across  2.78 us
  transfers between devices with their start and end apart: 12, of which 2 were waited for; matrix products, arithmetic and copies ran while one was open for 20% of the time, Pallas kernels for 0%

commit v1 on v0

v1 whole, which is shorter than its diff:
```python
import functools
import math

import jax
import jax.numpy as jnp
from jax import lax
from jax.experimental import pallas as pl
from jax.experimental.pallas import tpu as pltpu
from jax.sharding import PartitionSpec as P

TILE = 512
CG = 128
BLK = 128
ITERS = 3
CELL = 4
BETA = 16
REACH = 32
SLOTS = 1024
NTR = 8
NTC = 16
FORWARD_RANGE = 4.0
BACK_RATIO = 0.75
TARGET_LEVEL = 1.0
F32 = jnp.float32
BF16 = jnp.bfloat16
AXES = ("row", "col")
NT = (((1,), (1,)), ((), ()))


def pairings():
    def number(r, c):
        return r * NTC + c

    def table(partner):
        return [(number(r, c), number(*partner(r, c))) for r in range(NTR) for c in range(NTC)]

    def odd(i):
        return ((i - 1) ^ 1) + 1

    row_even = table(lambda r, c: (r ^ 1, c))
    row_odd = table(lambda r, c: (r, c ^ 1) if r in (0, NTR - 1) else (odd(r), c))
    col_even = table(lambda r, c: (r, c ^ 1))
    col_odd = table(lambda r, c: (r ^ 1, c) if c in (0, NTC - 1) else (r, odd(c)))
    return row_even, row_odd, col_even, col_odd


def two_parts(value):
    high = value.astype(BF16)
    low = (value - high.astype(F32)).astype(BF16)
    return high, low


def stacked_dot(value, other, dims):
    rows = value.shape[0]
    parts = jnp.concatenate(two_parts(value), axis=0)
    both = lax.dot_general(parts, other, dims, preferred_element_type=F32)
    return both[:rows] + both[rows:]


def weighted(value, high, low):
    rows = value.shape[0]
    first, second = two_parts(value)
    both = jnp.dot(jnp.concatenate([first, second], axis=0), high, preferred_element_type=F32)
    return both[:rows] + both[rows:] + jnp.dot(first, low, preferred_element_type=F32)


def overlap(low_edge, high_edge, cells):
    begin = cells * CELL
    covered = jnp.minimum(high_edge, begin + CELL) - jnp.maximum(low_edge, begin)
    return jnp.maximum(covered, 0).astype(F32) * (1.0 / CELL)


def spread(distance):
    scaled = distance.astype(F32) / BETA
    inside = jnp.abs(distance) <= REACH
    return jnp.where(inside, jnp.exp(-scaled * scaled) / (math.sqrt(math.pi) * BETA), 0.0)


def iota(shape, axis):
    return lax.broadcasted_iota(jnp.int32, shape, axis)


def is_even(axis):
    return lax.rem(lax.axis_index(axis), 2) == 0


def row_strips(dose, px_t, py_edges, send_even, send_odd):
    edges = stacked_dot(py_edges * dose, px_t, NT)
    top, bottom = edges[:REACH], edges[REACH:]
    even = is_even("row")
    send_even[...] = jnp.where(even, bottom, top)
    send_odd[...] = jnp.where(even, top, bottom)


def start_kernel(boxes, counts, tails, doses, dose_out, send_even, send_odd):
    col = lax.axis_index("col")
    totals = (counts[...] - 1) * BLK + tails[...]
    total = jnp.sum(jnp.where(iota((1, NTC), 1) == col, totals, 0), axis=1, keepdims=True)
    live = iota((1, SLOTS), 1) < total
    dose = jnp.where(live, doses[...], 0.0)
    dose_out[...] = dose
    px_t = overlap(boxes[0], boxes[2], iota((CG, SLOTS), 0)).astype(BF16)
    edge_cells = iota((2 * REACH, SLOTS), 0)
    edge_cells = jnp.where(edge_cells < REACH, edge_cells, edge_cells + (CG - 2 * REACH))
    py_edges = overlap(boxes[1], boxes[3], edge_cells)
    row_strips(dose, px_t, py_edges, send_even, send_odd)


def sens_kernel(boxes, gain, px_out, py_out, sens_out):
    px_out[...] = overlap(boxes[0], boxes[2], iota((CG, SLOTS), 0)).astype(BF16)
    py_out[...] = overlap(boxes[1], boxes[3], iota((CG, SLOTS), 0)).astype(BF16)
    pixel_x = (boxes[0] + boxes[2]) // 2
    pixel_y = (boxes[1] + boxes[3]) // 2
    pixels = iota((TILE, SLOTS), 0)
    chosen_x = jnp.where(pixels == pixel_x, 1.0, 0.0).astype(BF16)
    picked = stacked_dot(gain[...], chosen_x, (((1,), (0,)), ((), ())))
    sens_out[...] = jnp.sum(jnp.where(pixels == pixel_y, picked, 0.0), axis=0, keepdims=True)


def setup_kernel(boxes, wy_high, wy_low, wx_out, pairs):
    cell_x = (boxes[0] + boxes[2]) // (2 * CELL)
    cell_y = (boxes[1] + boxes[3]) // (2 * CELL)
    y = iota((2 * CG, SLOTS), 0)
    place = jnp.where(y < CG, y, jnp.where(y < CG + REACH, y - (CG + REACH), y - REACH))
    weight = jnp.where(y < CG + 2 * REACH, spread(cell_y - place), 0.0)
    wy_high[...], wy_low[...] = two_parts(weight)
    x = iota((CG + 2 * REACH, SLOTS), 0)
    place = jnp.where(x < CG, x, jnp.where(x < CG + REACH, x - (CG + REACH), x - REACH))
    wx_out[...] = spread(cell_x - place)
    inverse = 1.0 / FORWARD_RANGE
    box = [boxes[k].astype(F32) for k in range(4)]
    centre_x = (box[0] + box[2]) * (0.5 * inverse)
    centre_y = (box[1] + box[3]) * (0.5 * inverse)
    columns = jnp.concatenate([b * inverse for b in box] + [jnp.zeros((4, SLOTS), F32)], axis=0)
    step = 128
    for first in range(0, SLOTS, step):
        side = jnp.transpose(columns[:, first : first + step])
        along_x = lax.erf(centre_x - side[:, 0:1]) - lax.erf(centre_x - side[:, 2:3])
        along_y = lax.erf(centre_y - side[:, 1:2]) - lax.erf(centre_y - side[:, 3:4])
        pairs[first : first + step, :] = (0.25 * along_x) * along_y


def forward_kernel(dose_in, pairs, forward):
    dose = dose_in[...]
    folded = jnp.concatenate([dose[:, k * 128 : (k + 1) * 128] for k in range(8)], axis=0)
    columns = jnp.transpose(folded)
    total = jnp.zeros((8, SLOTS), F32)
    for k in range(8):
        part = columns[:, k : k + 1] * pairs[k * 128 : (k + 1) * 128, :]
        total += jnp.sum(part.reshape(16, 8, SLOTS), axis=0)
    forward[...] = jnp.sum(total, axis=0, keepdims=True)


def coarse_kernel(dose_in, px, py, coarse_t):
    coarse_t[...] = stacked_dot(px[...].astype(F32) * dose_in[...], py[...], NT)


def middle_kernel(got_even, got_odd, coarse_t, tall_t, send_even, send_odd):
    row = lax.axis_index("row")
    even = lax.rem(row, 2) == 0
    from_even, from_odd = got_even[...], got_odd[...]
    above = jnp.where(even, from_odd, from_even)
    below = jnp.where(even, from_even, from_odd)
    above = jnp.where(row == 0, 0.0, above)
    below = jnp.where(row == NTR - 1, 0.0, below)
    outer = jnp.concatenate([above, below, jnp.zeros((CG - 2 * REACH, CG), F32)], axis=0)
    tall = jnp.concatenate([coarse_t[...], jnp.transpose(outer)], axis=1)
    tall_t[...] = tall
    even = is_even("col")
    left, right = tall[:REACH], tall[CG - REACH :]
    send_even[...] = jnp.where(even, right, left)
    send_odd[...] = jnp.where(even, left, right)


def inner_kernel(tall_t, wy_high, wy_low, wx, inner):
    across = weighted(tall_t[...], wy_high[...], wy_low[...])
    inner[...] = jnp.sum(across * wx[:CG, :], axis=0, keepdims=True)


def new_dose(got_even, got_odd, forward, inner, sens, dose_in, wy_high, wy_low, wx):
    col = lax.axis_index("col")
    even = lax.rem(col, 2) == 0
    from_even, from_odd = got_even[...], got_odd[...]
    left = jnp.where(even, from_odd, from_even)
    right = jnp.where(even, from_even, from_odd)
    left = jnp.where(col == 0, 0.0, left)
    right = jnp.where(col == NTC - 1, 0.0, right)
    across = weighted(jnp.concatenate([left, right], axis=0), wy_high[...], wy_low[...])
    background = inner[...] + jnp.sum(across * wx[CG:, :], axis=0, keepdims=True)
    exposure = sens[...] * (forward[...] + BACK_RATIO * background) / (1.0 + BACK_RATIO)
    dose = dose_in[...]
    live = dose > 0.0
    return jnp.where(live, dose * TARGET_LEVEL / jnp.where(live, exposure, 1.0), 0.0), jnp.where(live, exposure, 0.0)


def update_kernel(got_even, got_odd, forward, inner, sens, dose_in, wy_high, wy_low, wx, px, py, dose_out, send_even, send_odd):
    dose, _ = new_dose(got_even, got_odd, forward, inner, sens, dose_in, wy_high, wy_low, wx)
    dose_out[...] = dose
    py_edges = jnp.concatenate([py[:REACH, :], py[CG - REACH :, :]], axis=0).astype(F32)
    row_strips(dose, px[...], py_edges, send_even, send_odd)


def final_kernel(got_even, got_odd, forward, inner, sens, dose_in, wy_high, wy_low, wx, dose_out, exposure_out):
    dose_out[...], exposure_out[...] = new_dose(got_even, got_odd, forward, inner, sens, dose_in, wy_high, wy_low, wx)


def shape(*dims, dtype=F32):
    return jax.ShapeDtypeStruct(dims, dtype)


def call(kernel, outs, name, vmem=16, flops=0, moved=0):
    return pl.pallas_call(
        kernel,
        out_shape=outs,
        name=name,
        compiler_params=pltpu.CompilerParams(vmem_limit_bytes=vmem << 20),
        cost_estimate=pl.CostEstimate(flops=flops, bytes_accessed=moved, transcendentals=0),
    )


def body(shot_boxes, block_counts, tail_shots, doses, pixel_gain):
    row_even, row_odd, col_even, col_odd = pairings()
    row = shape(1, SLOTS)
    strip = shape(REACH, CG)
    wide = shape(REACH, 2 * CG)
    dose, strip_even, strip_odd = call(start_kernel, (row, strip, strip), "start")(shot_boxes, block_counts, tail_shots, doses)
    for sweep in range(ITERS):
        got_even = lax.ppermute(strip_even, AXES, row_even)
        got_odd = lax.ppermute(strip_odd, AXES, row_odd)
        if sweep == 0:
            px, py, sens = call(sens_kernel, (shape(CG, SLOTS, dtype=BF16), shape(CG, SLOTS, dtype=BF16), row), "sens")(shot_boxes, pixel_gain)
        coarse_t = call(coarse_kernel, shape(CG, CG), "coarse")(dose, px, py)
        tall_t, wide_even, wide_odd = call(middle_kernel, (shape(CG, 2 * CG), wide, wide), "middle")(got_even, got_odd, coarse_t)
        far_even = lax.ppermute(wide_even, AXES, col_even)
        far_odd = lax.ppermute(wide_odd, AXES, col_odd)
        if sweep == 0:
            wy_high, wy_low, wx, pairs = call(
                setup_kernel,
                (shape(2 * CG, SLOTS, dtype=BF16), shape(2 * CG, SLOTS, dtype=BF16), shape(CG + 2 * REACH, SLOTS), shape(SLOTS, SLOTS)),
                "setup",
            )(shot_boxes)
        forward = call(forward_kernel, row, "forward")(dose, pairs)
        inner = call(inner_kernel, row, "inner")(tall_t, wy_high, wy_low, wx)
        common = (far_even, far_odd, forward, inner, sens, dose, wy_high, wy_low, wx)
        if sweep < ITERS - 1:
            dose, strip_even, strip_odd = call(update_kernel, (row, strip, strip), "update")(*common, px, py)
    return call(final_kernel, (row, row), "final")(*common)


def solution(mesh):
    placed = (P(None, "row", "col"), P("row", None), P("row", None), P("row", "col"), P("row", "col"))
    return jax.shard_map(body, mesh=mesh, in_specs=placed, out_specs=(P("row", "col"), P("row", "col")), check_vma=False)
```

time: 97.7 us -> 40.8 us (0.42)
  the two profiles are of different devices: /device:TPU:62 before, /device:TPU:64 now
where the time goes in v1:
time: 40.8 us; the launch traced here: 40.4 us
  waiting for transfers between devices  13.1 us (32%)
  Pallas kernels  11.8 us (29%)
  starting transfers between devices  10 us (25%)
  local copies, waits for them, and re-layouts  4.65 us (11%)
  between operations  0.88 us (2%)
    ppermute x3, starting transfers between devices, body(): far_odd = lax.ppermute(wide_odd, AXES, col_odd)  5.45 us
    ppermute x3, waiting for transfers between devices, body(): far_odd = lax.ppermute(wide_odd, AXES, col_odd)  5.21 us
    ppermute x3, waiting for transfers between devices, body(): got_odd = lax.ppermute(strip_odd, AXES, row_odd)  5.18 us
    unnamed x12, local copies, waits for them, and re-layouts  4.65 us
    pallas_call x1, Pallas kernels, body(): call(setup_kernel, (shape(2 * CG, SLOTS, dtype=BF16), shape(2 * CG, SLOTS...  3.65 us
    ppermute x3, starting transfers between devices, body(): got_odd = lax.ppermute(strip_odd, AXES, row_odd)  2.63 us
    ppermute x3, waiting for transfers between devices, body(): far_even = lax.ppermute(wide_even, AXES, col_even)  1.98 us
    ppermute x3, starting transfers between devices, body(): far_even = lax.ppermute(wide_even, AXES, col_even)  1.67 us
  transfers between devices with their start and end apart: 12, of which 7 were waited for; matrix products, arithmetic and copies ran while one was open for 0% of the time, Pallas kernels for 22%

profile of v1, /device:TPU:64, one launch (start us, length us, event | category | flops | bytes accessed | tf_op | source)
XLA Modules:
  0.0 40.4 jit_solution(1739259399319082081)
XLA Ops:
  0.6 0.0 copy-start.1
  0.6 0.7 %copy-done.1 = s32[4,1,1024]{2,1,0:T(1,128)S(1)} copy-done((s32[4,1,1024]{2,1,0:T(1,128)S(1)}, s32[4,1,1024]{2,1,0:T(1,128)}, u32[]{:S(2)}) %copy-start.1) | copy-done | bytes 16408
  1.4 0.0 copy-start.3
  1.4 0.7 %copy-done.3 = f32[1,1024]{1,0:T(1,128)S(1)} copy-done((f32[1,1024]{1,0:T(1,128)S(1)}, f32[1,1024]{1,0:T(1,128)}, u32[]{:S(2)}) %copy-start.3) | copy-done | bytes 4120
  2.0 0.0 copy-start.4
  2.0 0.7 %copy-done.4 = s32[1,16]{1,0:T(1,128)S(1)} copy-done((s32[1,16]{1,0:T(1,128)S(1)}, s32[1,16]{1,0:T(1,128)}, u32[]{:S(2)}) %copy-start.4) | copy-done | bytes 88
  2.7 0.0 copy-start.5
  2.7 0.7 %copy-done.5 = s32[1,16]{1,0:T(1,128)S(1)} copy-done((s32[1,16]{1,0:T(1,128)S(1)}, s32[1,16]{1,0:T(1,128)}, u32[]{:S(2)}) %copy-start.5) | copy-done | bytes 88
  3.4 0.4 %start.1 = (f32[1,1024]{1,0:T(1,128)S(1)}, f32[32,128]{1,0:T(8,128)S(1)}, f32[32,128]{1,0:T(8,128)S(1)}) custom-call(s32[4,1,1024]{2,1,0:T(1,128)S(1)} %copy-done.1, s32[1,16]{1,0:T(1,128)S(1)} %copy-done.4, s32[1,16]{1,0:T(1,128)S(1)} %copy-done.5, f32[1,1024]{1,0:T(1,128)S(1)} %copy-done.3), custom_call_target="tpu_custom_call" | custom-call | tf_op jit(solution)/shard_map/start/pallas_call | solution.py:226
  3.8 0.1 collective-permute-start
  3.9 1.6 %collective-permute-start.1 = (f32[32,128]{1,0:T(8,128)S(1)}, f32[32,128]{1,0:T(8,128)S(1)}, u32[]{:S(2)}, u32[]{:S(2)}) collective-permute-start(f32[32,128]{1,0:T(8,128)S(1)} %get-tuple-element.28), channel_id=1, source_target_pairs={{0,1},{1,0},{2,3},{3,2},{4,5},{5,4},{6,7},{7,6},{8,9},{9,8},{10,11... | collective-permute-start | bytes 49160 | tf_op jit(solution)/shard_map/ppermute | solution.py:229
  5.5 0.0 copy-start
  5.5 1.2 %copy-done = f32[512,512]{1,0:T(8,128)S(1)} copy-done((f32[512,512]{1,0:T(8,128)S(1)}, f32[512,512]{1,0:T(8,128)}, u32[]{:S(2)}) %copy-start) | copy-done | bytes 1048600
  6.7 1.7 %sens.1 = (bf16[128,1024]{1,0:T(8,128)(2,1)S(1)}, bf16[128,1024]{1,0:T(8,128)(2,1)S(1)}, f32[1,1024]{1,0:T(1,128)S(1)}) custom-call(s32[4,1,1024]{2,1,0:T(1,128)S(1)} %copy-done.1, f32[512,512]{1,0:T(8,128)S(1)} %copy-done), custom_call_target="tpu_custom_call" | custom-call | tf_op jit(solution)/shard_map/sens/pallas_call | solution.py:231
  8.4 0.3 coarse.3.coarse_t
  8.7 0.0 collective-permute-done.got_even
  8.7 0.0 collective-permute-done.1.got_odd
  8.7 0.1 middle.3
  8.8 0.6 %collective-permute-start.2 = (f32[32,256]{1,0:T(8,128)S(1)}, f32[32,256]{1,0:T(8,128)S(1)}, u32[]{:S(2)}, u32[]{:S(2)}) collective-permute-start(f32[32,256]{1,0:T(8,128)S(1)} %get-tuple-element.32), channel_id=1, source_target_pairs={{0,1},{1,0},{2,3},{3,2},{4,5},{5,4},{6,7},{7,6},{8,9},{9,8},{10,11... | collective-permute-start | bytes 98312 | tf_op jit(solution)/shard_map/ppermute | solution.py:234
  9.4 2.3 %collective-permute-start.3 = (f32[32,256]{1,0:T(8,128)S(1)}, f32[32,256]{1,0:T(8,128)S(1)}, u32[]{:S(2)}, u32[]{:S(2)}) collective-permute-start(f32[32,256]{1,0:T(8,128)S(1)} %get-tuple-element.33), channel_id=1, source_target_pairs={{0,16},{1,2},{2,1},{3,4},{4,3},{5,6},{6,5},{7,8},{8,7},{9,10},{10,... | collective-permute-start | bytes 98312 | tf_op jit(solution)/shard_map/ppermute | solution.py:235
  11.7 0.0 copy-start.2
  11.7 0.7 %copy-done.2 = s32[4,1,1024]{2,1,0:T(1,128)S(1)} copy-done((s32[4,1,1024]{2,1,0:T(1,128)S(1)}, s32[4,1,1024]{2,1,0:T(1,128)}, u32[]{:S(2)}) %copy-start.2) | copy-done | bytes 16408
  12.4 3.7 %setup.1 = (bf16[256,1024]{1,0:T(8,128)(2,1)S(1)}, bf16[256,1024]{1,0:T(8,128)(2,1)S(1)}, f32[192,1024]{1,0:T(8,128)S(1)}, f32[1024,1024]{1,0:T(8,128)S(1)}) custom-call(s32[4,1,1024]{2,1,0:T(1,128)S(1)} %copy-done.2), custom_call_target="tpu_custom_call" | custom-call | tf_op jit(solution)/shard_map/setup/pallas_call | solution.py:237
  16.1 0.5 %forward.3 = f32[1,1024]{1,0:T(1,128)S(1)} custom-call(f32[1,1024]{1,0:T(1,128)S(1)} %get-tuple-element.29.dose_in, f32[1024,1024]{1,0:T(8,128)S(1)} %get-tuple-element.34.pairs), custom_call_target="tpu_custom_call" | custom-call | tf_op jit(solution)/shard_map/forward/pallas_call | solution.py:242
  16.6 0.4 inner.3
  17.0 0.0 collective-permute-done.2.got_even
  17.0 0.0 collective-permute-done.3.got_odd
  17.0 0.6 %update.2 = (f32[1,1024]{1,0:T(1,128)S(1)}, f32[32,128]{1,0:T(8,128)S(1)}, f32[32,128]{1,0:T(8,128)S(1)}) custom-call(f32[32,256]{1,0:T(8,128)S(1)} %collective-permute-done.2.got_even, f32[32,256]{1,0:T(8,128)S(1)} %collective-permute-done.3.got_odd, f32[1,1024]{1,0:T(1,128)S(1)} %forward.3, f32[1,1024]{1,0:T(1,128)S(1)} %inner.3, ...), custom_call_target="tpu_custom_call" | custom-call | tf_op jit(solution)/shard_map/update/pallas_call | solution.py:246
  17.6 0.1 collective-permute-start.4
  17.7 1.0 %collective-permute-start.5 = (f32[32,128]{1,0:T(8,128)S(1)}, f32[32,128]{1,0:T(8,128)S(1)}, u32[]{:S(2)}, u32[]{:S(2)}) collective-permute-start(f32[32,128]{1,0:T(8,128)S(1)} %get-tuple-element.41), channel_id=1, source_target_pairs={{0,1},{1,0},{2,3},{3,2},{4,5},{5,4},{6,7},{7,6},{8,9},{9,8},{10,11... | collective-permute-start | bytes 49160 | tf_op jit(solution)/shard_map/ppermute | solution.py:229
  18.7 0.3 coarse.4.coarse_t
  19.0 0.0 collective-permute-done.4.got_even
  19.0 2.5 %collective-permute-done.5.got_odd = f32[32,128]{1,0:T(8,128)S(1)} collective-permute-done((f32[32,128]{1,0:T(8,128)S(1)}, f32[32,128]{1,0:T(8,128)S(1)}, u32[]{:S(2)}, u32[]{:S(2)}) %collective-permute-start.5) | collective-permute-done | bytes 16416 | tf_op jit(solution)/shard_map/ppermute | solution.py:229
  21.6 0.1 middle.4
  21.7 1.0 %collective-permute-start.6 = (f32[32,256]{1,0:T(8,128)S(1)}, f32[32,256]{1,0:T(8,128)S(1)}, u32[]{:S(2)}, u32[]{:S(2)}) collective-permute-start(f32[32,256]{1,0:T(8,128)S(1)} %get-tuple-element.43), channel_id=1, source_target_pairs={{0,1},{1,0},{2,3},{3,2},{4,5},{5,4},{6,7},{7,6},{8,9},{9,8},{10,11... | collective-permute-start | bytes 98312 | tf_op jit(solution)/shard_map/ppermute | solution.py:234
  22.6 1.5 %collective-permute-start.7 = (f32[32,256]{1,0:T(8,128)S(1)}, f32[32,256]{1,0:T(8,128)S(1)}, u32[]{:S(2)}, u32[]{:S(2)}) collective-permute-start(f32[32,256]{1,0:T(8,128)S(1)} %get-tuple-element.44), channel_id=1, source_target_pairs={{0,16},{1,2},{2,1},{3,4},{4,3},{5,6},{6,5},{7,8},{8,7},{9,10},{10,... | collective-permute-start | bytes 98312 | tf_op jit(solution)/shard_map/ppermute | solution.py:235
  24.2 0.5 %forward.4 = f32[1,1024]{1,0:T(1,128)S(1)} custom-call(f32[1,1024]{1,0:T(1,128)S(1)} %get-tuple-element.42.dose_in, f32[1024,1024]{1,0:T(8,128)S(1)} %get-tuple-element.34.pairs), custom_call_target="tpu_custom_call" | custom-call | tf_op jit(solution)/shard_map/forward/pallas_call | solution.py:242
  24.7 0.4 inner.4
  25.1 0.6 %collective-permute-done.6.got_even = f32[32,256]{1,0:T(8,128)S(1)} collective-permute-done((f32[32,256]{1,0:T(8,128)S(1)}, f32[32,256]{1,0:T(8,128)S(1)}, u32[]{:S(2)}, u32[]{:S(2)}) %collective-permute-start.6) | collective-permute-done | bytes 32800 | tf_op jit(solution)/shard_map/ppermute | solution.py:234
  25.7 3.0 %collective-permute-done.7.got_odd = f32[32,256]{1,0:T(8,128)S(1)} collective-permute-done((f32[32,256]{1,0:T(8,128)S(1)}, f32[32,256]{1,0:T(8,128)S(1)}, u32[]{:S(2)}, u32[]{:S(2)}) %collective-permute-start.7) | collective-permute-done | bytes 32800 | tf_op jit(solution)/shard_map/ppermute | solution.py:235
  28.7 0.6 %update.3 = (f32[1,1024]{1,0:T(1,128)S(1)}, f32[32,128]{1,0:T(8,128)S(1)}, f32[32,128]{1,0:T(8,128)S(1)}) custom-call(f32[32,256]{1,0:T(8,128)S(1)} %collective-permute-done.6.got_even, f32[32,256]{1,0:T(8,128)S(1)} %collective-permute-done.7.got_odd, f32[1,1024]{1,0:T(1,128)S(1)} %forward.4, f32[1,1024]{1,0:T(1,128)S(1)} %inner.4, ...), custom_call_target="tpu_custom_call" | custom-call | tf_op jit(solution)/shard_map/update/pallas_call | solution.py:246
  29.3 0.1 collective-permute-start.8
  29.4 0.1 collective-permute-start.9
  29.5 0.3 coarse.5.coarse_t
  29.8 0.8 %collective-permute-done.8.got_even = f32[32,128]{1,0:T(8,128)S(1)} collective-permute-done((f32[32,128]{1,0:T(8,128)S(1)}, f32[32,128]{1,0:T(8,128)S(1)}, u32[]{:S(2)}, u32[]{:S(2)}) %collective-permute-start.8) | collective-permute-done | bytes 16416 | tf_op jit(solution)/shard_map/ppermute | solution.py:228
  30.6 2.6 %collective-permute-done.9.got_odd = f32[32,128]{1,0:T(8,128)S(1)} collective-permute-done((f32[32,128]{1,0:T(8,128)S(1)}, f32[32,128]{1,0:T(8,128)S(1)}, u32[]{:S(2)}, u32[]{:S(2)}) %collective-permute-start.9) | collective-permute-done | bytes 16416 | tf_op jit(solution)/shard_map/ppermute | solution.py:229
  33.2 0.1 middle.5
  33.3 0.1 collective-permute-start.10
  33.4 1.6 %collective-permute-start.11 = (f32[32,256]{1,0:T(8,128)S(1)}, f32[32,256]{1,0:T(8,128)S(1)}, u32[]{:S(2)}, u32[]{:S(2)}) collective-permute-start(f32[32,256]{1,0:T(8,128)S(1)} %get-tuple-element.50), channel_id=1, source_target_pairs={{0,16},{1,2},{2,1},{3,4},{4,3},{5,6},{6,5},{7,8},{8,7},{9,10},{10,... | collective-permute-start | bytes 98312 | tf_op jit(solution)/shard_map/ppermute | solution.py:235
  35.0 0.5 %forward.5 = f32[1,1024]{1,0:T(1,128)S(1)} custom-call(f32[1,1024]{1,0:T(1,128)S(1)} %get-tuple-element.48.dose_in, f32[1024,1024]{1,0:T(8,128)S(1)} %get-tuple-element.34.pairs), custom_call_target="tpu_custom_call" | custom-call | tf_op jit(solution)/shard_map/forward/pallas_call | solution.py:242
  35.5 0.4 inner.5
  35.9 1.4 %collective-permute-done.10.got_even = f32[32,256]{1,0:T(8,128)S(1)} collective-permute-done((f32[32,256]{1,0:T(8,128)S(1)}, f32[32,256]{1,0:T(8,128)S(1)}, u32[]{:S(2)}, u32[]{:S(2)}) %collective-permute-start.10) | collective-permute-done | bytes 32800 | tf_op jit(solution)/shard_map/ppermute | solution.py:234
  37.3 2.2 %collective-permute-done.11.got_odd = f32[32,256]{1,0:T(8,128)S(1)} collective-permute-done((f32[32,256]{1,0:T(8,128)S(1)}, f32[32,256]{1,0:T(8,128)S(1)}, u32[]{:S(2)}, u32[]{:S(2)}) %collective-permute-start.11) | collective-permute-done | bytes 32800 | tf_op jit(solution)/shard_map/ppermute | solution.py:235
  39.5 0.9 %final.1 = (f32[1,1024]{1,0:T(1,128)}, f32[1,1024]{1,0:T(1,128)}) custom-call(f32[32,256]{1,0:T(8,128)S(1)} %collective-permute-done.10.got_even, f32[32,256]{1,0:T(8,128)S(1)} %collective-permute-done.11.got_odd, f32[1,1024]{1,0:T(1,128)S(1)} %forward.5, f32[1,1024]{1,0:T(1,128)S(1)} %inner.5, f32[1,1024]{1,0:T(1,128)S(1)} %get-tuple-element.39.sens, ...), custom_call_target="tpu_custom_call" | custom-call | tf_op jit(solution)/shard_map/final/pallas_call | solution.py:247
Async XLA Ops:
  0.6 0.7 %copy-start.1 = (s32[4,1,1024]{2,1,0:T(1,128)S(1)}, s32[4,1,1024]{2,1,0:T(1,128)}, u32[]{:S(2)}) copy-start(s32[4,1,1024]{2,1,0:T(1,128)} %boxes.5) | copy-start | bytes 49156
  1.4 0.7 %copy-start.3 = (f32[1,1024]{1,0:T(1,128)S(1)}, f32[1,1024]{1,0:T(1,128)}, u32[]{:S(2)}) copy-start(f32[1,1024]{1,0:T(1,128)} %doses.1) | copy-start | bytes 12292
  2.0 0.7 %copy-start.4 = (s32[1,16]{1,0:T(1,128)S(1)}, s32[1,16]{1,0:T(1,128)}, u32[]{:S(2)}) copy-start(s32[1,16]{1,0:T(1,128)} %counts.1) | copy-start | bytes 196
  2.7 0.7 %copy-start.5 = (s32[1,16]{1,0:T(1,128)S(1)}, s32[1,16]{1,0:T(1,128)}, u32[]{:S(2)}) copy-start(s32[1,16]{1,0:T(1,128)} %tails.1) | copy-start | bytes 196
  3.8 4.9 %collective-permute-start = (f32[32,128]{1,0:T(8,128)S(1)}, f32[32,128]{1,0:T(8,128)S(1)}, u32[]{:S(2)}, u32[]{:S(2)}) collective-permute-start(f32[32,128]{1,0:T(8,128)S(1)} %get-tuple-element.27), channel_id=1, source_target_pairs={{0,16},{1,17},{2,18},{3,19},{4,20},{5,21},{6,22},{7,23},{8,24},{9,... | collective-permute-start | bytes 49160 | tf_op jit(solution)/shard_map/ppermute | solution.py:228
  3.9 4.8 %collective-permute-start.1 = (f32[32,128]{1,0:T(8,128)S(1)}, f32[32,128]{1,0:T(8,128)S(1)}, u32[]{:S(2)}, u32[]{:S(2)}) collective-permute-start(f32[32,128]{1,0:T(8,128)S(1)} %get-tuple-element.28), channel_id=1, source_target_pairs={{0,1},{1,0},{2,3},{3,2},{4,5},{5,4},{6,7},{7,6},{8,9},{9,8},{10,11... | collective-permute-start | bytes 49160 | tf_op jit(solution)/shard_map/ppermute | solution.py:229
  5.5 1.2 %copy-start = (f32[512,512]{1,0:T(8,128)S(1)}, f32[512,512]{1,0:T(8,128)}, u32[]{:S(2)}) copy-start(f32[512,512]{1,0:T(8,128)} %gain.1) | copy-start | bytes 3145732
  8.8 8.2 %collective-permute-start.2 = (f32[32,256]{1,0:T(8,128)S(1)}, f32[32,256]{1,0:T(8,128)S(1)}, u32[]{:S(2)}, u32[]{:S(2)}) collective-permute-start(f32[32,256]{1,0:T(8,128)S(1)} %get-tuple-element.32), channel_id=1, source_target_pairs={{0,1},{1,0},{2,3},{3,2},{4,5},{5,4},{6,7},{7,6},{8,9},{9,8},{10,11... | collective-permute-start | bytes 98312 | tf_op jit(solution)/shard_map/ppermute | solution.py:234
  9.4 7.6 %collective-permute-start.3 = (f32[32,256]{1,0:T(8,128)S(1)}, f32[32,256]{1,0:T(8,128)S(1)}, u32[]{:S(2)}, u32[]{:S(2)}) collective-permute-start(f32[32,256]{1,0:T(8,128)S(1)} %get-tuple-element.33), channel_id=1, source_target_pairs={{0,16},{1,2},{2,1},{3,4},{4,3},{5,6},{6,5},{7,8},{8,7},{9,10},{10,... | collective-permute-start | bytes 98312 | tf_op jit(solution)/shard_map/ppermute | solution.py:235
  11.7 0.7 %copy-start.2 = (s32[4,1,1024]{2,1,0:T(1,128)S(1)}, s32[4,1,1024]{2,1,0:T(1,128)}, u32[]{:S(2)}) copy-start(s32[4,1,1024]{2,1,0:T(1,128)} %boxes.5) | copy-start | bytes 49156
  17.6 1.4 %collective-permute-start.4 = (f32[32,128]{1,0:T(8,128)S(1)}, f32[32,128]{1,0:T(8,128)S(1)}, u32[]{:S(2)}, u32[]{:S(2)}) collective-permute-start(f32[32,128]{1,0:T(8,128)S(1)} %get-tuple-element.40), channel_id=1, source_target_pairs={{0,16},{1,17},{2,18},{3,19},{4,20},{5,21},{6,22},{7,23},{8,24},{9,... | collective-permute-start | bytes 49160 | tf_op jit(solution)/shard_map/ppermute | solution.py:228
  17.7 3.8 %collective-permute-start.5 = (f32[32,128]{1,0:T(8,128)S(1)}, f32[32,128]{1,0:T(8,128)S(1)}, u32[]{:S(2)}, u32[]{:S(2)}) collective-permute-start(f32[32,128]{1,0:T(8,128)S(1)} %get-tuple-element.41), channel_id=1, source_target_pairs={{0,1},{1,0},{2,3},{3,2},{4,5},{5,4},{6,7},{7,6},{8,9},{9,8},{10,11... | collective-permute-start | bytes 49160 | tf_op jit(solution)/shard_map/ppermute | solution.py:229
  21.7 4.0 %collective-permute-start.6 = (f32[32,256]{1,0:T(8,128)S(1)}, f32[32,256]{1,0:T(8,128)S(1)}, u32[]{:S(2)}, u32[]{:S(2)}) collective-permute-start(f32[32,256]{1,0:T(8,128)S(1)} %get-tuple-element.43), channel_id=1, source_target_pairs={{0,1},{1,0},{2,3},{3,2},{4,5},{5,4},{6,7},{7,6},{8,9},{9,8},{10,11... | collective-permute-start | bytes 98312 | tf_op jit(solution)/shard_map/ppermute | solution.py:234
  22.6 6.0 %collective-permute-start.7 = (f32[32,256]{1,0:T(8,128)S(1)}, f32[32,256]{1,0:T(8,128)S(1)}, u32[]{:S(2)}, u32[]{:S(2)}) collective-permute-start(f32[32,256]{1,0:T(8,128)S(1)} %get-tuple-element.44), channel_id=1, source_target_pairs={{0,16},{1,2},{2,1},{3,4},{4,3},{5,6},{6,5},{7,8},{8,7},{9,10},{10,... | collective-permute-start | bytes 98312 | tf_op jit(solution)/shard_map/ppermute | solution.py:235
  29.3 1.3 %collective-permute-start.8 = (f32[32,128]{1,0:T(8,128)S(1)}, f32[32,128]{1,0:T(8,128)S(1)}, u32[]{:S(2)}, u32[]{:S(2)}) collective-permute-start(f32[32,128]{1,0:T(8,128)S(1)} %get-tuple-element.46), channel_id=1, source_target_pairs={{0,16},{1,17},{2,18},{3,19},{4,20},{5,21},{6,22},{7,23},{8,24},{9,... | collective-permute-start | bytes 49160 | tf_op jit(solution)/shard_map/ppermute | solution.py:228
  29.4 3.8 %collective-permute-start.9 = (f32[32,128]{1,0:T(8,128)S(1)}, f32[32,128]{1,0:T(8,128)S(1)}, u32[]{:S(2)}, u32[]{:S(2)}) collective-permute-start(f32[32,128]{1,0:T(8,128)S(1)} %get-tuple-element.47), channel_id=1, source_target_pairs={{0,1},{1,0},{2,3},{3,2},{4,5},{5,4},{6,7},{7,6},{8,9},{9,8},{10,11... | collective-permute-start | bytes 49160 | tf_op jit(solution)/shard_map/ppermute | solution.py:229
  33.3 4.0 %collective-permute-start.10 = (f32[32,256]{1,0:T(8,128)S(1)}, f32[32,256]{1,0:T(8,128)S(1)}, u32[]{:S(2)}, u32[]{:S(2)}) collective-permute-start(f32[32,256]{1,0:T(8,128)S(1)} %get-tuple-element.49), channel_id=1, source_target_pairs={{0,1},{1,0},{2,3},{3,2},{4,5},{5,4},{6,7},{7,6},{8,9},{9,8},{10,11... | collective-permute-start | bytes 98312 | tf_op jit(solution)/shard_map/ppermute | solution.py:234
  33.4 6.1 %collective-permute-start.11 = (f32[32,256]{1,0:T(8,128)S(1)}, f32[32,256]{1,0:T(8,128)S(1)}, u32[]{:S(2)}, u32[]{:S(2)}) collective-permute-start(f32[32,256]{1,0:T(8,128)S(1)} %get-tuple-element.50), channel_id=1, source_target_pairs={{0,16},{1,2},{2,1},{3,4},{4,3},{5,6},{6,5},{7,8},{8,7},{9,10},{10,... | collective-permute-start | bytes 98312 | tf_op jit(solution)/shard_map/ppermute | solution.py:235

commit v2 on v1

--- a/solution.py
+++ b/solution.py
@@ -1,4 +1,3 @@
-import functools
 import math
 
 import jax
@@ -7,6 +6,7 @@
 from jax.experimental import pallas as pl
 from jax.experimental.pallas import tpu as pltpu
 from jax.sharding import PartitionSpec as P
+
 
 TILE = 512
 CG = 128
@@ -25,6 +25,8 @@
 BF16 = jnp.bfloat16
 AXES = ("row", "col")
 NT = (((1,), (1,)), ((), ()))
+MAXB = 8
+EARLY = 5 * BLK
 
 
 def pairings():
@@ -92,7 +94,15 @@
     send_odd[...] = jnp.where(even, top, bottom)
 
 
-def start_kernel(boxes, counts, tails, doses, dose_out, send_even, send_odd):
+def start_kernel(boxes_in, counts_in, tails_in, doses_in, boxes, dose_out, send_even, send_odd, counts, tails, doses, arrived):
+    copies = [
+        pltpu.make_async_copy(source, target, arrived.at[k])
+        for k, (source, target) in enumerate(((boxes_in, boxes), (counts_in, counts), (tails_in, tails), (doses_in, doses)))
+    ]
+    for copy in copies:
+        copy.start()
+    for copy in copies:
+        copy.wait()
     col = lax.axis_index("col")
     totals = (counts[...] - 1) * BLK + tails[...]
     total = jnp.sum(jnp.where(iota((1, NTC), 1) == col, totals, 0), axis=1, keepdims=True)
@@ -106,18 +116,32 @@
     row_strips(dose, px_t, py_edges, send_even, send_odd)
 
 
-def sens_kernel(boxes, gain, px_out, py_out, sens_out):
-    px_out[...] = overlap(boxes[0], boxes[2], iota((CG, SLOTS), 0)).astype(BF16)
-    py_out[...] = overlap(boxes[1], boxes[3], iota((CG, SLOTS), 0)).astype(BF16)
-    pixel_x = (boxes[0] + boxes[2]) // 2
-    pixel_y = (boxes[1] + boxes[3]) // 2
-    pixels = iota((TILE, SLOTS), 0)
-    chosen_x = jnp.where(pixels == pixel_x, 1.0, 0.0).astype(BF16)
-    picked = stacked_dot(gain[...], chosen_x, (((1,), (0,)), ((), ())))
-    sens_out[...] = jnp.sum(jnp.where(pixels == pixel_y, picked, 0.0), axis=0, keepdims=True)
-
-
-def setup_kernel(boxes, wy_high, wy_low, wx_out, pairs):
+def build_pairs(boxes, pairs, first_shot):
+    inverse = 1.0 / FORWARD_RANGE
+    box = [boxes[k].astype(F32) for k in range(4)]
+    centre_x = (box[0] + box[2]) * (0.5 * inverse)
+    centre_y = (box[1] + box[3]) * (0.5 * inverse)
+    columns = jnp.concatenate([b * inverse for b in box] + [jnp.zeros((4, SLOTS), F32)], axis=0)
+    for at in range(0, pairs.shape[0], BLK):
+        side = jnp.transpose(columns[:, first_shot + at : first_shot + at + BLK])
+        along_x = lax.erf(centre_x - side[:, 0:1]) - lax.erf(centre_x - side[:, 2:3])
+        along_y = lax.erf(centre_y - side[:, 1:2]) - lax.erf(centre_y - side[:, 3:4])
+        pairs[at : at + BLK, :] = (0.25 * along_x) * along_y
+
+
+def early_kernel(boxes, dose_in, gain_in, px_out, py_out, coarse_t, pairs, gain, arrived):
+    copy = pltpu.make_async_copy(gain_in, gain, arrived)
+    copy.start()
+    px = overlap(boxes[0], boxes[2], iota((CG, SLOTS), 0))
+    py = overlap(boxes[1], boxes[3], iota((CG, SLOTS), 0)).astype(BF16)
+    px_out[...] = px.astype(BF16)
+    py_out[...] = py
+    coarse_t[...] = stacked_dot(px * dose_in[...], py, NT)
+    build_pairs(boxes, pairs, 0)
+    copy.wait()
+
+
+def late_kernel(boxes, gain, wy_high, wy_low, wx_out, pairs, sens_out):
     cell_x = (boxes[0] + boxes[2]) // (2 * CELL)
     cell_y = (boxes[1] + boxes[3]) // (2 * CELL)
     y = iota((2 * CG, SLOTS), 0)
@@ -127,27 +151,24 @@
     x = iota((CG + 2 * REACH, SLOTS), 0)
     place = jnp.where(x < CG, x, jnp.where(x < CG + REACH, x - (CG + REACH), x - REACH))
     wx_out[...] = spread(cell_x - place)
-    inverse = 1.0 / FORWARD_RANGE
-    box = [boxes[k].astype(F32) for k in range(4)]
-    centre_x = (box[0] + box[2]) * (0.5 * inverse)
-    centre_y = (box[1] + box[3]) * (0.5 * inverse)
-    columns = jnp.concatenate([b * inverse for b in box] + [jnp.zeros((4, SLOTS), F32)], axis=0)
-    step = 128
-    for first in range(0, SLOTS, step):
-        side = jnp.transpose(columns[:, first : first + step])
-        along_x = lax.erf(centre_x - side[:, 0:1]) - lax.erf(centre_x - side[:, 2:3])
-        along_y = lax.erf(centre_y - side[:, 1:2]) - lax.erf(centre_y - side[:, 3:4])
-        pairs[first : first + step, :] = (0.25 * along_x) * along_y
-
-
-def forward_kernel(dose_in, pairs, forward):
+    pixel_x = (boxes[0] + boxes[2]) // 2
+    pixel_y = (boxes[1] + boxes[3]) // 2
+    pixels = iota((TILE, SLOTS), 0)
+    chosen_x = jnp.where(pixels == pixel_x, 1.0, 0.0).astype(BF16)
+    picked = stacked_dot(gain[...], chosen_x, (((1,), (0,)), ((), ())))
+    sens_out[...] = jnp.sum(jnp.where(pixels == pixel_y, picked, 0.0), axis=0, keepdims=True)
+    build_pairs(boxes, pairs, EARLY)
+
+
+def forward_kernel(dose_in, early_pairs, late_pairs, forward):
     dose = dose_in[...]
-    folded = jnp.concatenate([dose[:, k * 128 : (k + 1) * 128] for k in range(8)], axis=0)
+    folded = jnp.concatenate([dose[:, k * BLK : (k + 1) * BLK] for k in range(MAXB)], axis=0)
     columns = jnp.transpose(folded)
     total = jnp.zeros((8, SLOTS), F32)
-    for k in range(8):
-        part = columns[:, k : k + 1] * pairs[k * 128 : (k + 1) * 128, :]
-        total += jnp.sum(part.reshape(16, 8, SLOTS), axis=0)
+    for k in range(MAXB):
+        at = k * BLK
+        pairs = early_pairs[at : at + BLK, :] if at < EARLY else late_pairs[at - EARLY : at - EARLY + BLK, :]
+        total += jnp.sum((columns[:, k : k + 1] * pairs).reshape(BLK // 8, 8, SLOTS), axis=0)
     forward[...] = jnp.sum(total, axis=0, keepdims=True)
 
 
@@ -208,13 +229,18 @@
     return jax.ShapeDtypeStruct(dims, dtype)
 
 
-def call(kernel, outs, name, vmem=16, flops=0, moved=0):
+HBM = pl.BlockSpec(memory_space=pltpu.HBM)
+VMEM = pl.BlockSpec(memory_space=pltpu.VMEM)
+
+
+def call(kernel, outs, vmem=16, ins=None, scratch=()):
+    extra = {} if ins is None else {"in_specs": ins}
     return pl.pallas_call(
         kernel,
         out_shape=outs,
-        name=name,
+        scratch_shapes=scratch,
         compiler_params=pltpu.CompilerParams(vmem_limit_bytes=vmem << 20),
-        cost_estimate=pl.CostEstimate(flops=flops, bytes_accessed=moved, transcendentals=0),
+        **extra,
     )
 
 
@@ -223,28 +249,38 @@
     row = shape(1, SLOTS)
     strip = shape(REACH, CG)
     wide = shape(REACH, 2 * CG)
-    dose, strip_even, strip_odd = call(start_kernel, (row, strip, strip), "start")(shot_boxes, block_counts, tail_shots, doses)
+    half = shape(2 * CG, SLOTS, dtype=BF16)
+    boxes, dose, strip_even, strip_odd = call(
+        start_kernel,
+        (shape(4, 1, SLOTS, dtype=jnp.int32), row, strip, strip),
+        ins=[HBM] * 4,
+        scratch=(pltpu.VMEM((1, NTC), jnp.int32), pltpu.VMEM((1, NTC), jnp.int32), pltpu.VMEM((1, SLOTS), F32), pltpu.SemaphoreType.DMA((4,))),
+    )(*[pltpu.with_memory_space_constraint(a, pltpu.HBM) for a in (shot_boxes, block_counts, tail_shots, doses)])
     for sweep in range(ITERS):
+        got_odd = lax.ppermute(strip_odd, AXES, row_odd)
         got_even = lax.ppermute(strip_even, AXES, row_even)
-        got_odd = lax.ppermute(strip_odd, AXES, row_odd)
         if sweep == 0:
-            px, py, sens = call(sens_kernel, (shape(CG, SLOTS, dtype=BF16), shape(CG, SLOTS, dtype=BF16), row), "sens")(shot_boxes, pixel_gain)
-        coarse_t = call(coarse_kernel, shape(CG, CG), "coarse")(dose, px, py)
-        tall_t, wide_even, wide_odd = call(middle_kernel, (shape(CG, 2 * CG), wide, wide), "middle")(got_even, got_odd, coarse_t)
+            px, py, coarse_t, early_pairs, gain = call(
+                early_kernel,
+                (shape(CG, SLOTS, dtype=BF16), shape(CG, SLOTS, dtype=BF16), shape(CG, CG), shape(EARLY, SLOTS), shape(TILE, TILE)),
+                ins=[VMEM, VMEM, HBM],
+                scratch=(pltpu.SemaphoreType.DMA,),
+            )(boxes, dose, pltpu.with_memory_space_constraint(pixel_gain, pltpu.HBM))
+        else:
+            coarse_t = call(coarse_kernel, shape(CG, CG))(dose, px, py)
+        tall_t, wide_even, wide_odd = call(middle_kernel, (shape(CG, 2 * CG), wide, wide))(got_even, got_odd, coarse_t)
+        far_odd = lax.ppermute(wide_odd, AXES, col_odd)
         far_even = lax.ppermute(wide_even, AXES, col_even)
-        far_odd = lax.ppermute(wide_odd, AXES, col_odd)
         if sweep == 0:
-            wy_high, wy_low, wx, pairs = call(
-                setup_kernel,
-                (shape(2 * CG, SLOTS, dtype=BF16), shape(2 * CG, SLOTS, dtype=BF16), shape(CG + 2 * REACH, SLOTS), shape(SLOTS, SLOTS)),
-                "setup",
-            )(shot_boxes)
-        forward = call(forward_kernel, row, "forward")(dose, pairs)
-        inner = call(inner_kernel, row, "inner")(tall_t, wy_high, wy_low, wx)
+            wy_high, wy_low, wx, late_pairs, sens = call(
+                late_kernel, (half, half, shape(CG + 2 * REACH, SLOTS), shape(SLOTS - EARLY, SLOTS), row)
+            )(boxes, gain)
+        forward = call(forward_kernel, row)(dose, early_pairs, late_pairs)
+        inner = call(inner_kernel, row)(tall_t, wy_high, wy_low, wx)
         common = (far_even, far_odd, forward, inner, sens, dose, wy_high, wy_low, wx)
         if sweep < ITERS - 1:
-            dose, strip_even, strip_odd = call(update_kernel, (row, strip, strip), "update")(*common, px, py)
-    return call(final_kernel, (row, row), "final")(*common)
+            dose, strip_even, strip_odd = call(update_kernel, (row, strip, strip))(*common, px, py)
+    return call(final_kernel, (row, row))(*common)
 
 
 def solution(mesh):

time: 40.8 us -> 36.6 us (0.90)
  local copies, waits for them, and re-layouts: 4.65 us -> 0 us
  waiting for transfers between devices: 13.1 us -> 14.6 us
  starting transfers between devices: 10 us -> 9.39 us
    unnamed x12 -> x0, local copies, waits for them, and re-layouts: 4.65 us -> none
    ppermute x3, starting transfers between devices: 5.45 us -> 4.79 us  [body(): far_odd = lax.ppermute(wide_odd, AXES, col_odd)]
    ppermute x3, starting transfers between devices: 1.67 us -> 2.17 us  [body(): far_even = lax.ppermute(wide_even, AXES, col_even)]
    ppermute x3, waiting for transfers between devices: 1.98 us -> 2.48 us  [body(): far_even = lax.ppermute(wide_even, AXES, col_even)]
    ppermute x3, starting transfers between devices: 2.63 us -> 2.17 us  [body(): got_odd = lax.ppermute(strip_odd, AXES, row_odd)]
    ppermute x3, waiting for transfers between devices: 5.18 us -> 5.62 us  [body(): got_odd = lax.ppermute(strip_odd, AXES, row_odd)]
    pallas_call x18 -> x17, Pallas kernels: 11.8 us -> 11.6 us  [the longest x1 2.86 us: body(): call(late_kernel, (half, half, shape(CG + 2 * REACH, SLOTS), shape(SLOTS...]
  transfers between devices with their start and end apart: 12 -> 12, of which waited for: 7 -> 10; matrix products, arithmetic and copies ran while one was open for 0% -> 0% of each run, Pallas kernels for 22% -> 22%
where the time goes in v2:
time: 36.6 us; the launch traced here: 36.4 us
  waiting for transfers between devices  14.6 us (40%)
  Pallas kernels  11.6 us (32%)
  starting transfers between devices  9.39 us (26%)
  between operations  0.84 us (2%)
    ppermute x3, waiting for transfers between devices, body(): got_odd = lax.ppermute(strip_odd, AXES, row_odd)  5.62 us
    ppermute x3, waiting for transfers between devices, body(): far_odd = lax.ppermute(wide_odd, AXES, col_odd)  5.38 us
    ppermute x3, starting transfers between devices, body(): far_odd = lax.ppermute(wide_odd, AXES, col_odd)  4.79 us
    pallas_call x1, Pallas kernels, body(): call(late_kernel, (half, half, shape(CG + 2 * REACH, SLOTS), shape(SLOTS...  2.86 us
    ppermute x3, waiting for transfers between devices, body(): far_even = lax.ppermute(wide_even, AXES, col_even)  2.48 us
    ppermute x3, starting transfers between devices, body(): got_odd = lax.ppermute(strip_odd, AXES, row_odd)  2.17 us
    ppermute x3, starting transfers between devices, body(): far_even = lax.ppermute(wide_even, AXES, col_even)  2.17 us
    pallas_call x1, Pallas kernels, body(): call(early_kernel, (shape(CG, SLOTS, dtype=BF16), shape(CG, SLOTS, dtype=...  1.91 us
  transfers between devices with their start and end apart: 12, of which 10 were waited for; matrix products, arithmetic and copies ran while one was open for 0% of the time, Pallas kernels for 22%

profile of v2, /device:TPU:64, one launch (start us, length us, event | category | flops | bytes accessed | tf_op | source)
XLA Modules:
  0.0 36.4 jit_solution(4732373467697333185)
XLA Ops:
  0.6 1.2 %shard_map.68 = (s32[4,1,1024]{2,1,0:T(1,128)S(1)}, f32[1,1024]{1,0:T(1,128)S(1)}, f32[32,128]{1,0:T(8,128)S(1)}, f32[32,128]{1,0:T(8,128)S(1)}) custom-call(s32[4,1,1024]{2,1,0:T(1,128)} %boxes_in.1, s32[1,16]{1,0:T(1,128)} %counts_in.1, s32[1,16]{1,0:T(1,128)} %tails_in.1, f32[1,1024]{1,0:T(1,128)} %doses_in.1), custom_call_target="tpu_custom_call" | custom-call | tf_op jit(solution)/shard_map/pallas_call | solution.py:253
  1.9 0.1 collective-permute-start
  1.9 1.6 %collective-permute-start.1 = (f32[32,128]{1,0:T(8,128)S(1)}, f32[32,128]{1,0:T(8,128)S(1)}, u32[]{:S(2)}, u32[]{:S(2)}) collective-permute-start(f32[32,128]{1,0:T(8,128)S(1)} %get-tuple-element.32), channel_id=1, source_target_pairs={{0,1},{1,0},{2,3},{3,2},{4,5},{5,4},{6,7},{7,6},{8,9},{9,8},{10,11... | collective-permute-start | bytes 49160 | tf_op jit(solution)/shard_map/ppermute | solution.py:260
  3.5 1.9 %shard_map.69 = (bf16[128,1024]{1,0:T(8,128)(2,1)S(1)}, bf16[128,1024]{1,0:T(8,128)(2,1)S(1)}, f32[128,128]{1,0:T(8,128)S(1)}, f32[640,1024]{1,0:T(8,128)S(1)}, f32[512,512]{1,0:T(8,128)S(1)}) custom-call(s32[4,1,1024]{2,1,0:T(1,128)S(1)} %get-tuple-element.33.boxes, f32[1,1024]{1,0:T(1,128)S(1)} %get-tuple-element.34.dose_in, f32[512,512]{1,0:T(8,128)} %gain_in.1), custom_call_target="tpu_custom_call" | custom-call | tf_op jit(solution)/shard_map/pallas_call | solution.py:263
  5.4 0.0 collective-permute-done.got_even
  5.4 0.3 collective-permute-done.1.got_odd
  5.8 0.1 shard_map.70
  5.9 1.6 %collective-permute-start.2 = (f32[32,256]{1,0:T(8,128)S(1)}, f32[32,256]{1,0:T(8,128)S(1)}, u32[]{:S(2)}, u32[]{:S(2)}) collective-permute-start(f32[32,256]{1,0:T(8,128)S(1)} %get-tuple-element.36), channel_id=1, source_target_pairs={{0,1},{1,0},{2,3},{3,2},{4,5},{5,4},{6,7},{7,6},{8,9},{9,8},{10,11... | collective-permute-start | bytes 98312 | tf_op jit(solution)/shard_map/ppermute | solution.py:273
  7.4 1.6 %collective-permute-start.3 = (f32[32,256]{1,0:T(8,128)S(1)}, f32[32,256]{1,0:T(8,128)S(1)}, u32[]{:S(2)}, u32[]{:S(2)}) collective-permute-start(f32[32,256]{1,0:T(8,128)S(1)} %get-tuple-element.37), channel_id=1, source_target_pairs={{0,16},{1,2},{2,1},{3,4},{4,3},{5,6},{6,5},{7,8},{8,7},{9,10},{10,... | collective-permute-start | bytes 98312 | tf_op jit(solution)/shard_map/ppermute | solution.py:272
  9.1 2.9 %shard_map.71 = (bf16[256,1024]{1,0:T(8,128)(2,1)S(1)}, bf16[256,1024]{1,0:T(8,128)(2,1)S(1)}, f32[192,1024]{1,0:T(8,128)S(1)}, f32[384,1024]{1,0:T(8,128)S(1)}, f32[1,1024]{1,0:T(1,128)S(1)}) custom-call(s32[4,1,1024]{2,1,0:T(1,128)S(1)} %get-tuple-element.33.boxes, f32[512,512]{1,0:T(8,128)S(1)} %get-tuple-element.39.gain), custom_call_target="tpu_custom_call" | custom-call | tf_op jit(solution)/shard_map/pallas_call | solution.py:275
  12.0 0.5 %shard_map.72.forward = f32[1,1024]{1,0:T(1,128)S(1)} custom-call(f32[1,1024]{1,0:T(1,128)S(1)} %get-tuple-element.34.dose_in, f32[640,1024]{1,0:T(8,128)S(1)} %get-tuple-element.38.early_pairs, f32[384,1024]{1,0:T(8,128)S(1)} %get-tuple-element.40.late_pairs), custom_call_target="tpu_custom_call" | custom-call | tf_op jit(solution)/shard_map/pallas_call | solution.py:278
  12.4 0.4 %shard_map.73.inner = f32[1,1024]{1,0:T(1,128)S(1)} custom-call(f32[128,256]{1,0:T(8,128)S(1)} %get-tuple-element.41.tall_t, bf16[256,1024]{1,0:T(8,128)(2,1)S(1)} %get-tuple-element.42.wy_high, bf16[256,1024]{1,0:T(8,128)(2,1)S(1)} %get-tuple-element.43.wy_low, f32[192,1024]{1,0:T(8,128)S(1)} %get-tuple-element.44.wx), custom_call_target="tpu_custom_call" | custom-call | tf_op jit(solution)/shard_map/pallas_call | solution.py:279
  12.8 0.0 collective-permute-done.2.got_even
  12.8 0.6 %collective-permute-done.3.got_odd = f32[32,256]{1,0:T(8,128)S(1)} collective-permute-done((f32[32,256]{1,0:T(8,128)S(1)}, f32[32,256]{1,0:T(8,128)S(1)}, u32[]{:S(2)}, u32[]{:S(2)}) %collective-permute-start.3) | collective-permute-done | bytes 32800 | tf_op jit(solution)/shard_map/ppermute | solution.py:272
  13.5 0.6 %shard_map.74 = (f32[1,1024]{1,0:T(1,128)S(1)}, f32[32,128]{1,0:T(8,128)S(1)}, f32[32,128]{1,0:T(8,128)S(1)}) custom-call(f32[32,256]{1,0:T(8,128)S(1)} %collective-permute-done.2.got_even, f32[32,256]{1,0:T(8,128)S(1)} %collective-permute-done.3.got_odd, f32[1,1024]{1,0:T(1,128)S(1)} %shard_map.72.forward, f32[1,1024]{1,0:T(1,128)S(1)} %shard_map.73.inner, ...), custom_call_target="tpu_custom_call" | custom-call | tf_op jit(solution)/shard_map/pallas_call | solution.py:282
  14.1 0.1 collective-permute-start.4
  14.2 0.5 %collective-permute-start.5 = (f32[32,128]{1,0:T(8,128)S(1)}, f32[32,128]{1,0:T(8,128)S(1)}, u32[]{:S(2)}, u32[]{:S(2)}) collective-permute-start(f32[32,128]{1,0:T(8,128)S(1)} %get-tuple-element.49), channel_id=1, source_target_pairs={{0,1},{1,0},{2,3},{3,2},{4,5},{5,4},{6,7},{7,6},{8,9},{9,8},{10,11... | collective-permute-start | bytes 49160 | tf_op jit(solution)/shard_map/ppermute | solution.py:260
  14.7 0.3 shard_map.75.coarse_t
  15.0 0.3 collective-permute-done.4.got_even
  15.4 2.6 %collective-permute-done.5.got_odd = f32[32,128]{1,0:T(8,128)S(1)} collective-permute-done((f32[32,128]{1,0:T(8,128)S(1)}, f32[32,128]{1,0:T(8,128)S(1)}, u32[]{:S(2)}, u32[]{:S(2)}) %collective-permute-start.5) | collective-permute-done | bytes 16416 | tf_op jit(solution)/shard_map/ppermute | solution.py:260
  18.0 0.1 shard_map.76
  18.1 0.5 %collective-permute-start.6 = (f32[32,256]{1,0:T(8,128)S(1)}, f32[32,256]{1,0:T(8,128)S(1)}, u32[]{:S(2)}, u32[]{:S(2)}) collective-permute-start(f32[32,256]{1,0:T(8,128)S(1)} %get-tuple-element.51), channel_id=1, source_target_pairs={{0,1},{1,0},{2,3},{3,2},{4,5},{5,4},{6,7},{7,6},{8,9},{9,8},{10,11... | collective-permute-start | bytes 98312 | tf_op jit(solution)/shard_map/ppermute | solution.py:273
  18.6 1.5 %collective-permute-start.7 = (f32[32,256]{1,0:T(8,128)S(1)}, f32[32,256]{1,0:T(8,128)S(1)}, u32[]{:S(2)}, u32[]{:S(2)}) collective-permute-start(f32[32,256]{1,0:T(8,128)S(1)} %get-tuple-element.52), channel_id=1, source_target_pairs={{0,16},{1,2},{2,1},{3,4},{4,3},{5,6},{6,5},{7,8},{8,7},{9,10},{10,... | collective-permute-start | bytes 98312 | tf_op jit(solution)/shard_map/ppermute | solution.py:272
  20.2 0.5 %shard_map.77.forward = f32[1,1024]{1,0:T(1,128)S(1)} custom-call(f32[1,1024]{1,0:T(1,128)S(1)} %get-tuple-element.50.dose_in, f32[640,1024]{1,0:T(8,128)S(1)} %get-tuple-element.38.early_pairs, f32[384,1024]{1,0:T(8,128)S(1)} %get-tuple-element.40.late_pairs), custom_call_target="tpu_custom_call" | custom-call | tf_op jit(solution)/shard_map/pallas_call | solution.py:278
  20.7 0.4 %shard_map.78.inner = f32[1,1024]{1,0:T(1,128)S(1)} custom-call(f32[128,256]{1,0:T(8,128)S(1)} %get-tuple-element.53.tall_t, bf16[256,1024]{1,0:T(8,128)(2,1)S(1)} %get-tuple-element.42.wy_high, bf16[256,1024]{1,0:T(8,128)(2,1)S(1)} %get-tuple-element.43.wy_low, f32[192,1024]{1,0:T(8,128)S(1)} %get-tuple-element.44.wx), custom_call_target="tpu_custom_call" | custom-call | tf_op jit(solution)/shard_map/pallas_call | solution.py:279
  21.0 1.1 %collective-permute-done.6.got_even = f32[32,256]{1,0:T(8,128)S(1)} collective-permute-done((f32[32,256]{1,0:T(8,128)S(1)}, f32[32,256]{1,0:T(8,128)S(1)}, u32[]{:S(2)}, u32[]{:S(2)}) %collective-permute-start.6) | collective-permute-done | bytes 32800 | tf_op jit(solution)/shard_map/ppermute | solution.py:273
  22.1 2.5 %collective-permute-done.7.got_odd = f32[32,256]{1,0:T(8,128)S(1)} collective-permute-done((f32[32,256]{1,0:T(8,128)S(1)}, f32[32,256]{1,0:T(8,128)S(1)}, u32[]{:S(2)}, u32[]{:S(2)}) %collective-permute-start.7) | collective-permute-done | bytes 32800 | tf_op jit(solution)/shard_map/ppermute | solution.py:272
  24.7 0.6 %shard_map.79 = (f32[1,1024]{1,0:T(1,128)S(1)}, f32[32,128]{1,0:T(8,128)S(1)}, f32[32,128]{1,0:T(8,128)S(1)}) custom-call(f32[32,256]{1,0:T(8,128)S(1)} %collective-permute-done.6.got_even, f32[32,256]{1,0:T(8,128)S(1)} %collective-permute-done.7.got_odd, f32[1,1024]{1,0:T(1,128)S(1)} %shard_map.77.forward, f32[1,1024]{1,0:T(1,128)S(1)} %shard_map.78.inner, ...), custom_call_target="tpu_custom_call" | custom-call | tf_op jit(solution)/shard_map/pallas_call | solution.py:282
  25.3 0.1 collective-permute-start.8
  25.4 0.1 collective-permute-start.9
  25.5 0.3 shard_map.80.coarse_t
  25.8 0.8 %collective-permute-done.8.got_even = f32[32,128]{1,0:T(8,128)S(1)} collective-permute-done((f32[32,128]{1,0:T(8,128)S(1)}, f32[32,128]{1,0:T(8,128)S(1)}, u32[]{:S(2)}, u32[]{:S(2)}) %collective-permute-start.8) | collective-permute-done | bytes 16416 | tf_op jit(solution)/shard_map/ppermute | solution.py:261
  26.6 2.6 %collective-permute-done.9.got_odd = f32[32,128]{1,0:T(8,128)S(1)} collective-permute-done((f32[32,128]{1,0:T(8,128)S(1)}, f32[32,128]{1,0:T(8,128)S(1)}, u32[]{:S(2)}, u32[]{:S(2)}) %collective-permute-start.9) | collective-permute-done | bytes 16416 | tf_op jit(solution)/shard_map/ppermute | solution.py:260
  29.2 0.1 shard_map.81
  29.3 0.1 collective-permute-start.10
  29.4 1.6 %collective-permute-start.11 = (f32[32,256]{1,0:T(8,128)S(1)}, f32[32,256]{1,0:T(8,128)S(1)}, u32[]{:S(2)}, u32[]{:S(2)}) collective-permute-start(f32[32,256]{1,0:T(8,128)S(1)} %get-tuple-element.58), channel_id=1, source_target_pairs={{0,16},{1,2},{2,1},{3,4},{4,3},{5,6},{6,5},{7,8},{8,7},{9,10},{10,... | collective-permute-start | bytes 98312 | tf_op jit(solution)/shard_map/ppermute | solution.py:272
  31.0 0.5 %shard_map.82.forward = f32[1,1024]{1,0:T(1,128)S(1)} custom-call(f32[1,1024]{1,0:T(1,128)S(1)} %get-tuple-element.56.dose_in, f32[640,1024]{1,0:T(8,128)S(1)} %get-tuple-element.38.early_pairs, f32[384,1024]{1,0:T(8,128)S(1)} %get-tuple-element.40.late_pairs), custom_call_target="tpu_custom_call" | custom-call | tf_op jit(solution)/shard_map/pallas_call | solution.py:278
  31.5 0.4 %shard_map.83.inner = f32[1,1024]{1,0:T(1,128)S(1)} custom-call(f32[128,256]{1,0:T(8,128)S(1)} %get-tuple-element.59.tall_t, bf16[256,1024]{1,0:T(8,128)(2,1)S(1)} %get-tuple-element.42.wy_high, bf16[256,1024]{1,0:T(8,128)(2,1)S(1)} %get-tuple-element.43.wy_low, f32[192,1024]{1,0:T(8,128)S(1)} %get-tuple-element.44.wx), custom_call_target="tpu_custom_call" | custom-call | tf_op jit(solution)/shard_map/pallas_call | solution.py:279
  31.9 1.4 %collective-permute-done.10.got_even = f32[32,256]{1,0:T(8,128)S(1)} collective-permute-done((f32[32,256]{1,0:T(8,128)S(1)}, f32[32,256]{1,0:T(8,128)S(1)}, u32[]{:S(2)}, u32[]{:S(2)}) %collective-permute-start.10) | collective-permute-done | bytes 32800 | tf_op jit(solution)/shard_map/ppermute | solution.py:273
  33.3 2.2 %collective-permute-done.11.got_odd = f32[32,256]{1,0:T(8,128)S(1)} collective-permute-done((f32[32,256]{1,0:T(8,128)S(1)}, f32[32,256]{1,0:T(8,128)S(1)}, u32[]{:S(2)}, u32[]{:S(2)}) %collective-permute-start.11) | collective-permute-done | bytes 32800 | tf_op jit(solution)/shard_map/ppermute | solution.py:272
  35.5 0.9 %shard_map.84 = (f32[1,1024]{1,0:T(1,128)}, f32[1,1024]{1,0:T(1,128)}) custom-call(f32[32,256]{1,0:T(8,128)S(1)} %collective-permute-done.10.got_even, f32[32,256]{1,0:T(8,128)S(1)} %collective-permute-done.11.got_odd, f32[1,1024]{1,0:T(1,128)S(1)} %shard_map.82.forward, f32[1,1024]{1,0:T(1,128)S(1)} %shard_map.83.inner, ...), custom_call_target="tpu_custom_call" | custom-call | tf_op jit(solution)/shard_map/pallas_call | solution.py:283
Async XLA Ops:
  1.9 3.6 %collective-permute-start = (f32[32,128]{1,0:T(8,128)S(1)}, f32[32,128]{1,0:T(8,128)S(1)}, u32[]{:S(2)}, u32[]{:S(2)}) collective-permute-start(f32[32,128]{1,0:T(8,128)S(1)} %get-tuple-element.31), channel_id=1, source_target_pairs={{0,16},{1,17},{2,18},{3,19},{4,20},{5,21},{6,22},{7,23},{8,24},{9,... | collective-permute-start | bytes 49160 | tf_op jit(solution)/shard_map/ppermute | solution.py:261
  1.9 3.8 %collective-permute-start.1 = (f32[32,128]{1,0:T(8,128)S(1)}, f32[32,128]{1,0:T(8,128)S(1)}, u32[]{:S(2)}, u32[]{:S(2)}) collective-permute-start(f32[32,128]{1,0:T(8,128)S(1)} %get-tuple-element.32), channel_id=1, source_target_pairs={{0,1},{1,0},{2,3},{3,2},{4,5},{5,4},{6,7},{7,6},{8,9},{9,8},{10,11... | collective-permute-start | bytes 49160 | tf_op jit(solution)/shard_map/ppermute | solution.py:260
  5.9 7.0 %collective-permute-start.2 = (f32[32,256]{1,0:T(8,128)S(1)}, f32[32,256]{1,0:T(8,128)S(1)}, u32[]{:S(2)}, u32[]{:S(2)}) collective-permute-start(f32[32,256]{1,0:T(8,128)S(1)} %get-tuple-element.36), channel_id=1, source_target_pairs={{0,1},{1,0},{2,3},{3,2},{4,5},{5,4},{6,7},{7,6},{8,9},{9,8},{10,11... | collective-permute-start | bytes 98312 | tf_op jit(solution)/shard_map/ppermute | solution.py:273
  7.4 6.0 %collective-permute-start.3 = (f32[32,256]{1,0:T(8,128)S(1)}, f32[32,256]{1,0:T(8,128)S(1)}, u32[]{:S(2)}, u32[]{:S(2)}) collective-permute-start(f32[32,256]{1,0:T(8,128)S(1)} %get-tuple-element.37), channel_id=1, source_target_pairs={{0,16},{1,2},{2,1},{3,4},{4,3},{5,6},{6,5},{7,8},{8,7},{9,10},{10,... | collective-permute-start | bytes 98312 | tf_op jit(solution)/shard_map/ppermute | solution.py:272
  14.1 1.3 %collective-permute-start.4 = (f32[32,128]{1,0:T(8,128)S(1)}, f32[32,128]{1,0:T(8,128)S(1)}, u32[]{:S(2)}, u32[]{:S(2)}) collective-permute-start(f32[32,128]{1,0:T(8,128)S(1)} %get-tuple-element.48), channel_id=1, source_target_pairs={{0,16},{1,17},{2,18},{3,19},{4,20},{5,21},{6,22},{7,23},{8,24},{9,... | collective-permute-start | bytes 49160 | tf_op jit(solution)/shard_map/ppermute | solution.py:261
  14.2 3.8 %collective-permute-start.5 = (f32[32,128]{1,0:T(8,128)S(1)}, f32[32,128]{1,0:T(8,128)S(1)}, u32[]{:S(2)}, u32[]{:S(2)}) collective-permute-start(f32[32,128]{1,0:T(8,128)S(1)} %get-tuple-element.49), channel_id=1, source_target_pairs={{0,1},{1,0},{2,3},{3,2},{4,5},{5,4},{6,7},{7,6},{8,9},{9,8},{10,11... | collective-permute-start | bytes 49160 | tf_op jit(solution)/shard_map/ppermute | solution.py:260
  18.1 4.0 %collective-permute-start.6 = (f32[32,256]{1,0:T(8,128)S(1)}, f32[32,256]{1,0:T(8,128)S(1)}, u32[]{:S(2)}, u32[]{:S(2)}) collective-permute-start(f32[32,256]{1,0:T(8,128)S(1)} %get-tuple-element.51), channel_id=1, source_target_pairs={{0,1},{1,0},{2,3},{3,2},{4,5},{5,4},{6,7},{7,6},{8,9},{9,8},{10,11... | collective-permute-start | bytes 98312 | tf_op jit(solution)/shard_map/ppermute | solution.py:273
  18.6 6.0 %collective-permute-start.7 = (f32[32,256]{1,0:T(8,128)S(1)}, f32[32,256]{1,0:T(8,128)S(1)}, u32[]{:S(2)}, u32[]{:S(2)}) collective-permute-start(f32[32,256]{1,0:T(8,128)S(1)} %get-tuple-element.52), channel_id=1, source_target_pairs={{0,16},{1,2},{2,1},{3,4},{4,3},{5,6},{6,5},{7,8},{8,7},{9,10},{10,... | collective-permute-start | bytes 98312 | tf_op jit(solution)/shard_map/ppermute | solution.py:272
  25.3 1.3 %collective-permute-start.8 = (f32[32,128]{1,0:T(8,128)S(1)}, f32[32,128]{1,0:T(8,128)S(1)}, u32[]{:S(2)}, u32[]{:S(2)}) collective-permute-start(f32[32,128]{1,0:T(8,128)S(1)} %get-tuple-element.54), channel_id=1, source_target_pairs={{0,16},{1,17},{2,18},{3,19},{4,20},{5,21},{6,22},{7,23},{8,24},{9,... | collective-permute-start | bytes 49160 | tf_op jit(solution)/shard_map/ppermute | solution.py:261
  25.4 3.8 %collective-permute-start.9 = (f32[32,128]{1,0:T(8,128)S(1)}, f32[32,128]{1,0:T(8,128)S(1)}, u32[]{:S(2)}, u32[]{:S(2)}) collective-permute-start(f32[32,128]{1,0:T(8,128)S(1)} %get-tuple-element.55), channel_id=1, source_target_pairs={{0,1},{1,0},{2,3},{3,2},{4,5},{5,4},{6,7},{7,6},{8,9},{9,8},{10,11... | collective-permute-start | bytes 49160 | tf_op jit(solution)/shard_map/ppermute | solution.py:260
  29.3 4.0 %collective-permute-start.10 = (f32[32,256]{1,0:T(8,128)S(1)}, f32[32,256]{1,0:T(8,128)S(1)}, u32[]{:S(2)}, u32[]{:S(2)}) collective-permute-start(f32[32,256]{1,0:T(8,128)S(1)} %get-tuple-element.57), channel_id=1, source_target_pairs={{0,1},{1,0},{2,3},{3,2},{4,5},{5,4},{6,7},{7,6},{8,9},{9,8},{10,11... | collective-permute-start | bytes 98312 | tf_op jit(solution)/shard_map/ppermute | solution.py:273
  29.4 6.1 %collective-permute-start.11 = (f32[32,256]{1,0:T(8,128)S(1)}, f32[32,256]{1,0:T(8,128)S(1)}, u32[]{:S(2)}, u32[]{:S(2)}) collective-permute-start(f32[32,256]{1,0:T(8,128)S(1)} %get-tuple-element.58), channel_id=1, source_target_pairs={{0,16},{1,2},{2,1},{3,4},{4,3},{5,6},{6,5},{7,8},{8,7},{9,10},{10,... | collective-permute-start | bytes 98312 | tf_op jit(solution)/shard_map/ppermute | solution.py:272

commit v3 on v2

v3 whole, which is shorter than its diff:
```python
import math

import jax
import jax.numpy as jnp
from jax import lax
from jax.experimental import pallas as pl
from jax.experimental.pallas import tpu as pltpu
from jax.sharding import PartitionSpec as P


TILE = 512
CG = 128
BLK = 128
CELL = 4
BETA = 16
REACH = 32
SLOTS = 1024
NTR = 8
NTC = 16
FORWARD_RANGE = 4.0
BACK_RATIO = 0.75
TARGET_LEVEL = 1.0
F32 = jnp.float32
BF16 = jnp.bfloat16
AXES = ("row", "col")
NT = (((1,), (1,)), ((), ()))
MAXB = 8
SIDE = CG + REACH
ALL = CG + 2 * REACH


def pairings():
    def number(r, c):
        return r * NTC + c

    def table(partner):
        return [(number(r, c), number(*partner(r, c))) for r in range(NTR) for c in range(NTC)]

    def odd(i):
        return ((i - 1) ^ 1) + 1

    row_even = table(lambda r, c: (r ^ 1, c))
    row_odd = table(lambda r, c: (r, c ^ 1) if r in (0, NTR - 1) else (odd(r), c))
    col_even = table(lambda r, c: (r, c ^ 1))
    col_odd = table(lambda r, c: (r ^ 1, c) if c in (0, NTC - 1) else (r, odd(c)))
    return row_even, row_odd, col_even, col_odd


def two_parts(value):
    high = value.astype(BF16)
    low = (value - high.astype(F32)).astype(BF16)
    return high, low


def stacked_dot(value, other, dims):
    rows = value.shape[0]
    parts = jnp.concatenate(two_parts(value), axis=0)
    both = lax.dot_general(parts, other, dims, preferred_element_type=F32)
    return both[:rows] + both[rows:]


def weighted(columns, high, low):
    first, second = two_parts(columns)
    return jnp.dot(
        jnp.concatenate([first, first, second], axis=1), jnp.concatenate([high, low, high], axis=0), preferred_element_type=F32
    )


def overlap(low_edge, high_edge, cells):
    begin = cells * CELL
    covered = jnp.minimum(high_edge, begin + CELL) - jnp.maximum(low_edge, begin)
    return jnp.maximum(covered, 0).astype(F32) * (1.0 / CELL)


def spread(distance):
    scaled = distance.astype(F32) / BETA
    inside = jnp.abs(distance) <= REACH
    return jnp.where(inside, jnp.exp(-scaled * scaled) / (math.sqrt(math.pi) * BETA), 0.0)


def iota(shape, axis):
    return lax.broadcasted_iota(jnp.int32, shape, axis)


def is_even(axis):
    return lax.rem(lax.axis_index(axis), 2) == 0


def sides(from_even, from_odd):
    col = lax.axis_index("col")
    even = lax.rem(col, 2) == 0
    left = jnp.where(even, from_odd, from_even)
    right = jnp.where(even, from_even, from_odd)
    return jnp.where(col == 0, 0.0, left), jnp.where(col == NTC - 1, 0.0, right)


def outer_rows(from_even, from_odd):
    row = lax.axis_index("row")
    even = lax.rem(row, 2) == 0
    above = jnp.where(even, from_odd, from_even)
    below = jnp.where(even, from_even, from_odd)
    return jnp.concatenate([jnp.where(row == 0, 0.0, above), jnp.where(row == NTR - 1, 0.0, below)], axis=0)


def send_rows(edges, send_even, send_odd):
    even = is_even("row")
    top, bottom = edges[:REACH], edges[REACH:]
    send_even[...] = jnp.where(even, bottom, top)
    send_odd[...] = jnp.where(even, top, bottom)


def boxes_of(tile):
    return [tile[k].astype(jnp.int32) for k in range(4)]


def edge_part(py):
    return jnp.concatenate([py[:REACH, :], py[CG - REACH :, :]], axis=0).astype(F32)


def start_kernel(boxes_in, counts_in, tails_in, doses_in, tile, boxes, counts, tails, doses, arrived):
    copies = [
        pltpu.make_async_copy(source, target, arrived.at[k])
        for k, (source, target) in enumerate(((boxes_in, boxes), (counts_in, counts), (tails_in, tails), (doses_in, doses)))
    ]
    for copy in copies:
        copy.start()
    for copy in copies:
        copy.wait()
    col = lax.axis_index("col")
    totals = (counts[...] - 1) * BLK + tails[...]
    total = jnp.sum(jnp.where(iota((1, NTC), 1) == col, totals, 0), axis=1, keepdims=True)
    live = iota((1, SLOTS), 1) < total
    for k in range(4):
        tile[k] = boxes[k].astype(F32)
    tile[4] = jnp.where(live, doses[...], 0.0)


def as_columns(dose):
    return jnp.transpose(jnp.concatenate([dose[:, k * BLK : (k + 1) * BLK] for k in range(MAXB)], axis=0))


def folded_sum(value):
    return jnp.sum(value.reshape(BLK // 8, 8, SLOTS), axis=0)


def early_kernel(tile, gain_in, px_out, py_out, pairs, told, gain, arrived):
    copy = pltpu.make_async_copy(gain_in, gain, arrived)
    copy.start()
    inverse = 1.0 / FORWARD_RANGE
    box = [tile[k] for k in range(4)]
    centre_x = (box[0] + box[2]) * (0.5 * inverse)
    centre_y = (box[1] + box[3]) * (0.5 * inverse)
    columns = jnp.concatenate([b * inverse for b in box] + [tile[4], jnp.zeros((3, SLOTS), F32)], axis=0)
    total = jnp.zeros((8, SLOTS), F32)
    for at in range(0, SLOTS, BLK):
        side = jnp.transpose(columns[:, at : at + BLK])
        along_x = lax.erf(centre_x - side[:, 0:1]) - lax.erf(centre_x - side[:, 2:3])
        along_y = lax.erf(centre_y - side[:, 1:2]) - lax.erf(centre_y - side[:, 3:4])
        block = (0.25 * along_x) * along_y
        pairs[at : at + BLK, :] = block
        total += folded_sum(side[:, 4:5] * block)
    told[0] = jnp.sum(total, axis=0, keepdims=True)
    boxes = boxes_of(tile)
    px_out[...] = overlap(boxes[0], boxes[2], iota((CG, SLOTS), 0)).astype(BF16)
    py_out[...] = overlap(boxes[1], boxes[3], iota((CG, SLOTS), 0)).astype(BF16)
    pixel_x = (boxes[0] + boxes[2]) // 2
    pixel_y = (boxes[1] + boxes[3]) // 2
    pixels = iota((TILE, SLOTS), 0)
    chosen_x = jnp.where(pixels == pixel_x, 1.0, 0.0).astype(BF16)
    copy.wait()
    picked = stacked_dot(gain[...], chosen_x, (((1,), (0,)), ((), ())))
    told[1] = jnp.sum(jnp.where(pixels == pixel_y, picked, 0.0), axis=0, keepdims=True)


def first_strips_kernel(own, got_even, got_odd, px, py, left_out, right_out, px_left, px_right, send_even, send_odd):
    left, right = sides(got_even[...], got_odd[...])
    left_out[...] = left
    right_out[...] = right
    edge_cells = iota((2 * REACH, SLOTS), 0)
    edge_cells = jnp.where(edge_cells < REACH, edge_cells, edge_cells + (CG - 2 * REACH))
    edges = [stacked_dot(edge_part(py) * own[4], px[...], NT)]
    for tile, px_out in ((left, px_left), (right, px_right)):
        boxes = boxes_of(tile)
        across = overlap(boxes[0], boxes[2], iota((CG, SLOTS), 0)).astype(BF16)
        px_out[...] = across
        edges.append(stacked_dot(overlap(boxes[1], boxes[3], edge_cells) * tile[4], across, NT))
    send_rows(jnp.concatenate([edges[1], edges[0], edges[2]], axis=1), send_even, send_odd)


def strips_kernel(doses, px_left, px, px_right, py_left, py, py_right, send_even, send_odd):
    pieces = ((0, px_left, py_left), (1, px, py), (2, px_right, py_right))
    edges = [stacked_dot(edge_part(down) * doses[k], across[...], NT) for k, across, down in pieces]
    send_rows(jnp.concatenate(edges, axis=1), send_even, send_odd)


def last_strips_kernel(doses, px_left, px, px_right, py_left, py, py_right, send_even, send_odd):
    edges = [
        stacked_dot(edge_part(py) * doses[1], px[...], NT),
        stacked_dot(edge_part(py_left) * doses[0], px_left[CG - REACH :, :], NT),
        stacked_dot(edge_part(py_right) * doses[2], px_right[:REACH, :], NT),
        jnp.zeros((2 * REACH, 2 * CG - ALL), F32),
    ]
    send_rows(jnp.concatenate(edges, axis=1), send_even, send_odd)


def per_tile(left, own, right):
    return (
        jnp.concatenate([left, own[:REACH]], axis=0),
        jnp.concatenate([own, left[CG - REACH :], right[:REACH]], axis=0),
        jnp.concatenate([right, own[CG - REACH :]], axis=0),
    )


def inner_sums(doses, px, py, wy_high, wy_low, wx, inner):
    coarse = [stacked_dot(across.astype(F32) * dose, down, NT) for dose, across, down in zip(doses, px, py)]
    for k, columns in enumerate(per_tile(*coarse)):
        across = weighted(columns, wy_high[k, :CG, :], wy_low[k, :CG, :])
        inner[k] = jnp.sum(across * wx[k][...], axis=0, keepdims=True)


def late_kernel(own, left, right, px_left, px, px_right, py, py_left, py_right, wy_high, wy_low, wx_left, wx, wx_right, inner):
    tiles = (left, own, right)
    boxes = [boxes_of(tile) for tile in tiles]
    y = iota((ALL, SLOTS), 0)
    y = jnp.where(y < CG, y, jnp.where(y < CG + REACH, y - (CG + REACH), y - REACH))
    x = iota((SIDE, SLOTS), 0)
    places = (x, y, jnp.where(x < CG, x, x - (CG + REACH)))
    for k, (box, place, out) in enumerate(zip(boxes, places, (wx_left, wx, wx_right))):
        out[...] = spread((box[0] + box[2]) // (2 * CELL) - place)
        wy_high[k], wy_low[k] = two_parts(spread((box[1] + box[3]) // (2 * CELL) - y))
    for box, out in ((boxes[0], py_left), (boxes[2], py_right)):
        out[...] = overlap(box[1], box[3], iota((CG, SLOTS), 0)).astype(BF16)
    inner_sums(
        [tile[4] for tile in tiles],
        (px_left[...], px[...], px_right[...]),
        (py_left[...], py[...], py_right[...]),
        wy_high,
        wy_low,
        (wx_left, wx, wx_right),
        inner,
    )


def inner_kernel(doses, px_left, px, px_right, py_left, py, py_right, wy_high, wy_low, wx_left, wx, wx_right, inner):
    inner_sums(
        [doses[k] for k in range(3)],
        (px_left[...], px[...], px_right[...]),
        (py_left[...], py[...], py_right[...]),
        wy_high,
        wy_low,
        (wx_left, wx, wx_right),
        inner,
    )


def last_inner_kernel(doses, px_left, px, px_right, py_left, py, py_right, wy_high, wy_low, wx, pairs, inner, forward):
    coarse = jnp.concatenate(
        [
            stacked_dot(px[...].astype(F32) * doses[1], py[...], NT),
            stacked_dot(px_left[CG - REACH :, :].astype(F32) * doses[0], py_left[...], NT),
            stacked_dot(px_right[:REACH, :].astype(F32) * doses[2], py_right[...], NT),
        ],
        axis=0,
    )
    across = weighted(coarse, wy_high[1, :CG, :], wy_low[1, :CG, :])
    inner[...] = jnp.sum(across * wx[...], axis=0, keepdims=True)
    forward[...] = pair_sum(doses[1], pairs)


def pair_sum(dose, pairs):
    columns = as_columns(dose)
    total = jnp.zeros((8, SLOTS), F32)
    for k in range(MAXB):
        total += folded_sum(columns[:, k : k + 1] * pairs[k * BLK : (k + 1) * BLK, :])
    return jnp.sum(total, axis=0, keepdims=True)


def forward_kernel(doses, pairs, told):
    told[0] = pair_sum(doses[1], pairs)


def exposed(dose, sens, forward, background):
    live = dose > 0.0
    exposure = sens * (forward + BACK_RATIO * background) / (1.0 + BACK_RATIO)
    return jnp.where(live, dose * TARGET_LEVEL / jnp.where(live, exposure, 1.0), 0.0), jnp.where(live, exposure, 0.0)


def update(got_even, got_odd, doses, sens, forward, inner, wy_high, wy_low, wx, doses_out):
    outer = outer_rows(got_even[...], got_odd[...])
    outer_t = [jnp.transpose(outer[:, k * CG : (k + 1) * CG]) for k in range(3)]
    for k, columns in enumerate(per_tile(*outer_t)):
        across = weighted(columns, wy_high[k, CG:, :], wy_low[k, CG:, :])
        background = inner[k] + jnp.sum(across * wx[k][...], axis=0, keepdims=True)
        doses_out[k], _ = exposed(doses[k], sens[k], forward[k], background)


def first_update_kernel(
    got_even, got_odd, told, told_even, told_odd, own, left, right, inner, wy_high, wy_low, wx_left, wx, wx_right, doses_out, sens_out
):
    told_left, told_right = sides(told_even[...], told_odd[...])
    forward, sens = zip((told_left[0], told_left[1]), (told[0], told[1]), (told_right[0], told_right[1]))
    for k in range(3):
        sens_out[k] = sens[k]
    update(got_even, got_odd, (left[4], own[4], right[4]), sens, forward, inner, wy_high, wy_low, (wx_left, wx, wx_right), doses_out)


def update_kernel(got_even, got_odd, told, told_even, told_odd, doses, sens, inner, wy_high, wy_low, wx_left, wx, wx_right, doses_out):
    told_left, told_right = sides(told_even[...], told_odd[...])
    update(
        got_even,
        got_odd,
        [doses[k] for k in range(3)],
        [sens[k] for k in range(3)],
        (told_left[0], told[0], told_right[0]),
        inner,
        wy_high,
        wy_low,
        (wx_left, wx, wx_right),
        doses_out,
    )


def final_kernel(got_even, got_odd, doses, sens, inner, forward, wy_high, wy_low, wx, dose_out, exposure_out):
    outer = outer_rows(got_even[...], got_odd[...])
    columns = jnp.concatenate([jnp.transpose(outer[:, :CG]), jnp.transpose(outer[:, CG:])[: 2 * REACH]], axis=0)
    across = weighted(columns, wy_high[1, CG:, :], wy_low[1, CG:, :])
    background = inner[...] + jnp.sum(across * wx[...], axis=0, keepdims=True)
    dose_out[...], exposure_out[...] = exposed(doses[1], sens[1], forward[...], background)


def shape(*dims, dtype=F32):
    return jax.ShapeDtypeStruct(dims, dtype)


HBM = pl.BlockSpec(memory_space=pltpu.HBM)
VMEM = pl.BlockSpec(memory_space=pltpu.VMEM)


def call(kernel, outs, vmem=24, ins=None, scratch=()):
    extra = {} if ins is None else {"in_specs": ins}
    return pl.pallas_call(
        kernel,
        out_shape=outs,
        scratch_shapes=scratch,
        compiler_params=pltpu.CompilerParams(vmem_limit_bytes=vmem << 20),
        **extra,
    )


def in_hbm(*arrays):
    return [pltpu.with_memory_space_constraint(array, pltpu.HBM) for array in arrays]


def send(value, table):
    return lax.ppermute(value, AXES, table)


def body(shot_boxes, block_counts, tail_shots, doses, pixel_gain):
    row_even, row_odd, col_even, col_odd = pairings()
    row = shape(1, SLOTS)
    rows = shape(3, 1, SLOTS)
    cover = shape(CG, SLOTS, dtype=BF16)
    tile = shape(5, 1, SLOTS)
    weights = shape(3, ALL, SLOTS, dtype=BF16)
    strip = shape(REACH, 3 * CG)
    short = shape(REACH, 2 * CG)
    own = call(
        start_kernel,
        tile,
        ins=[HBM] * 4,
        scratch=(
            pltpu.VMEM((4, 1, SLOTS), jnp.int32),
            pltpu.VMEM((1, NTC), jnp.int32),
            pltpu.VMEM((1, NTC), jnp.int32),
            pltpu.VMEM((1, SLOTS), F32),
            pltpu.SemaphoreType.DMA((4,)),
        ),
    )(*in_hbm(shot_boxes, block_counts, tail_shots, doses))
    far_odd = send(own, col_odd)
    far_even = send(own, col_even)
    px, py, pairs, told = call(
        early_kernel,
        (cover, cover, shape(SLOTS, SLOTS), shape(2, 1, SLOTS)),
        ins=[VMEM, HBM],
        scratch=(pltpu.VMEM((TILE, TILE), F32), pltpu.SemaphoreType.DMA),
    )(own, *in_hbm(pixel_gain))
    told_odd = send(told, col_odd)
    left, right, px_left, px_right, strip_even, strip_odd = call(
        first_strips_kernel, (tile, tile, cover, cover, strip, strip)
    )(own, far_even, far_odd, px, py)
    got_odd = send(strip_odd, row_odd)
    got_even = send(strip_even, row_even)
    told_even = send(told, col_even)
    py_left, py_right, wy_high, wy_low, wx_left, wx, wx_right, inner = call(
        late_kernel, (cover, cover, weights, weights, shape(SIDE, SLOTS), shape(ALL, SLOTS), shape(SIDE, SLOTS), rows)
    )(own, left, right, px_left, px, px_right, py)
    covers = (px_left, px, px_right, py_left, py, py_right)
    weighing = (wy_high, wy_low, wx_left, wx, wx_right)
    doses3, sens = call(first_update_kernel, (rows, rows))(
        got_even, got_odd, told, told_even, told_odd, own, left, right, inner, *weighing
    )
    told = call(forward_kernel, shape(1, 1, SLOTS))(doses3, pairs)
    told_odd = send(told, col_odd)
    strip_even, strip_odd = call(strips_kernel, (strip, strip))(doses3, *covers)
    got_odd = send(strip_odd, row_odd)
    got_even = send(strip_even, row_even)
    told_even = send(told, col_even)
    inner = call(inner_kernel, rows)(doses3, *covers, *weighing)
    doses3 = call(update_kernel, rows)(got_even, got_odd, told, told_even, told_odd, doses3, sens, inner, *weighing)
    strip_even, strip_odd = call(last_strips_kernel, (short, short))(doses3, *covers)
    got_odd = send(strip_odd, row_odd)
    got_even = send(strip_even, row_even)
    inner, forward = call(last_inner_kernel, (row, row))(doses3, *covers, wy_high, wy_low, wx, pairs)
    return call(final_kernel, (row, row))(got_even, got_odd, doses3, sens, inner, forward, wy_high, wy_low, wx)


def solution(mesh):
    placed = (P(None, "row", "col"), P("row", None), P("row", None), P("row", "col"), P("row", "col"))
    return jax.shard_map(body, mesh=mesh, in_specs=placed, out_specs=(P("row", "col"), P("row", "col")), check_vma=False)
```

time: 36.6 us -> 34 us (0.929)
  the two profiles are of different devices: /device:TPU:64 before, /device:TPU:97 now
where the time goes in v3:
time: 34 us; the launch traced here: 33.8 us
  Pallas kernels  15.9 us (47%)
  starting transfers between devices  13.2 us (39%)
  waiting for transfers between devices  3.98 us (12%)
  between operations  0.73 us (2%)
    ppermute x12, starting transfers between devices, send(): return lax.ppermute(value, AXES, table)  13.2 us
    pallas_call x1, Pallas kernels, body(): call(early_kernel, (cover, cover, shape(SLOTS, SLOTS), shape(2, 1, SLOTS)...  4.93 us
    ppermute x12, waiting for transfers between devices, send(): return lax.ppermute(value, AXES, table)  3.98 us
    pallas_call x1, Pallas kernels, body(): call(late_kernel, (cover, cover, weights, weights, shape(SIDE, SLOTS), sh...  3.14 us
    pallas_call x1, Pallas kernels, body(): inner = call(inner_kernel, rows)(doses3, *covers, *weighing)  1.31 us
    pallas_call x1, Pallas kernels, body(): call(final_kernel, (row, row))  1.08 us
    pallas_call x1, Pallas kernels, body(): call(last_inner_kernel, (row, row))  0.95 us
    pallas_call x1, Pallas kernels, body(): call(first_strips_kernel, (tile, tile, cover, cover, strip, strip))  0.88 us
  transfers between devices with their start and end apart: 12, of which 3 were waited for; matrix products, arithmetic and copies ran while one was open for 0% of the time, Pallas kernels for 32%

profile of v3, /device:TPU:97, one launch (start us, length us, event | category | flops | bytes accessed | tf_op | source)
XLA Modules:
  0.0 33.8 jit_solution(13728438912893159144)
XLA Ops:
  0.6 0.9 %shard_map.68.tile.own = f32[5,1,1024]{2,1,0:T(1,128)S(1)} custom-call(s32[4,1,1024]{2,1,0:T(1,128)} %boxes_in.1, s32[1,16]{1,0:T(1,128)} %counts_in.1, s32[1,16]{1,0:T(1,128)} %tails_in.1, f32[1,1024]{1,0:T(1,128)} %doses_in.1), custom_call_target="tpu_custom_call" | custom-call | tf_op jit(solution)/shard_map/pallas_call | solution.py:367
  1.5 2.4 %collective-permute-start.1 = (f32[5,1,1024]{2,1,0:T(1,128)S(1)}, f32[5,1,1024]{2,1,0:T(1,128)S(1)}, u32[]{:S(2)}, u32[]{:S(2)}) collective-permute-start(f32[5,1,1024]{2,1,0:T(1,128)S(1)} %shard_map.68.tile.own), channel_id=1, source_target_pairs={{0,16},{1,2},{2,1},{3,4},{4,3},{5,6},{6,5},{7,8},{8,7},{9,10},{10,... | collective-permute-start | bytes 61448 | tf_op jit(solution)/shard_map/ppermute | solution.py:355
  3.9 0.1 collective-permute-start
  4.0 4.9 %shard_map.69 = (bf16[128,1024]{1,0:T(8,128)(2,1)S(1)}, bf16[128,1024]{1,0:T(8,128)(2,1)S(1)}, f32[1024,1024]{1,0:T(8,128)S(1)}, f32[2,1,1024]{2,1,0:T(1,128)S(1)}) custom-call(f32[5,1,1024]{2,1,0:T(1,128)S(1)} %shard_map.68.tile.own, f32[512,512]{1,0:T(8,128)} %gain_in.1), custom_call_target="tpu_custom_call" | custom-call | tf_op jit(solution)/shard_map/pallas_call | solution.py:381
  8.9 0.0 collective-permute-done.1.got_odd
  9.0 0.0 collective-permute-done.got_even
  9.0 0.9 %shard_map.70 = (f32[5,1,1024]{2,1,0:T(1,128)S(1)}, f32[5,1,1024]{2,1,0:T(1,128)S(1)}, bf16[128,1024]{1,0:T(8,128)(2,1)S(1)}, bf16[128,1024]{1,0:T(8,128)(2,1)S(...) custom-call(f32[5,1,1024]{2,1,0:T(1,128)S(1)} %shard_map.68.tile.own, f32[5,1,1024]{2,1,0:T(1,128)S(1)} %collective-permute-done.got_even, ...), custom_call_target="tpu_custom_call" | custom-call | tf_op jit(solution)/shard_map/pallas_call | solution.py:388
  9.9 1.3 %collective-permute-start.2 = (f32[32,384]{1,0:T(8,128)S(1)}, f32[32,384]{1,0:T(8,128)S(1)}, u32[]{:S(2)}, u32[]{:S(2)}) collective-permute-start(f32[32,384]{1,0:T(8,128)S(1)} %get-tuple-element.30), channel_id=1, source_target_pairs={{0,16},{1,17},{2,18},{3,19},{4,20},{5,21},{6,22},{7,23},{8,24},{9,... | collective-permute-start | bytes 147464 | tf_op jit(solution)/shard_map/ppermute | solution.py:355
  11.2 1.3 %collective-permute-start.3 = (f32[32,384]{1,0:T(8,128)S(1)}, f32[32,384]{1,0:T(8,128)S(1)}, u32[]{:S(2)}, u32[]{:S(2)}) collective-permute-start(f32[32,384]{1,0:T(8,128)S(1)} %get-tuple-element.31), channel_id=1, source_target_pairs={{0,1},{1,0},{2,3},{3,2},{4,5},{5,4},{6,7},{7,6},{8,9},{9,8},{10,11... | collective-permute-start | bytes 147464 | tf_op jit(solution)/shard_map/ppermute | solution.py:355
  12.4 0.9 %collective-permute-start.5 = (f32[2,1,1024]{2,1,0:T(1,128)S(1)}, f32[2,1,1024]{2,1,0:T(1,128)S(1)}, u32[]{:S(2)}, u32[]{:S(2)}) collective-permute-start(f32[2,1,1024]{2,1,0:T(1,128)S(1)} %get-tuple-element.32.told), channel_id=1, source_target_pairs={{0,16},{1,2},{2,1},{3,4},{4,3},{5,6},{6,5},{7,8},{8,7},{9,10},{10,... | collective-permute-start | bytes 24584 | tf_op jit(solution)/shard_map/ppermute | solution.py:355
  13.3 0.5 %collective-permute-start.4 = (f32[2,1,1024]{2,1,0:T(1,128)S(1)}, f32[2,1,1024]{2,1,0:T(1,128)S(1)}, u32[]{:S(2)}, u32[]{:S(2)}) collective-permute-start(f32[2,1,1024]{2,1,0:T(1,128)S(1)} %get-tuple-element.32.told), channel_id=1, source_target_pairs={{0,1},{1,0},{2,3},{3,2},{4,5},{5,4},{6,7},{7,6},{8,9},{9,8},{10,11... | collective-permute-start | bytes 24584 | tf_op jit(solution)/shard_map/ppermute | solution.py:355
  13.8 3.1 %shard_map.71 = (bf16[128,1024]{1,0:T(8,128)(2,1)S(1)}, bf16[128,1024]{1,0:T(8,128)(2,1)S(1)}, bf16[3,192,1024]{2,1,0:T(8,128)(2,1)S(1)}, bf16[3,192,1024]{2,1,0...) custom-call(f32[5,1,1024]{2,1,0:T(1,128)S(1)} %shard_map.68.tile.own, ...), custom_call_target="tpu_custom_call" | custom-call | tf_op jit(solution)/shard_map/pallas_call | solution.py:394
  17.0 0.1 collective-permute-done.5.told_odd
  17.1 0.0 collective-permute-done.4.told_even
  17.1 0.0 collective-permute-done.2.got_even
  17.1 0.0 collective-permute-done.3.got_odd
  17.1 0.7 %shard_map.72 = (f32[3,1,1024]{2,1,0:T(1,128)S(1)}, f32[3,1,1024]{2,1,0:T(1,128)S(1)}) custom-call(f32[32,384]{1,0:T(8,128)S(1)} %collective-permute-done.2.got_even, f32[32,384]{1,0:T(8,128)S(1)} %collective-permute-done.3.got_odd, f32[2,1,1024]{2,1,0:T(1,128)S(1)} %get-tuple-element.32.told, f32[2,1,1024]{2,1,0:T(1,128)S(1)} %collective-permute-done.4.told_even, ...), custom_call_target="tpu_custom_call" | custom-call | tf_op jit(solution)/shard_map/pallas_call | solution.py:399
  17.8 0.4 %shard_map.73 = (f32[32,384]{1,0:T(8,128)S(1)}, f32[32,384]{1,0:T(8,128)S(1)}) custom-call(f32[3,1,1024]{2,1,0:T(1,128)S(1)} %get-tuple-element.43.doses, bf16[128,1024]{1,0:T(8,128)(2,1)S(1)} %get-tuple-element.35.px_left, bf16[128,1024]{1,0:T(8,128)(2,1)S(1)} %get-tuple-element.28.px, bf16[128,1024]{1,0:T(8,128)(2,1)S(1)} %get-tuple-element.36.px_right, ...), custom_call_target="tpu_custom_call" | custom-call | tf_op jit(solution)/shard_map/pallas_call | solution.py:404
  18.2 1.7 %collective-permute-start.6 = (f32[32,384]{1,0:T(8,128)S(1)}, f32[32,384]{1,0:T(8,128)S(1)}, u32[]{:S(2)}, u32[]{:S(2)}) collective-permute-start(f32[32,384]{1,0:T(8,128)S(1)} %get-tuple-element.46), channel_id=1, source_target_pairs={{0,16},{1,17},{2,18},{3,19},{4,20},{5,21},{6,22},{7,23},{8,24},{9,... | collective-permute-start | bytes 147464 | tf_op jit(solution)/shard_map/ppermute | solution.py:355
  19.9 0.3 collective-permute-start.7
  20.2 0.5 %shard_map.74.told = f32[1,1,1024]{2,1,0:T(1,128)S(1)} custom-call(f32[3,1,1024]{2,1,0:T(1,128)S(1)} %get-tuple-element.43.doses, f32[1024,1024]{1,0:T(8,128)S(1)} %get-tuple-element.48.pairs), custom_call_target="tpu_custom_call" | custom-call | tf_op jit(solution)/shard_map/pallas_call | solution.py:402
  20.6 2.0 %collective-permute-start.9 = (f32[1,1,1024]{2,1,0:T(1,128)S(1)}, f32[1,1,1024]{2,1,0:T(1,128)S(1)}, u32[]{:S(2)}, u32[]{:S(2)}) collective-permute-start(f32[1,1,1024]{2,1,0:T(1,128)S(1)} %shard_map.74.told), channel_id=1, source_target_pairs={{0,16},{1,2},{2,1},{3,4},{4,3},{5,6},{6,5},{7,8},{8,7},{9,10},{10,... | collective-permute-start | bytes 12296 | tf_op jit(solution)/shard_map/ppermute | solution.py:355
  22.7 0.0 collective-permute-start.8
  22.7 1.3 %shard_map.75.inner = f32[3,1,1024]{2,1,0:T(1,128)S(1)} custom-call(f32[3,1,1024]{2,1,0:T(1,128)S(1)} %get-tuple-element.43.doses, bf16[128,1024]{1,0:T(8,128)(2,1)S(1)} %get-tuple-element.35.px_left, bf16[128,1024]{1,0:T(8,128)(2,1)S(1)} %get-tuple-element.28.px, bf16[128,1024]{1,0:T(8,128)(2,1)S(1)} %get-tuple-element.36.px_right, ...), custom_call_target="tpu_custom_call" | custom-call | tf_op jit(solution)/shard_map/pallas_call | solution.py:408
  24.0 1.3 %collective-permute-done.9.told_odd = f32[1,1,1024]{2,1,0:T(1,128)S(1)} collective-permute-done((f32[1,1,1024]{2,1,0:T(1,128)S(1)}, f32[1,1,1024]{2,1,0:T(1,128)S(1)}, u32[]{:S(2)}, u32[]{:S(2)}) %collective-permute-start.9) | collective-permute-done | bytes 4128 | tf_op jit(solution)/shard_map/ppermute | solution.py:355
  25.3 0.0 collective-permute-done.8.told_even
  25.3 0.0 collective-permute-done.6.got_even
  25.3 0.0 collective-permute-done.7.got_odd
  25.3 0.7 %shard_map.76.doses = f32[3,1,1024]{2,1,0:T(1,128)S(1)} custom-call(f32[32,384]{1,0:T(8,128)S(1)} %collective-permute-done.6.got_even, f32[32,384]{1,0:T(8,128)S(1)} %collective-permute-done.7.got_odd, f32[1,1,1024]{2,1,0:T(1,128)S(1)} %shard_map.74.told, f32[1,1,1024]{2,1,0:T(1,128)S(1)} %collective-permute-done.8.told_even, ...), custom_call_target="tpu_custom_call" | custom-call | tf_op jit(solution)/shard_map/pallas_call | solution.py:409
  26.0 0.4 %shard_map.77 = (f32[32,256]{1,0:T(8,128)S(1)}, f32[32,256]{1,0:T(8,128)S(1)}) custom-call(f32[3,1,1024]{2,1,0:T(1,128)S(1)} %shard_map.76.doses, bf16[128,1024]{1,0:T(8,128)(2,1)S(1)} %get-tuple-element.35.px_left, bf16[128,1024]{1,0:T(8,128)(2,1)S(1)} %get-tuple-element.28.px, bf16[128,1024]{1,0:T(8,128)(2,1)S(1)} %get-tuple-element.36.px_right, ...), custom_call_target="tpu_custom_call" | custom-call | tf_op jit(solution)/shard_map/pallas_call | solution.py:410
  26.4 2.7 %collective-permute-start.10 = (f32[32,256]{1,0:T(8,128)S(1)}, f32[32,256]{1,0:T(8,128)S(1)}, u32[]{:S(2)}, u32[]{:S(2)}) collective-permute-start(f32[32,256]{1,0:T(8,128)S(1)} %get-tuple-element.50), channel_id=1, source_target_pairs={{0,16},{1,17},{2,18},{3,19},{4,20},{5,21},{6,22},{7,23},{8,24},{9,... | collective-permute-start | bytes 98312 | tf_op jit(solution)/shard_map/ppermute | solution.py:355
  29.1 0.1 collective-permute-start.11
  29.2 1.0 %shard_map.78 = (f32[1,1024]{1,0:T(1,128)S(1)}, f32[1,1024]{1,0:T(1,128)S(1)}) custom-call(f32[3,1,1024]{2,1,0:T(1,128)S(1)} %shard_map.76.doses, bf16[128,1024]{1,0:T(8,128)(2,1)S(1)} %get-tuple-element.35.px_left, bf16[128,1024]{1,0:T(8,128)(2,1)S(1)} %get-tuple-element.28.px, bf16[128,1024]{1,0:T(8,128)(2,1)S(1)} %get-tuple-element.36.px_right, ...), custom_call_target="tpu_custom_call" | custom-call | tf_op jit(solution)/shard_map/pallas_call | solution.py:413
  30.2 0.0 collective-permute-done.10.got_even
  30.2 2.5 %collective-permute-done.11.got_odd = f32[32,256]{1,0:T(8,128)S(1)} collective-permute-done((f32[32,256]{1,0:T(8,128)S(1)}, f32[32,256]{1,0:T(8,128)S(1)}, u32[]{:S(2)}, u32[]{:S(2)}) %collective-permute-start.11) | collective-permute-done | bytes 32800 | tf_op jit(solution)/shard_map/ppermute | solution.py:355
  32.7 1.1 %shard_map.79 = (f32[1,1024]{1,0:T(1,128)}, f32[1,1024]{1,0:T(1,128)}) custom-call(f32[32,256]{1,0:T(8,128)S(1)} %collective-permute-done.10.got_even, f32[32,256]{1,0:T(8,128)S(1)} %collective-permute-done.11.got_odd, f32[3,1,1024]{2,1,0:T(1,128)S(1)} %shard_map.76.doses, f32[3,1,1024]{2,1,0:T(1,128)S(1)} %get-tuple-element.49.sens, ...), custom_call_target="tpu_custom_call" | custom-call | tf_op jit(solution)/shard_map/pallas_call | solution.py:414
Async XLA Ops:
  1.5 7.4 %collective-permute-start.1 = (f32[5,1,1024]{2,1,0:T(1,128)S(1)}, f32[5,1,1024]{2,1,0:T(1,128)S(1)}, u32[]{:S(2)}, u32[]{:S(2)}) collective-permute-start(f32[5,1,1024]{2,1,0:T(1,128)S(1)} %shard_map.68.tile.own), channel_id=1, source_target_pairs={{0,16},{1,2},{2,1},{3,4},{4,3},{5,6},{6,5},{7,8},{8,7},{9,10},{10,... | collective-permute-start | bytes 61448 | tf_op jit(solution)/shard_map/ppermute | solution.py:355
  3.9 5.1 %collective-permute-start = (f32[5,1,1024]{2,1,0:T(1,128)S(1)}, f32[5,1,1024]{2,1,0:T(1,128)S(1)}, u32[]{:S(2)}, u32[]{:S(2)}) collective-permute-start(f32[5,1,1024]{2,1,0:T(1,128)S(1)} %shard_map.68.tile.own), channel_id=1, source_target_pairs={{0,1},{1,0},{2,3},{3,2},{4,5},{5,4},{6,7},{7,6},{8,9},{9,8},{10,11... | collective-permute-start | bytes 61448 | tf_op jit(solution)/shard_map/ppermute | solution.py:355
  9.9 7.2 %collective-permute-start.2 = (f32[32,384]{1,0:T(8,128)S(1)}, f32[32,384]{1,0:T(8,128)S(1)}, u32[]{:S(2)}, u32[]{:S(2)}) collective-permute-start(f32[32,384]{1,0:T(8,128)S(1)} %get-tuple-element.30), channel_id=1, source_target_pairs={{0,16},{1,17},{2,18},{3,19},{4,20},{5,21},{6,22},{7,23},{8,24},{9,... | collective-permute-start | bytes 147464 | tf_op jit(solution)/shard_map/ppermute | solution.py:355
  11.2 5.9 %collective-permute-start.3 = (f32[32,384]{1,0:T(8,128)S(1)}, f32[32,384]{1,0:T(8,128)S(1)}, u32[]{:S(2)}, u32[]{:S(2)}) collective-permute-start(f32[32,384]{1,0:T(8,128)S(1)} %get-tuple-element.31), channel_id=1, source_target_pairs={{0,1},{1,0},{2,3},{3,2},{4,5},{5,4},{6,7},{7,6},{8,9},{9,8},{10,11... | collective-permute-start | bytes 147464 | tf_op jit(solution)/shard_map/ppermute | solution.py:355
  12.4 4.6 %collective-permute-start.5 = (f32[2,1,1024]{2,1,0:T(1,128)S(1)}, f32[2,1,1024]{2,1,0:T(1,128)S(1)}, u32[]{:S(2)}, u32[]{:S(2)}) collective-permute-start(f32[2,1,1024]{2,1,0:T(1,128)S(1)} %get-tuple-element.32.told), channel_id=1, source_target_pairs={{0,16},{1,2},{2,1},{3,4},{4,3},{5,6},{6,5},{7,8},{8,7},{9,10},{10,... | collective-permute-start | bytes 24584 | tf_op jit(solution)/shard_map/ppermute | solution.py:355
  13.3 3.7 %collective-permute-start.4 = (f32[2,1,1024]{2,1,0:T(1,128)S(1)}, f32[2,1,1024]{2,1,0:T(1,128)S(1)}, u32[]{:S(2)}, u32[]{:S(2)}) collective-permute-start(f32[2,1,1024]{2,1,0:T(1,128)S(1)} %get-tuple-element.32.told), channel_id=1, source_target_pairs={{0,1},{1,0},{2,3},{3,2},{4,5},{5,4},{6,7},{7,6},{8,9},{9,8},{10,11... | collective-permute-start | bytes 24584 | tf_op jit(solution)/shard_map/ppermute | solution.py:355
  18.2 7.1 %collective-permute-start.6 = (f32[32,384]{1,0:T(8,128)S(1)}, f32[32,384]{1,0:T(8,128)S(1)}, u32[]{:S(2)}, u32[]{:S(2)}) collective-permute-start(f32[32,384]{1,0:T(8,128)S(1)} %get-tuple-element.46), channel_id=1, source_target_pairs={{0,16},{1,17},{2,18},{3,19},{4,20},{5,21},{6,22},{7,23},{8,24},{9,... | collective-permute-start | bytes 147464 | tf_op jit(solution)/shard_map/ppermute | solution.py:355
  19.9 5.4 %collective-permute-start.7 = (f32[32,384]{1,0:T(8,128)S(1)}, f32[32,384]{1,0:T(8,128)S(1)}, u32[]{:S(2)}, u32[]{:S(2)}) collective-permute-start(f32[32,384]{1,0:T(8,128)S(1)} %get-tuple-element.47), channel_id=1, source_target_pairs={{0,1},{1,0},{2,3},{3,2},{4,5},{5,4},{6,7},{7,6},{8,9},{9,8},{10,11... | collective-permute-start | bytes 147464 | tf_op jit(solution)/shard_map/ppermute | solution.py:355
  20.6 4.6 %collective-permute-start.9 = (f32[1,1,1024]{2,1,0:T(1,128)S(1)}, f32[1,1,1024]{2,1,0:T(1,128)S(1)}, u32[]{:S(2)}, u32[]{:S(2)}) collective-permute-start(f32[1,1,1024]{2,1,0:T(1,128)S(1)} %shard_map.74.told), channel_id=1, source_target_pairs={{0,16},{1,2},{2,1},{3,4},{4,3},{5,6},{6,5},{7,8},{8,7},{9,10},{10,... | collective-permute-start | bytes 12296 | tf_op jit(solution)/shard_map/ppermute | solution.py:355
  22.7 2.6 %collective-permute-start.8 = (f32[1,1,1024]{2,1,0:T(1,128)S(1)}, f32[1,1,1024]{2,1,0:T(1,128)S(1)}, u32[]{:S(2)}, u32[]{:S(2)}) collective-permute-start(f32[1,1,1024]{2,1,0:T(1,128)S(1)} %shard_map.74.told), channel_id=1, source_target_pairs={{0,1},{1,0},{2,3},{3,2},{4,5},{5,4},{6,7},{7,6},{8,9},{9,8},{10,11... | collective-permute-start | bytes 12296 | tf_op jit(solution)/shard_map/ppermute | solution.py:355
  26.4 3.7 %collective-permute-start.10 = (f32[32,256]{1,0:T(8,128)S(1)}, f32[32,256]{1,0:T(8,128)S(1)}, u32[]{:S(2)}, u32[]{:S(2)}) collective-permute-start(f32[32,256]{1,0:T(8,128)S(1)} %get-tuple-element.50), channel_id=1, source_target_pairs={{0,16},{1,17},{2,18},{3,19},{4,20},{5,21},{6,22},{7,23},{8,24},{9,... | collective-permute-start | bytes 98312 | tf_op jit(solution)/shard_map/ppermute | solution.py:355
  29.1 3.6 %collective-permute-start.11 = (f32[32,256]{1,0:T(8,128)S(1)}, f32[32,256]{1,0:T(8,128)S(1)}, u32[]{:S(2)}, u32[]{:S(2)}) collective-permute-start(f32[32,256]{1,0:T(8,128)S(1)} %get-tuple-element.51), channel_id=1, source_target_pairs={{0,1},{1,0},{2,3},{3,2},{4,5},{5,4},{6,7},{7,6},{8,9},{9,8},{10,11... | collective-permute-start | bytes 98312 | tf_op jit(solution)/shard_map/ppermute | solution.py:355

commit v4 on v3

--- a/solution.py
+++ b/solution.py
@@ -69,13 +69,15 @@
 def overlap(low_edge, high_edge, cells):
     begin = cells * CELL
     covered = jnp.minimum(high_edge, begin + CELL) - jnp.maximum(low_edge, begin)
-    return jnp.maximum(covered, 0).astype(F32) * (1.0 / CELL)
-
-
-def spread(distance):
-    scaled = distance.astype(F32) / BETA
-    inside = jnp.abs(distance) <= REACH
-    return jnp.where(inside, jnp.exp(-scaled * scaled) / (math.sqrt(math.pi) * BETA), 0.0)
+    return jnp.maximum(covered, 0.0) * (1.0 / CELL)
+
+
+def gauss(cells, places):
+    rate = math.sqrt(math.log2(math.e)) / BETA
+    level = -math.log2(math.sqrt(math.pi) * BETA)
+    scaled = cells * rate - places.astype(F32) * rate
+    square = scaled * scaled
+    return jnp.where(square <= (rate * (REACH + 0.5)) ** 2, jnp.exp2(level - square), 0.0)
 
 
 def iota(shape, axis):
@@ -111,6 +113,10 @@
 
 def boxes_of(tile):
     return [tile[k].astype(jnp.int32) for k in range(4)]
+
+
+def cells_from(first, count):
+    return (iota((count, SLOTS), 0) + first).astype(F32)
 
 
 def edge_part(py):
@@ -143,47 +149,60 @@
     return jnp.sum(value.reshape(BLK // 8, 8, SLOTS), axis=0)
 
 
-def early_kernel(tile, gain_in, px_out, py_out, pairs, told, gain, arrived):
+def early_kernel(tile, gain_in, px_out, py_out, pairs, told, gain, gain_parts, picked, chosen_x, arrived):
     copy = pltpu.make_async_copy(gain_in, gain, arrived)
     copy.start()
+    boxes = boxes_of(tile)
+    pixel_x = (boxes[0] + boxes[2]) // 2
+    pixel_y = (boxes[1] + boxes[3]) // 2
+    for at in range(0, TILE, 16):
+        chosen_x[at : at + 16, :] = jnp.where(iota((16, SLOTS), 0) + at == pixel_x, 1.0, 0.0).astype(BF16)
     inverse = 1.0 / FORWARD_RANGE
     box = [tile[k] for k in range(4)]
-    centre_x = (box[0] + box[2]) * (0.5 * inverse)
-    centre_y = (box[1] + box[3]) * (0.5 * inverse)
+    centre_x = jnp.broadcast_to((box[0] + box[2]) * (0.5 * inverse), (8, SLOTS))
+    centre_y = jnp.broadcast_to((box[1] + box[3]) * (0.5 * inverse), (8, SLOTS))
     columns = jnp.concatenate([b * inverse for b in box] + [tile[4], jnp.zeros((3, SLOTS), F32)], axis=0)
     total = jnp.zeros((8, SLOTS), F32)
-    for at in range(0, SLOTS, BLK):
+    for block in range(MAXB):
+        at = block * BLK
+        if block == 3:
+            copy.wait()
+            high, low = two_parts(gain[...])
+            gain_parts[...] = jnp.concatenate([high, low], axis=1)
+        if block >= 3 and block < 7:
+            lanes = slice((block - 3) * 256, (block - 2) * 256)
+            chosen = chosen_x[:, lanes]
+            picked[...] = jnp.dot(gain_parts[...], jnp.concatenate([chosen, chosen], axis=0), preferred_element_type=F32)
         side = jnp.transpose(columns[:, at : at + BLK])
-        along_x = lax.erf(centre_x - side[:, 0:1]) - lax.erf(centre_x - side[:, 2:3])
-        along_y = lax.erf(centre_y - side[:, 1:2]) - lax.erf(centre_y - side[:, 3:4])
-        block = (0.25 * along_x) * along_y
-        pairs[at : at + BLK, :] = block
-        total += folded_sum(side[:, 4:5] * block)
+        for down in range(0, BLK, 8):
+            low_x, low_y, high_x, high_y, dose = [side[down : down + 8, k : k + 1] for k in range(5)]
+            along_x = lax.erf(centre_x - low_x) - lax.erf(centre_x - high_x)
+            along_y = lax.erf(centre_y - low_y) - lax.erf(centre_y - high_y)
+            values = (0.25 * along_x) * along_y
+            pairs[at + down : at + down + 8, :] = values
+            total += dose * values
+        if block >= 3 and block < 7:
+            found = jnp.zeros((8, 256), F32)
+            for row in range(0, TILE, 8):
+                found += jnp.where(iota((8, 256), 0) + row == pixel_y[:, lanes], picked[row : row + 8, :], 0.0)
+            told[1, :, lanes] = jnp.sum(found, axis=0, keepdims=True)
+        if block < 3:
+            for first in range(block * 48, min(block * 48 + 48, CG), 16):
+                px_out[first : first + 16, :] = overlap(box[0], box[2], cells_from(first, 16)).astype(BF16)
+                py_out[first : first + 16, :] = overlap(box[1], box[3], cells_from(first, 16)).astype(BF16)
     told[0] = jnp.sum(total, axis=0, keepdims=True)
-    boxes = boxes_of(tile)
-    px_out[...] = overlap(boxes[0], boxes[2], iota((CG, SLOTS), 0)).astype(BF16)
-    py_out[...] = overlap(boxes[1], boxes[3], iota((CG, SLOTS), 0)).astype(BF16)
-    pixel_x = (boxes[0] + boxes[2]) // 2
-    pixel_y = (boxes[1] + boxes[3]) // 2
-    pixels = iota((TILE, SLOTS), 0)
-    chosen_x = jnp.where(pixels == pixel_x, 1.0, 0.0).astype(BF16)
-    copy.wait()
-    picked = stacked_dot(gain[...], chosen_x, (((1,), (0,)), ((), ())))
-    told[1] = jnp.sum(jnp.where(pixels == pixel_y, picked, 0.0), axis=0, keepdims=True)
 
 
 def first_strips_kernel(own, got_even, got_odd, px, py, left_out, right_out, px_left, px_right, send_even, send_odd):
     left, right = sides(got_even[...], got_odd[...])
     left_out[...] = left
     right_out[...] = right
-    edge_cells = iota((2 * REACH, SLOTS), 0)
-    edge_cells = jnp.where(edge_cells < REACH, edge_cells, edge_cells + (CG - 2 * REACH))
+    edge_cells = jnp.concatenate([cells_from(0, REACH), cells_from(CG - REACH, REACH)], axis=0)
     edges = [stacked_dot(edge_part(py) * own[4], px[...], NT)]
     for tile, px_out in ((left, px_left), (right, px_right)):
-        boxes = boxes_of(tile)
-        across = overlap(boxes[0], boxes[2], iota((CG, SLOTS), 0)).astype(BF16)
+        across = overlap(tile[0], tile[2], cells_from(0, CG)).astype(BF16)
         px_out[...] = across
-        edges.append(stacked_dot(overlap(boxes[1], boxes[3], edge_cells) * tile[4], across, NT))
+        edges.append(stacked_dot(overlap(tile[1], tile[3], edge_cells) * tile[4], across, NT))
     send_rows(jnp.concatenate([edges[1], edges[0], edges[2]], axis=1), send_even, send_odd)
 
 
@@ -221,15 +240,19 @@
 def late_kernel(own, left, right, px_left, px, px_right, py, py_left, py_right, wy_high, wy_low, wx_left, wx, wx_right, inner):
     tiles = (left, own, right)
     boxes = [boxes_of(tile) for tile in tiles]
-    y = iota((ALL, SLOTS), 0)
-    y = jnp.where(y < CG, y, jnp.where(y < CG + REACH, y - (CG + REACH), y - REACH))
-    x = iota((SIDE, SLOTS), 0)
-    places = (x, y, jnp.where(x < CG, x, x - (CG + REACH)))
-    for k, (box, place, out) in enumerate(zip(boxes, places, (wx_left, wx, wx_right))):
-        out[...] = spread((box[0] + box[2]) // (2 * CELL) - place)
-        wy_high[k], wy_low[k] = two_parts(spread((box[1] + box[3]) // (2 * CELL) - y))
-    for box, out in ((boxes[0], py_left), (boxes[2], py_right)):
-        out[...] = overlap(box[1], box[3], iota((CG, SLOTS), 0)).astype(BF16)
+    cells = [[((box[k] + box[k + 2]) // (2 * CELL)).astype(F32) for k in range(2)] for box in boxes]
+    for at in range(0, ALL, 16):
+        apart = CG + REACH if CG <= at < CG + REACH else (REACH if at >= CG + REACH else 0)
+        outer = iota((16, 1), 0) + (at - apart)
+        for k, box_cells in enumerate(cells):
+            wy_high[k, at : at + 16, :], wy_low[k, at : at + 16, :] = two_parts(gauss(box_cells[1], outer))
+        wx[at : at + 16, :] = gauss(cells[1][0], outer)
+        if at < SIDE:
+            columns = iota((16, 1), 0) + at
+            wx_left[at : at + 16, :] = gauss(cells[0][0], columns)
+            wx_right[at : at + 16, :] = gauss(cells[2][0], columns if at < CG else columns - SIDE)
+    for tile, out in ((left, py_left), (right, py_right)):
+        out[...] = overlap(tile[1], tile[3], cells_from(0, CG)).astype(BF16)
     inner_sums(
         [tile[4] for tile in tiles],
         (px_left[...], px[...], px_right[...]),
@@ -382,7 +405,13 @@
         early_kernel,
         (cover, cover, shape(SLOTS, SLOTS), shape(2, 1, SLOTS)),
         ins=[VMEM, HBM],
-        scratch=(pltpu.VMEM((TILE, TILE), F32), pltpu.SemaphoreType.DMA),
+        scratch=(
+            pltpu.VMEM((TILE, TILE), F32),
+            pltpu.VMEM((TILE, 2 * TILE), BF16),
+            pltpu.VMEM((TILE, 256), F32),
+            pltpu.VMEM((TILE, SLOTS), BF16),
+            pltpu.SemaphoreType.DMA,
+        ),
     )(own, *in_hbm(pixel_gain))
     told_odd = send(told, col_odd)
     left, right, px_left, px_right, strip_even, strip_odd = call(

time: 34 us -> 31.5 us (0.926)
  Pallas kernels: 15.9 us -> 13.5 us
    pallas_call x1, Pallas kernels: 4.93 us -> 3.82 us  [body(): call(early_kernel, (cover, cover, shape(SLOTS, SLOTS), shape(2, 1, SLOTS)...]
    pallas_call x1, Pallas kernels: 3.14 us -> 2.12 us  [body(): call(late_kernel, (cover, cover, weights, weights, shape(SIDE, SLOTS), sh...]
  transfers between devices with their start and end apart: 12 -> 12, of which waited for: 3 -> 3; matrix products, arithmetic and copies ran while one was open for 0% -> 0% of each run, Pallas kernels for 32% -> 28%
where the time goes in v4:
time: 31.5 us; the launch traced here: 31.3 us
  Pallas kernels  13.5 us (43%)
  starting transfers between devices  13.1 us (42%)
  waiting for transfers between devices  3.97 us (13%)
  between operations  0.74 us (2%)
    ppermute x12, starting transfers between devices, send(): return lax.ppermute(value, AXES, table)  13.1 us
    ppermute x12, waiting for transfers between devices, send(): return lax.ppermute(value, AXES, table)  3.97 us
    pallas_call x1, Pallas kernels, body(): call(early_kernel, (cover, cover, shape(SLOTS, SLOTS), shape(2, 1, SLOTS)...  3.82 us
    pallas_call x1, Pallas kernels, body(): call(late_kernel, (cover, cover, weights, weights, shape(SIDE, SLOTS), sh...  2.12 us
    pallas_call x1, Pallas kernels, body(): inner = call(inner_kernel, rows)(doses3, *covers, *weighing)  1.31 us
    pallas_call x1, Pallas kernels, body(): call(final_kernel, (row, row))  1.08 us
    pallas_call x1, Pallas kernels, body(): call(last_inner_kernel, (row, row))  0.95 us
    pallas_call x1, Pallas kernels, body(): call(start_kernel, tile, ins=[HBM] * 4, scratch=(pltpu.VMEM((4, 1, SLOTS)...  0.87 us
  transfers between devices with their start and end apart: 12, of which 3 were waited for; matrix products, arithmetic and copies ran while one was open for 0% of the time, Pallas kernels for 28%

profile of v4, /device:TPU:97, one launch (start us, length us, event | category | flops | bytes accessed | tf_op | source)
XLA Modules:
  0.0 31.3 jit_solution(9383718738193016127)
XLA Ops:
  0.6 0.9 %shard_map.68.tile.own = f32[5,1,1024]{2,1,0:T(1,128)S(1)} custom-call(s32[4,1,1024]{2,1,0:T(1,128)} %boxes_in.1, s32[1,16]{1,0:T(1,128)} %counts_in.1, s32[1,16]{1,0:T(1,128)} %tails_in.1, f32[1,1024]{1,0:T(1,128)} %doses_in.1), custom_call_target="tpu_custom_call" | custom-call | tf_op jit(solution)/shard_map/pallas_call | solution.py:390
  1.5 2.4 %collective-permute-start.1 = (f32[5,1,1024]{2,1,0:T(1,128)S(1)}, f32[5,1,1024]{2,1,0:T(1,128)S(1)}, u32[]{:S(2)}, u32[]{:S(2)}) collective-permute-start(f32[5,1,1024]{2,1,0:T(1,128)S(1)} %shard_map.68.tile.own), channel_id=1, source_target_pairs={{0,16},{1,2},{2,1},{3,4},{4,3},{5,6},{6,5},{7,8},{8,7},{9,10},{10,... | collective-permute-start | bytes 61448 | tf_op jit(solution)/shard_map/ppermute | solution.py:378
  3.9 0.1 collective-permute-start
  4.0 3.8 %shard_map.69 = (bf16[128,1024]{1,0:T(8,128)(2,1)S(1)}, bf16[128,1024]{1,0:T(8,128)(2,1)S(1)}, f32[1024,1024]{1,0:T(8,128)S(1)}, f32[2,1,1024]{2,1,0:T(1,128)S(1)}) custom-call(f32[5,1,1024]{2,1,0:T(1,128)S(1)} %shard_map.68.tile.own, f32[512,512]{1,0:T(8,128)} %gain_in.1), custom_call_target="tpu_custom_call" | custom-call | tf_op jit(solution)/shard_map/pallas_call | solution.py:404
  7.8 0.0 collective-permute-done.1.got_odd
  7.8 0.0 collective-permute-done.got_even
  7.9 0.7 %shard_map.70 = (f32[5,1,1024]{2,1,0:T(1,128)S(1)}, f32[5,1,1024]{2,1,0:T(1,128)S(1)}, bf16[128,1024]{1,0:T(8,128)(2,1)S(1)}, bf16[128,1024]{1,0:T(8,128)(2,1)S(...) custom-call(f32[5,1,1024]{2,1,0:T(1,128)S(1)} %shard_map.68.tile.own, f32[5,1,1024]{2,1,0:T(1,128)S(1)} %collective-permute-done.got_even, ...), custom_call_target="tpu_custom_call" | custom-call | tf_op jit(solution)/shard_map/pallas_call | solution.py:417
  8.5 1.3 %collective-permute-start.2 = (f32[32,384]{1,0:T(8,128)S(1)}, f32[32,384]{1,0:T(8,128)S(1)}, u32[]{:S(2)}, u32[]{:S(2)}) collective-permute-start(f32[32,384]{1,0:T(8,128)S(1)} %get-tuple-element.30), channel_id=1, source_target_pairs={{0,16},{1,17},{2,18},{3,19},{4,20},{5,21},{6,22},{7,23},{8,24},{9,... | collective-permute-start | bytes 147464 | tf_op jit(solution)/shard_map/ppermute | solution.py:378
  9.8 1.3 %collective-permute-start.3 = (f32[32,384]{1,0:T(8,128)S(1)}, f32[32,384]{1,0:T(8,128)S(1)}, u32[]{:S(2)}, u32[]{:S(2)}) collective-permute-start(f32[32,384]{1,0:T(8,128)S(1)} %get-tuple-element.31), channel_id=1, source_target_pairs={{0,1},{1,0},{2,3},{3,2},{4,5},{5,4},{6,7},{7,6},{8,9},{9,8},{10,11... | collective-permute-start | bytes 147464 | tf_op jit(solution)/shard_map/ppermute | solution.py:378
  11.1 1.4 %collective-permute-start.5 = (f32[2,1,1024]{2,1,0:T(1,128)S(1)}, f32[2,1,1024]{2,1,0:T(1,128)S(1)}, u32[]{:S(2)}, u32[]{:S(2)}) collective-permute-start(f32[2,1,1024]{2,1,0:T(1,128)S(1)} %get-tuple-element.32.told), channel_id=1, source_target_pairs={{0,16},{1,2},{2,1},{3,4},{4,3},{5,6},{6,5},{7,8},{8,7},{9,10},{10,... | collective-permute-start | bytes 24584 | tf_op jit(solution)/shard_map/ppermute | solution.py:378
  12.5 0.0 collective-permute-start.4
  12.5 2.1 %shard_map.71 = (bf16[128,1024]{1,0:T(8,128)(2,1)S(1)}, bf16[128,1024]{1,0:T(8,128)(2,1)S(1)}, bf16[3,192,1024]{2,1,0:T(8,128)(2,1)S(1)}, bf16[3,192,1024]{2,1,0...) custom-call(f32[5,1,1024]{2,1,0:T(1,128)S(1)} %shard_map.68.tile.own, ...), custom_call_target="tpu_custom_call" | custom-call | tf_op jit(solution)/shard_map/pallas_call | solution.py:423
  14.6 1.1 %collective-permute-done.5.told_odd = f32[2,1,1024]{2,1,0:T(1,128)S(1)} collective-permute-done((f32[2,1,1024]{2,1,0:T(1,128)S(1)}, f32[2,1,1024]{2,1,0:T(1,128)S(1)}, u32[]{:S(2)}, u32[]{:S(2)}) %collective-permute-start.5) | collective-permute-done | bytes 8224 | tf_op jit(solution)/shard_map/ppermute | solution.py:378
  15.7 0.0 collective-permute-done.4.told_even
  15.7 0.0 collective-permute-done.2.got_even
  15.7 0.0 collective-permute-done.3.got_odd
  15.7 0.7 %shard_map.72 = (f32[3,1,1024]{2,1,0:T(1,128)S(1)}, f32[3,1,1024]{2,1,0:T(1,128)S(1)}) custom-call(f32[32,384]{1,0:T(8,128)S(1)} %collective-permute-done.2.got_even, f32[32,384]{1,0:T(8,128)S(1)} %collective-permute-done.3.got_odd, f32[2,1,1024]{2,1,0:T(1,128)S(1)} %get-tuple-element.32.told, f32[2,1,1024]{2,1,0:T(1,128)S(1)} %collective-permute-done.4.told_even, ...), custom_call_target="tpu_custom_call" | custom-call | tf_op jit(solution)/shard_map/pallas_call | solution.py:428
  16.4 0.4 %shard_map.73 = (f32[32,384]{1,0:T(8,128)S(1)}, f32[32,384]{1,0:T(8,128)S(1)}) custom-call(f32[3,1,1024]{2,1,0:T(1,128)S(1)} %get-tuple-element.43.doses, bf16[128,1024]{1,0:T(8,128)(2,1)S(1)} %get-tuple-element.35.px_left, bf16[128,1024]{1,0:T(8,128)(2,1)S(1)} %get-tuple-element.28.px, bf16[128,1024]{1,0:T(8,128)(2,1)S(1)} %get-tuple-element.36.px_right, ...), custom_call_target="tpu_custom_call" | custom-call | tf_op jit(solution)/shard_map/pallas_call | solution.py:433
  16.8 1.7 %collective-permute-start.6 = (f32[32,384]{1,0:T(8,128)S(1)}, f32[32,384]{1,0:T(8,128)S(1)}, u32[]{:S(2)}, u32[]{:S(2)}) collective-permute-start(f32[32,384]{1,0:T(8,128)S(1)} %get-tuple-element.46), channel_id=1, source_target_pairs={{0,16},{1,17},{2,18},{3,19},{4,20},{5,21},{6,22},{7,23},{8,24},{9,... | collective-permute-start | bytes 147464 | tf_op jit(solution)/shard_map/ppermute | solution.py:378
  18.5 0.1 collective-permute-start.7
  18.7 0.5 %shard_map.74.told = f32[1,1,1024]{2,1,0:T(1,128)S(1)} custom-call(f32[3,1,1024]{2,1,0:T(1,128)S(1)} %get-tuple-element.43.doses, f32[1024,1024]{1,0:T(8,128)S(1)} %get-tuple-element.48.pairs), custom_call_target="tpu_custom_call" | custom-call | tf_op jit(solution)/shard_map/pallas_call | solution.py:431
  19.1 1.9 %collective-permute-start.9 = (f32[1,1,1024]{2,1,0:T(1,128)S(1)}, f32[1,1,1024]{2,1,0:T(1,128)S(1)}, u32[]{:S(2)}, u32[]{:S(2)}) collective-permute-start(f32[1,1,1024]{2,1,0:T(1,128)S(1)} %shard_map.74.told), channel_id=1, source_target_pairs={{0,16},{1,2},{2,1},{3,4},{4,3},{5,6},{6,5},{7,8},{8,7},{9,10},{10,... | collective-permute-start | bytes 12296 | tf_op jit(solution)/shard_map/ppermute | solution.py:378
  21.0 0.0 collective-permute-start.8
  21.0 1.3 %shard_map.75.inner = f32[3,1,1024]{2,1,0:T(1,128)S(1)} custom-call(f32[3,1,1024]{2,1,0:T(1,128)S(1)} %get-tuple-element.43.doses, bf16[128,1024]{1,0:T(8,128)(2,1)S(1)} %get-tuple-element.35.px_left, bf16[128,1024]{1,0:T(8,128)(2,1)S(1)} %get-tuple-element.28.px, bf16[128,1024]{1,0:T(8,128)(2,1)S(1)} %get-tuple-element.36.px_right, ...), custom_call_target="tpu_custom_call" | custom-call | tf_op jit(solution)/shard_map/pallas_call | solution.py:437
  22.3 1.5 %collective-permute-done.9.told_odd = f32[1,1,1024]{2,1,0:T(1,128)S(1)} collective-permute-done((f32[1,1,1024]{2,1,0:T(1,128)S(1)}, f32[1,1,1024]{2,1,0:T(1,128)S(1)}, u32[]{:S(2)}, u32[]{:S(2)}) %collective-permute-start.9) | collective-permute-done | bytes 4128 | tf_op jit(solution)/shard_map/ppermute | solution.py:378
  23.8 0.0 collective-permute-done.8.told_even
  23.8 0.0 collective-permute-done.6.got_even
  23.8 0.0 collective-permute-done.7.got_odd
  23.8 0.7 %shard_map.76.doses = f32[3,1,1024]{2,1,0:T(1,128)S(1)} custom-call(f32[32,384]{1,0:T(8,128)S(1)} %collective-permute-done.6.got_even, f32[32,384]{1,0:T(8,128)S(1)} %collective-permute-done.7.got_odd, f32[1,1,1024]{2,1,0:T(1,128)S(1)} %shard_map.74.told, f32[1,1,1024]{2,1,0:T(1,128)S(1)} %collective-permute-done.8.told_even, ...), custom_call_target="tpu_custom_call" | custom-call | tf_op jit(solution)/shard_map/pallas_call | solution.py:438
  24.5 0.4 %shard_map.77 = (f32[32,256]{1,0:T(8,128)S(1)}, f32[32,256]{1,0:T(8,128)S(1)}) custom-call(f32[3,1,1024]{2,1,0:T(1,128)S(1)} %shard_map.76.doses, bf16[128,1024]{1,0:T(8,128)(2,1)S(1)} %get-tuple-element.35.px_left, bf16[128,1024]{1,0:T(8,128)(2,1)S(1)} %get-tuple-element.28.px, bf16[128,1024]{1,0:T(8,128)(2,1)S(1)} %get-tuple-element.36.px_right, ...), custom_call_target="tpu_custom_call" | custom-call | tf_op jit(solution)/shard_map/pallas_call | solution.py:439
  24.9 1.6 %collective-permute-start.10 = (f32[32,256]{1,0:T(8,128)S(1)}, f32[32,256]{1,0:T(8,128)S(1)}, u32[]{:S(2)}, u32[]{:S(2)}) collective-permute-start(f32[32,256]{1,0:T(8,128)S(1)} %get-tuple-element.50), channel_id=1, source_target_pairs={{0,16},{1,17},{2,18},{3,19},{4,20},{5,21},{6,22},{7,23},{8,24},{9,... | collective-permute-start | bytes 98312 | tf_op jit(solution)/shard_map/ppermute | solution.py:378
  26.6 1.3 %collective-permute-start.11 = (f32[32,256]{1,0:T(8,128)S(1)}, f32[32,256]{1,0:T(8,128)S(1)}, u32[]{:S(2)}, u32[]{:S(2)}) collective-permute-start(f32[32,256]{1,0:T(8,128)S(1)} %get-tuple-element.51), channel_id=1, source_target_pairs={{0,1},{1,0},{2,3},{3,2},{4,5},{5,4},{6,7},{7,6},{8,9},{9,8},{10,11... | collective-permute-start | bytes 98312 | tf_op jit(solution)/shard_map/ppermute | solution.py:378
  27.9 1.0 %shard_map.78 = (f32[1,1024]{1,0:T(1,128)S(1)}, f32[1,1024]{1,0:T(1,128)S(1)}) custom-call(f32[3,1,1024]{2,1,0:T(1,128)S(1)} %shard_map.76.doses, bf16[128,1024]{1,0:T(8,128)(2,1)S(1)} %get-tuple-element.35.px_left, bf16[128,1024]{1,0:T(8,128)(2,1)S(1)} %get-tuple-element.28.px, bf16[128,1024]{1,0:T(8,128)(2,1)S(1)} %get-tuple-element.36.px_right, ...), custom_call_target="tpu_custom_call" | custom-call | tf_op jit(solution)/shard_map/pallas_call | solution.py:442
  28.8 0.0 collective-permute-done.10.got_even
  28.8 1.3 %collective-permute-done.11.got_odd = f32[32,256]{1,0:T(8,128)S(1)} collective-permute-done((f32[32,256]{1,0:T(8,128)S(1)}, f32[32,256]{1,0:T(8,128)S(1)}, u32[]{:S(2)}, u32[]{:S(2)}) %collective-permute-start.11) | collective-permute-done | bytes 32800 | tf_op jit(solution)/shard_map/ppermute | solution.py:378
  30.2 1.1 %shard_map.79 = (f32[1,1024]{1,0:T(1,128)}, f32[1,1024]{1,0:T(1,128)}) custom-call(f32[32,256]{1,0:T(8,128)S(1)} %collective-permute-done.10.got_even, f32[32,256]{1,0:T(8,128)S(1)} %collective-permute-done.11.got_odd, f32[3,1,1024]{2,1,0:T(1,128)S(1)} %shard_map.76.doses, f32[3,1,1024]{2,1,0:T(1,128)S(1)} %get-tuple-element.49.sens, ...), custom_call_target="tpu_custom_call" | custom-call | tf_op jit(solution)/shard_map/pallas_call | solution.py:443
Async XLA Ops:
  1.5 6.3 %collective-permute-start.1 = (f32[5,1,1024]{2,1,0:T(1,128)S(1)}, f32[5,1,1024]{2,1,0:T(1,128)S(1)}, u32[]{:S(2)}, u32[]{:S(2)}) collective-permute-start(f32[5,1,1024]{2,1,0:T(1,128)S(1)} %shard_map.68.tile.own), channel_id=1, source_target_pairs={{0,16},{1,2},{2,1},{3,4},{4,3},{5,6},{6,5},{7,8},{8,7},{9,10},{10,... | collective-permute-start | bytes 61448 | tf_op jit(solution)/shard_map/ppermute | solution.py:378
  3.9 4.0 %collective-permute-start = (f32[5,1,1024]{2,1,0:T(1,128)S(1)}, f32[5,1,1024]{2,1,0:T(1,128)S(1)}, u32[]{:S(2)}, u32[]{:S(2)}) collective-permute-start(f32[5,1,1024]{2,1,0:T(1,128)S(1)} %shard_map.68.tile.own), channel_id=1, source_target_pairs={{0,1},{1,0},{2,3},{3,2},{4,5},{5,4},{6,7},{7,6},{8,9},{9,8},{10,11... | collective-permute-start | bytes 61448 | tf_op jit(solution)/shard_map/ppermute | solution.py:378
  8.5 7.2 %collective-permute-start.2 = (f32[32,384]{1,0:T(8,128)S(1)}, f32[32,384]{1,0:T(8,128)S(1)}, u32[]{:S(2)}, u32[]{:S(2)}) collective-permute-start(f32[32,384]{1,0:T(8,128)S(1)} %get-tuple-element.30), channel_id=1, source_target_pairs={{0,16},{1,17},{2,18},{3,19},{4,20},{5,21},{6,22},{7,23},{8,24},{9,... | collective-permute-start | bytes 147464 | tf_op jit(solution)/shard_map/ppermute | solution.py:378
  9.8 5.9 %collective-permute-start.3 = (f32[32,384]{1,0:T(8,128)S(1)}, f32[32,384]{1,0:T(8,128)S(1)}, u32[]{:S(2)}, u32[]{:S(2)}) collective-permute-start(f32[32,384]{1,0:T(8,128)S(1)} %get-tuple-element.31), channel_id=1, source_target_pairs={{0,1},{1,0},{2,3},{3,2},{4,5},{5,4},{6,7},{7,6},{8,9},{9,8},{10,11... | collective-permute-start | bytes 147464 | tf_op jit(solution)/shard_map/ppermute | solution.py:378
  11.1 4.6 %collective-permute-start.5 = (f32[2,1,1024]{2,1,0:T(1,128)S(1)}, f32[2,1,1024]{2,1,0:T(1,128)S(1)}, u32[]{:S(2)}, u32[]{:S(2)}) collective-permute-start(f32[2,1,1024]{2,1,0:T(1,128)S(1)} %get-tuple-element.32.told), channel_id=1, source_target_pairs={{0,16},{1,2},{2,1},{3,4},{4,3},{5,6},{6,5},{7,8},{8,7},{9,10},{10,... | collective-permute-start | bytes 24584 | tf_op jit(solution)/shard_map/ppermute | solution.py:378
  12.5 3.2 %collective-permute-start.4 = (f32[2,1,1024]{2,1,0:T(1,128)S(1)}, f32[2,1,1024]{2,1,0:T(1,128)S(1)}, u32[]{:S(2)}, u32[]{:S(2)}) collective-permute-start(f32[2,1,1024]{2,1,0:T(1,128)S(1)} %get-tuple-element.32.told), channel_id=1, source_target_pairs={{0,1},{1,0},{2,3},{3,2},{4,5},{5,4},{6,7},{7,6},{8,9},{9,8},{10,11... | collective-permute-start | bytes 24584 | tf_op jit(solution)/shard_map/ppermute | solution.py:378
  16.8 7.0 %collective-permute-start.6 = (f32[32,384]{1,0:T(8,128)S(1)}, f32[32,384]{1,0:T(8,128)S(1)}, u32[]{:S(2)}, u32[]{:S(2)}) collective-permute-start(f32[32,384]{1,0:T(8,128)S(1)} %get-tuple-element.46), channel_id=1, source_target_pairs={{0,16},{1,17},{2,18},{3,19},{4,20},{5,21},{6,22},{7,23},{8,24},{9,... | collective-permute-start | bytes 147464 | tf_op jit(solution)/shard_map/ppermute | solution.py:378
  18.5 5.3 %collective-permute-start.7 = (f32[32,384]{1,0:T(8,128)S(1)}, f32[32,384]{1,0:T(8,128)S(1)}, u32[]{:S(2)}, u32[]{:S(2)}) collective-permute-start(f32[32,384]{1,0:T(8,128)S(1)} %get-tuple-element.47), channel_id=1, source_target_pairs={{0,1},{1,0},{2,3},{3,2},{4,5},{5,4},{6,7},{7,6},{8,9},{9,8},{10,11... | collective-permute-start | bytes 147464 | tf_op jit(solution)/shard_map/ppermute | solution.py:378
  19.1 4.6 %collective-permute-start.9 = (f32[1,1,1024]{2,1,0:T(1,128)S(1)}, f32[1,1,1024]{2,1,0:T(1,128)S(1)}, u32[]{:S(2)}, u32[]{:S(2)}) collective-permute-start(f32[1,1,1024]{2,1,0:T(1,128)S(1)} %shard_map.74.told), channel_id=1, source_target_pairs={{0,16},{1,2},{2,1},{3,4},{4,3},{5,6},{6,5},{7,8},{8,7},{9,10},{10,... | collective-permute-start | bytes 12296 | tf_op jit(solution)/shard_map/ppermute | solution.py:378
  21.0 2.8 %collective-permute-start.8 = (f32[1,1,1024]{2,1,0:T(1,128)S(1)}, f32[1,1,1024]{2,1,0:T(1,128)S(1)}, u32[]{:S(2)}, u32[]{:S(2)}) collective-permute-start(f32[1,1,1024]{2,1,0:T(1,128)S(1)} %shard_map.74.told), channel_id=1, source_target_pairs={{0,1},{1,0},{2,3},{3,2},{4,5},{5,4},{6,7},{7,6},{8,9},{9,8},{10,11... | collective-permute-start | bytes 12296 | tf_op jit(solution)/shard_map/ppermute | solution.py:378
  24.9 3.9 %collective-permute-start.10 = (f32[32,256]{1,0:T(8,128)S(1)}, f32[32,256]{1,0:T(8,128)S(1)}, u32[]{:S(2)}, u32[]{:S(2)}) collective-permute-start(f32[32,256]{1,0:T(8,128)S(1)} %get-tuple-element.50), channel_id=1, source_target_pairs={{0,16},{1,17},{2,18},{3,19},{4,20},{5,21},{6,22},{7,23},{8,24},{9,... | collective-permute-start | bytes 98312 | tf_op jit(solution)/shard_map/ppermute | solution.py:378
  26.6 3.6 %collective-permute-start.11 = (f32[32,256]{1,0:T(8,128)S(1)}, f32[32,256]{1,0:T(8,128)S(1)}, u32[]{:S(2)}, u32[]{:S(2)}) collective-permute-start(f32[32,256]{1,0:T(8,128)S(1)} %get-tuple-element.51), channel_id=1, source_target_pairs={{0,1},{1,0},{2,3},{3,2},{4,5},{5,4},{6,7},{7,6},{8,9},{9,8},{10,11... | collective-permute-start | bytes 98312 | tf_op jit(solution)/shard_map/ppermute | solution.py:378

commit v5 on v4

--- a/solution.py
+++ b/solution.py
@@ -206,17 +206,16 @@
     send_rows(jnp.concatenate([edges[1], edges[0], edges[2]], axis=1), send_even, send_odd)
 
 
-def strips_kernel(doses, px_left, px, px_right, py_left, py, py_right, send_even, send_odd):
-    pieces = ((0, px_left, py_left), (1, px, py), (2, px_right, py_right))
-    edges = [stacked_dot(edge_part(down) * doses[k], across[...], NT) for k, across, down in pieces]
+def strips(doses, px, py, send_even, send_odd):
+    edges = [stacked_dot(edge_part(down) * dose, across[...], NT) for dose, across, down in zip(doses, px, py)]
     send_rows(jnp.concatenate(edges, axis=1), send_even, send_odd)
 
 
-def last_strips_kernel(doses, px_left, px, px_right, py_left, py, py_right, send_even, send_odd):
+def last_strips(doses, px, py, send_even, send_odd):
     edges = [
-        stacked_dot(edge_part(py) * doses[1], px[...], NT),
-        stacked_dot(edge_part(py_left) * doses[0], px_left[CG - REACH :, :], NT),
-        stacked_dot(edge_part(py_right) * doses[2], px_right[:REACH, :], NT),
+        stacked_dot(edge_part(py[1]) * doses[1], px[1][...], NT),
+        stacked_dot(edge_part(py[0]) * doses[0], px[0][CG - REACH :, :], NT),
+        stacked_dot(edge_part(py[2]) * doses[2], px[2][:REACH, :], NT),
         jnp.zeros((2 * REACH, 2 * CG - ALL), F32),
     ]
     send_rows(jnp.concatenate(edges, axis=1), send_even, send_odd)
@@ -298,49 +297,49 @@
     return jnp.sum(total, axis=0, keepdims=True)
 
 
-def forward_kernel(doses, pairs, told):
-    told[0] = pair_sum(doses[1], pairs)
-
-
 def exposed(dose, sens, forward, background):
     live = dose > 0.0
     exposure = sens * (forward + BACK_RATIO * background) / (1.0 + BACK_RATIO)
     return jnp.where(live, dose * TARGET_LEVEL / jnp.where(live, exposure, 1.0), 0.0), jnp.where(live, exposure, 0.0)
 
 
-def update(got_even, got_odd, doses, sens, forward, inner, wy_high, wy_low, wx, doses_out):
+def new_doses(got_even, got_odd, doses, sens, forward, inner, wy_high, wy_low, wx):
     outer = outer_rows(got_even[...], got_odd[...])
     outer_t = [jnp.transpose(outer[:, k * CG : (k + 1) * CG]) for k in range(3)]
+    result = []
     for k, columns in enumerate(per_tile(*outer_t)):
         across = weighted(columns, wy_high[k, CG:, :], wy_low[k, CG:, :])
         background = inner[k] + jnp.sum(across * wx[k][...], axis=0, keepdims=True)
-        doses_out[k], _ = exposed(doses[k], sens[k], forward[k], background)
+        result.append(exposed(doses[k], sens[k], forward[k], background)[0])
+    return result
 
 
 def first_update_kernel(
-    got_even, got_odd, told, told_even, told_odd, own, left, right, inner, wy_high, wy_low, wx_left, wx, wx_right, doses_out, sens_out
+    got_even, got_odd, told, told_even, told_odd, own, left, right, inner, pairs, px_left, px, px_right, py_left, py, py_right,
+    wy_high, wy_low, wx_left, wx, wx_right, doses_out, sens_out, told_out, send_even, send_odd,
 ):
     told_left, told_right = sides(told_even[...], told_odd[...])
     forward, sens = zip((told_left[0], told_left[1]), (told[0], told[1]), (told_right[0], told_right[1]))
+    doses = new_doses(got_even, got_odd, (left[4], own[4], right[4]), sens, forward, inner, wy_high, wy_low, (wx_left, wx, wx_right))
     for k in range(3):
         sens_out[k] = sens[k]
-    update(got_even, got_odd, (left[4], own[4], right[4]), sens, forward, inner, wy_high, wy_low, (wx_left, wx, wx_right), doses_out)
-
-
-def update_kernel(got_even, got_odd, told, told_even, told_odd, doses, sens, inner, wy_high, wy_low, wx_left, wx, wx_right, doses_out):
+        doses_out[k] = doses[k]
+    told_out[0] = pair_sum(doses[1], pairs)
+    strips(doses, (px_left, px, px_right), (py_left, py, py_right), send_even, send_odd)
+
+
+def update_kernel(
+    got_even, got_odd, told, told_even, told_odd, doses, sens, inner, px_left, px, px_right, py_left, py, py_right,
+    wy_high, wy_low, wx_left, wx, wx_right, doses_out, send_even, send_odd,
+):
     told_left, told_right = sides(told_even[...], told_odd[...])
-    update(
-        got_even,
-        got_odd,
-        [doses[k] for k in range(3)],
-        [sens[k] for k in range(3)],
-        (told_left[0], told[0], told_right[0]),
-        inner,
-        wy_high,
-        wy_low,
-        (wx_left, wx, wx_right),
-        doses_out,
-    )
+    before = [doses[k] for k in range(3)]
+    factors = [sens[k] for k in range(3)]
+    forward = (told_left[0], told[0], told_right[0])
+    after = new_doses(got_even, got_odd, before, factors, forward, inner, wy_high, wy_low, (wx_left, wx, wx_right))
+    for k in range(3):
+        doses_out[k] = after[k]
+    last_strips(after, (px_left, px, px_right), (py_left, py, py_right), send_even, send_odd)
 
 
 def final_kernel(got_even, got_odd, doses, sens, inner, forward, wy_high, wy_low, wx, dose_out, exposure_out):
@@ -425,18 +424,17 @@
     )(own, left, right, px_left, px, px_right, py)
     covers = (px_left, px, px_right, py_left, py, py_right)
     weighing = (wy_high, wy_low, wx_left, wx, wx_right)
-    doses3, sens = call(first_update_kernel, (rows, rows))(
-        got_even, got_odd, told, told_even, told_odd, own, left, right, inner, *weighing
-    )
-    told = call(forward_kernel, shape(1, 1, SLOTS))(doses3, pairs)
-    told_odd = send(told, col_odd)
-    strip_even, strip_odd = call(strips_kernel, (strip, strip))(doses3, *covers)
+    doses3, sens, told_next, strip_even, strip_odd = call(first_update_kernel, (rows, rows, shape(1, 1, SLOTS), strip, strip))(
+        got_even, got_odd, told, told_even, told_odd, own, left, right, inner, pairs, *covers, *weighing
+    )
+    told_odd = send(told_next, col_odd)
     got_odd = send(strip_odd, row_odd)
+    told_even = send(told_next, col_even)
     got_even = send(strip_even, row_even)
-    told_even = send(told, col_even)
     inner = call(inner_kernel, rows)(doses3, *covers, *weighing)
-    doses3 = call(update_kernel, rows)(got_even, got_odd, told, told_even, told_odd, doses3, sens, inner, *weighing)
-    strip_even, strip_odd = call(last_strips_kernel, (short, short))(doses3, *covers)
+    doses3, strip_even, strip_odd = call(update_kernel, (rows, short, short))(
+        got_even, got_odd, told_next, told_even, told_odd, doses3, sens, inner, *covers, *weighing
+    )
     got_odd = send(strip_odd, row_odd)
     got_even = send(strip_even, row_even)
     inner, forward = call(last_inner_kernel, (row, row))(doses3, *covers, wy_high, wy_low, wx, pairs)

time: 31.5 us -> 31.1 us (0.987)
    pallas_call x5 -> x2, Pallas kernels: 2.69 us -> 2.44 us  [the longest x1 1.29 us: body(): call(first_update_kernel, (rows, rows, shape(1, 1, SLOTS), strip, strip))]
  transfers between devices with their start and end apart: 12 -> 12, of which waited for: 3 -> 3; matrix products, arithmetic and copies ran while one was open for 0% -> 0% of each run, Pallas kernels for 28% -> 27%
where the time goes in v5:
time: 31.1 us; the launch traced here: 30.9 us
  Pallas kernels  13.2 us (42%)
  starting transfers between devices  13 us (42%)
  waiting for transfers between devices  3.99 us (13%)
  between operations  0.73 us (2%)
    ppermute x12, starting transfers between devices, send(): return lax.ppermute(value, AXES, table)  13 us
    ppermute x12, waiting for transfers between devices, send(): return lax.ppermute(value, AXES, table)  3.99 us
    pallas_call x1, Pallas kernels, body(): call(early_kernel, (cover, cover, shape(SLOTS, SLOTS), shape(2, 1, SLOTS)...  3.84 us
    pallas_call x1, Pallas kernels, body(): call(late_kernel, (cover, cover, weights, weights, shape(SIDE, SLOTS), sh...  2.12 us
    pallas_call x1, Pallas kernels, body(): call(first_update_kernel, (rows, rows, shape(1, 1, SLOTS), strip, strip))  1.29 us
    pallas_call x1, Pallas kernels, body(): inner = call(inner_kernel, rows)(doses3, *covers, *weighing)  1.28 us
    pallas_call x1, Pallas kernels, body(): call(update_kernel, (rows, short, short))  1.16 us
    pallas_call x1, Pallas kernels, body(): call(final_kernel, (row, row))  1.09 us
  transfers between devices with their start and end apart: 12, of which 3 were waited for; matrix products, arithmetic and copies ran while one was open for 0% of the time, Pallas kernels for 27%

profile of v5, /device:TPU:97, one launch (start us, length us, event | category | flops | bytes accessed | tf_op | source)
XLA Modules:
  0.0 30.9 jit_solution(4659640371735897317)
XLA Ops:
  0.6 0.9 %shard_map.68.tile.own = f32[5,1,1024]{2,1,0:T(1,128)S(1)} custom-call(s32[4,1,1024]{2,1,0:T(1,128)} %boxes_in.1, s32[1,16]{1,0:T(1,128)} %counts_in.1, s32[1,16]{1,0:T(1,128)} %tails_in.1, f32[1,1024]{1,0:T(1,128)} %doses_in.1), custom_call_target="tpu_custom_call" | custom-call | tf_op jit(solution)/shard_map/pallas_call | solution.py:389
  1.5 2.4 %collective-permute-start.1 = (f32[5,1,1024]{2,1,0:T(1,128)S(1)}, f32[5,1,1024]{2,1,0:T(1,128)S(1)}, u32[]{:S(2)}, u32[]{:S(2)}) collective-permute-start(f32[5,1,1024]{2,1,0:T(1,128)S(1)} %shard_map.68.tile.own), channel_id=1, source_target_pairs={{0,16},{1,2},{2,1},{3,4},{4,3},{5,6},{6,5},{7,8},{8,7},{9,10},{10,... | collective-permute-start | bytes 61448 | tf_op jit(solution)/shard_map/ppermute | solution.py:377
  3.9 0.1 collective-permute-start
  4.0 3.8 %shard_map.69 = (bf16[128,1024]{1,0:T(8,128)(2,1)S(1)}, bf16[128,1024]{1,0:T(8,128)(2,1)S(1)}, f32[1024,1024]{1,0:T(8,128)S(1)}, f32[2,1,1024]{2,1,0:T(1,128)S(1)}) custom-call(f32[5,1,1024]{2,1,0:T(1,128)S(1)} %shard_map.68.tile.own, f32[512,512]{1,0:T(8,128)} %gain_in.1), custom_call_target="tpu_custom_call" | custom-call | tf_op jit(solution)/shard_map/pallas_call | solution.py:403
  7.9 0.0 collective-permute-done.1.got_odd
  7.9 0.0 collective-permute-done.got_even
  7.9 0.6 %shard_map.70 = (f32[5,1,1024]{2,1,0:T(1,128)S(1)}, f32[5,1,1024]{2,1,0:T(1,128)S(1)}, bf16[128,1024]{1,0:T(8,128)(2,1)S(1)}, bf16[128,1024]{1,0:T(8,128)(2,1)S(...) custom-call(f32[5,1,1024]{2,1,0:T(1,128)S(1)} %shard_map.68.tile.own, f32[5,1,1024]{2,1,0:T(1,128)S(1)} %collective-permute-done.got_even, ...), custom_call_target="tpu_custom_call" | custom-call | tf_op jit(solution)/shard_map/pallas_call | solution.py:416
  8.5 1.3 %collective-permute-start.2 = (f32[32,384]{1,0:T(8,128)S(1)}, f32[32,384]{1,0:T(8,128)S(1)}, u32[]{:S(2)}, u32[]{:S(2)}) collective-permute-start(f32[32,384]{1,0:T(8,128)S(1)} %get-tuple-element.32), channel_id=1, source_target_pairs={{0,16},{1,17},{2,18},{3,19},{4,20},{5,21},{6,22},{7,23},{8,24},{9,... | collective-permute-start | bytes 147464 | tf_op jit(solution)/shard_map/ppermute | solution.py:377
  9.8 1.3 %collective-permute-start.3 = (f32[32,384]{1,0:T(8,128)S(1)}, f32[32,384]{1,0:T(8,128)S(1)}, u32[]{:S(2)}, u32[]{:S(2)}) collective-permute-start(f32[32,384]{1,0:T(8,128)S(1)} %get-tuple-element.33), channel_id=1, source_target_pairs={{0,1},{1,0},{2,3},{3,2},{4,5},{5,4},{6,7},{7,6},{8,9},{9,8},{10,11... | collective-permute-start | bytes 147464 | tf_op jit(solution)/shard_map/ppermute | solution.py:377
  11.1 1.4 %collective-permute-start.5 = (f32[2,1,1024]{2,1,0:T(1,128)S(1)}, f32[2,1,1024]{2,1,0:T(1,128)S(1)}, u32[]{:S(2)}, u32[]{:S(2)}) collective-permute-start(f32[2,1,1024]{2,1,0:T(1,128)S(1)} %get-tuple-element.34.told), channel_id=1, source_target_pairs={{0,16},{1,2},{2,1},{3,4},{4,3},{5,6},{6,5},{7,8},{8,7},{9,10},{10,... | collective-permute-start | bytes 24584 | tf_op jit(solution)/shard_map/ppermute | solution.py:377
  12.5 0.0 collective-permute-start.4
  12.5 2.1 %shard_map.71 = (bf16[128,1024]{1,0:T(8,128)(2,1)S(1)}, bf16[128,1024]{1,0:T(8,128)(2,1)S(1)}, bf16[3,192,1024]{2,1,0:T(8,128)(2,1)S(1)}, bf16[3,192,1024]{2,1,0...) custom-call(f32[5,1,1024]{2,1,0:T(1,128)S(1)} %shard_map.68.tile.own, ...), custom_call_target="tpu_custom_call" | custom-call | tf_op jit(solution)/shard_map/pallas_call | solution.py:422
  14.6 1.1 %collective-permute-done.5.told_odd = f32[2,1,1024]{2,1,0:T(1,128)S(1)} collective-permute-done((f32[2,1,1024]{2,1,0:T(1,128)S(1)}, f32[2,1,1024]{2,1,0:T(1,128)S(1)}, u32[]{:S(2)}, u32[]{:S(2)}) %collective-permute-start.5) | collective-permute-done | bytes 8224 | tf_op jit(solution)/shard_map/ppermute | solution.py:377
  15.7 0.0 collective-permute-done.4.told_even
  15.7 0.0 collective-permute-done.2.got_even
  15.7 0.0 collective-permute-done.3.got_odd
  15.7 1.3 %shard_map.72 = (f32[3,1,1024]{2,1,0:T(1,128)S(1)}, f32[3,1,1024]{2,1,0:T(1,128)S(1)}, f32[1,1,1024]{2,1,0:T(1,128)S(1)}, f32[32,384]{1,0:T(8,128)S(1)}, f32[32,384]{1,0:T(8,128)S(1)}) custom-call(f32[32,384]{1,0:T(8,128)S(1)} %collective-permute-done.2.got_even, f32[32,384]{1,0:T(8,128)S(1)} %collective-permute-done.3.got_odd, ...), custom_call_target="tpu_custom_call" | custom-call | tf_op jit(solution)/shard_map/pallas_call | solution.py:427
  17.0 1.7 %collective-permute-start.6 = (f32[32,384]{1,0:T(8,128)S(1)}, f32[32,384]{1,0:T(8,128)S(1)}, u32[]{:S(2)}, u32[]{:S(2)}) collective-permute-start(f32[32,384]{1,0:T(8,128)S(1)} %get-tuple-element.48), channel_id=1, source_target_pairs={{0,16},{1,17},{2,18},{3,19},{4,20},{5,21},{6,22},{7,23},{8,24},{9,... | collective-permute-start | bytes 147464 | tf_op jit(solution)/shard_map/ppermute | solution.py:377
  18.7 0.1 collective-permute-start.7
  18.9 1.8 %collective-permute-start.9 = (f32[1,1,1024]{2,1,0:T(1,128)S(1)}, f32[1,1,1024]{2,1,0:T(1,128)S(1)}, u32[]{:S(2)}, u32[]{:S(2)}) collective-permute-start(f32[1,1,1024]{2,1,0:T(1,128)S(1)} %get-tuple-element.50.told), channel_id=1, source_target_pairs={{0,16},{1,2},{2,1},{3,4},{4,3},{5,6},{6,5},{7,8},{8,7},{9,10},{10,... | collective-permute-start | bytes 12296 | tf_op jit(solution)/shard_map/ppermute | solution.py:377
  20.6 0.0 collective-permute-start.8
  20.6 1.3 %shard_map.73.inner = f32[3,1,1024]{2,1,0:T(1,128)S(1)} custom-call(f32[3,1,1024]{2,1,0:T(1,128)S(1)} %get-tuple-element.51.doses, bf16[128,1024]{1,0:T(8,128)(2,1)S(1)} %get-tuple-element.37.px_left, bf16[128,1024]{1,0:T(8,128)(2,1)S(1)} %get-tuple-element.30.px, bf16[128,1024]{1,0:T(8,128)(2,1)S(1)} %get-tuple-element.38.px_right, ...), custom_call_target="tpu_custom_call" | custom-call | tf_op jit(solution)/shard_map/pallas_call | solution.py:434
  21.9 1.5 %collective-permute-done.9.told_odd = f32[1,1,1024]{2,1,0:T(1,128)S(1)} collective-permute-done((f32[1,1,1024]{2,1,0:T(1,128)S(1)}, f32[1,1,1024]{2,1,0:T(1,128)S(1)}, u32[]{:S(2)}, u32[]{:S(2)}) %collective-permute-start.9) | collective-permute-done | bytes 4128 | tf_op jit(solution)/shard_map/ppermute | solution.py:377
  23.4 0.0 collective-permute-done.8.told_even
  23.4 0.0 collective-permute-done.6.got_even
  23.4 0.0 collective-permute-done.7.got_odd
  23.4 1.2 %shard_map.74 = (f32[3,1,1024]{2,1,0:T(1,128)S(1)}, f32[32,256]{1,0:T(8,128)S(1)}, f32[32,256]{1,0:T(8,128)S(1)}) custom-call(f32[32,384]{1,0:T(8,128)S(1)} %collective-permute-done.6.got_even, f32[32,384]{1,0:T(8,128)S(1)} %collective-permute-done.7.got_odd, f32[1,1,1024]{2,1,0:T(1,128)S(1)} %get-tuple-element.50.told, ...), custom_call_target="tpu_custom_call" | custom-call | tf_op jit(solution)/shard_map/pallas_call | solution.py:435
  24.6 1.6 %collective-permute-start.10 = (f32[32,256]{1,0:T(8,128)S(1)}, f32[32,256]{1,0:T(8,128)S(1)}, u32[]{:S(2)}, u32[]{:S(2)}) collective-permute-start(f32[32,256]{1,0:T(8,128)S(1)} %get-tuple-element.53), channel_id=1, source_target_pairs={{0,16},{1,17},{2,18},{3,19},{4,20},{5,21},{6,22},{7,23},{8,24},{9,... | collective-permute-start | bytes 98312 | tf_op jit(solution)/shard_map/ppermute | solution.py:377
  26.2 1.3 %collective-permute-start.11 = (f32[32,256]{1,0:T(8,128)S(1)}, f32[32,256]{1,0:T(8,128)S(1)}, u32[]{:S(2)}, u32[]{:S(2)}) collective-permute-start(f32[32,256]{1,0:T(8,128)S(1)} %get-tuple-element.54), channel_id=1, source_target_pairs={{0,1},{1,0},{2,3},{3,2},{4,5},{5,4},{6,7},{7,6},{8,9},{9,8},{10,11... | collective-permute-start | bytes 98312 | tf_op jit(solution)/shard_map/ppermute | solution.py:377
  27.5 1.0 %shard_map.75 = (f32[1,1024]{1,0:T(1,128)S(1)}, f32[1,1024]{1,0:T(1,128)S(1)}) custom-call(f32[3,1,1024]{2,1,0:T(1,128)S(1)} %get-tuple-element.55.doses, bf16[128,1024]{1,0:T(8,128)(2,1)S(1)} %get-tuple-element.37.px_left, bf16[128,1024]{1,0:T(8,128)(2,1)S(1)} %get-tuple-element.30.px, bf16[128,1024]{1,0:T(8,128)(2,1)S(1)} %get-tuple-element.38.px_right, ...), custom_call_target="tpu_custom_call" | custom-call | tf_op jit(solution)/shard_map/pallas_call | solution.py:440
  28.5 0.0 collective-permute-done.10.got_even
  28.5 1.3 %collective-permute-done.11.got_odd = f32[32,256]{1,0:T(8,128)S(1)} collective-permute-done((f32[32,256]{1,0:T(8,128)S(1)}, f32[32,256]{1,0:T(8,128)S(1)}, u32[]{:S(2)}, u32[]{:S(2)}) %collective-permute-start.11) | collective-permute-done | bytes 32800 | tf_op jit(solution)/shard_map/ppermute | solution.py:377
  29.8 1.1 %shard_map.76 = (f32[1,1024]{1,0:T(1,128)}, f32[1,1024]{1,0:T(1,128)}) custom-call(f32[32,256]{1,0:T(8,128)S(1)} %collective-permute-done.10.got_even, f32[32,256]{1,0:T(8,128)S(1)} %collective-permute-done.11.got_odd, f32[3,1,1024]{2,1,0:T(1,128)S(1)} %get-tuple-element.55.doses, f32[3,1,1024]{2,1,0:T(1,128)S(1)} %get-tuple-element.52.sens, ...), custom_call_target="tpu_custom_call" | custom-call | tf_op jit(solution)/shard_map/pallas_call | solution.py:441
Async XLA Ops:
  1.5 6.4 %collective-permute-start.1 = (f32[5,1,1024]{2,1,0:T(1,128)S(1)}, f32[5,1,1024]{2,1,0:T(1,128)S(1)}, u32[]{:S(2)}, u32[]{:S(2)}) collective-permute-start(f32[5,1,1024]{2,1,0:T(1,128)S(1)} %shard_map.68.tile.own), channel_id=1, source_target_pairs={{0,16},{1,2},{2,1},{3,4},{4,3},{5,6},{6,5},{7,8},{8,7},{9,10},{10,... | collective-permute-start | bytes 61448 | tf_op jit(solution)/shard_map/ppermute | solution.py:377
  3.9 4.0 %collective-permute-start = (f32[5,1,1024]{2,1,0:T(1,128)S(1)}, f32[5,1,1024]{2,1,0:T(1,128)S(1)}, u32[]{:S(2)}, u32[]{:S(2)}) collective-permute-start(f32[5,1,1024]{2,1,0:T(1,128)S(1)} %shard_map.68.tile.own), channel_id=1, source_target_pairs={{0,1},{1,0},{2,3},{3,2},{4,5},{5,4},{6,7},{7,6},{8,9},{9,8},{10,11... | collective-permute-start | bytes 61448 | tf_op jit(solution)/shard_map/ppermute | solution.py:377
  8.5 7.2 %collective-permute-start.2 = (f32[32,384]{1,0:T(8,128)S(1)}, f32[32,384]{1,0:T(8,128)S(1)}, u32[]{:S(2)}, u32[]{:S(2)}) collective-permute-start(f32[32,384]{1,0:T(8,128)S(1)} %get-tuple-element.32), channel_id=1, source_target_pairs={{0,16},{1,17},{2,18},{3,19},{4,20},{5,21},{6,22},{7,23},{8,24},{9,... | collective-permute-start | bytes 147464 | tf_op jit(solution)/shard_map/ppermute | solution.py:377
  9.8 5.9 %collective-permute-start.3 = (f32[32,384]{1,0:T(8,128)S(1)}, f32[32,384]{1,0:T(8,128)S(1)}, u32[]{:S(2)}, u32[]{:S(2)}) collective-permute-start(f32[32,384]{1,0:T(8,128)S(1)} %get-tuple-element.33), channel_id=1, source_target_pairs={{0,1},{1,0},{2,3},{3,2},{4,5},{5,4},{6,7},{7,6},{8,9},{9,8},{10,11... | collective-permute-start | bytes 147464 | tf_op jit(solution)/shard_map/ppermute | solution.py:377
  11.1 4.6 %collective-permute-start.5 = (f32[2,1,1024]{2,1,0:T(1,128)S(1)}, f32[2,1,1024]{2,1,0:T(1,128)S(1)}, u32[]{:S(2)}, u32[]{:S(2)}) collective-permute-start(f32[2,1,1024]{2,1,0:T(1,128)S(1)} %get-tuple-element.34.told), channel_id=1, source_target_pairs={{0,16},{1,2},{2,1},{3,4},{4,3},{5,6},{6,5},{7,8},{8,7},{9,10},{10,... | collective-permute-start | bytes 24584 | tf_op jit(solution)/shard_map/ppermute | solution.py:377
  12.5 3.2 %collective-permute-start.4 = (f32[2,1,1024]{2,1,0:T(1,128)S(1)}, f32[2,1,1024]{2,1,0:T(1,128)S(1)}, u32[]{:S(2)}, u32[]{:S(2)}) collective-permute-start(f32[2,1,1024]{2,1,0:T(1,128)S(1)} %get-tuple-element.34.told), channel_id=1, source_target_pairs={{0,1},{1,0},{2,3},{3,2},{4,5},{5,4},{6,7},{7,6},{8,9},{9,8},{10,11... | collective-permute-start | bytes 24584 | tf_op jit(solution)/shard_map/ppermute | solution.py:377
  17.0 6.4 %collective-permute-start.6 = (f32[32,384]{1,0:T(8,128)S(1)}, f32[32,384]{1,0:T(8,128)S(1)}, u32[]{:S(2)}, u32[]{:S(2)}) collective-permute-start(f32[32,384]{1,0:T(8,128)S(1)} %get-tuple-element.48), channel_id=1, source_target_pairs={{0,16},{1,17},{2,18},{3,19},{4,20},{5,21},{6,22},{7,23},{8,24},{9,... | collective-permute-start | bytes 147464 | tf_op jit(solution)/shard_map/ppermute | solution.py:377
  18.7 4.7 %collective-permute-start.7 = (f32[32,384]{1,0:T(8,128)S(1)}, f32[32,384]{1,0:T(8,128)S(1)}, u32[]{:S(2)}, u32[]{:S(2)}) collective-permute-start(f32[32,384]{1,0:T(8,128)S(1)} %get-tuple-element.49), channel_id=1, source_target_pairs={{0,1},{1,0},{2,3},{3,2},{4,5},{5,4},{6,7},{7,6},{8,9},{9,8},{10,11... | collective-permute-start | bytes 147464 | tf_op jit(solution)/shard_map/ppermute | solution.py:377
  18.9 4.6 %collective-permute-start.9 = (f32[1,1,1024]{2,1,0:T(1,128)S(1)}, f32[1,1,1024]{2,1,0:T(1,128)S(1)}, u32[]{:S(2)}, u32[]{:S(2)}) collective-permute-start(f32[1,1,1024]{2,1,0:T(1,128)S(1)} %get-tuple-element.50.told), channel_id=1, source_target_pairs={{0,16},{1,2},{2,1},{3,4},{4,3},{5,6},{6,5},{7,8},{8,7},{9,10},{10,... | collective-permute-start | bytes 12296 | tf_op jit(solution)/shard_map/ppermute | solution.py:377
  20.6 2.8 %collective-permute-start.8 = (f32[1,1,1024]{2,1,0:T(1,128)S(1)}, f32[1,1,1024]{2,1,0:T(1,128)S(1)}, u32[]{:S(2)}, u32[]{:S(2)}) collective-permute-start(f32[1,1,1024]{2,1,0:T(1,128)S(1)} %get-tuple-element.50.told), channel_id=1, source_target_pairs={{0,1},{1,0},{2,3},{3,2},{4,5},{5,4},{6,7},{7,6},{8,9},{9,8},{10,11... | collective-permute-start | bytes 12296 | tf_op jit(solution)/shard_map/ppermute | solution.py:377
  24.6 3.9 %collective-permute-start.10 = (f32[32,256]{1,0:T(8,128)S(1)}, f32[32,256]{1,0:T(8,128)S(1)}, u32[]{:S(2)}, u32[]{:S(2)}) collective-permute-start(f32[32,256]{1,0:T(8,128)S(1)} %get-tuple-element.53), channel_id=1, source_target_pairs={{0,16},{1,17},{2,18},{3,19},{4,20},{5,21},{6,22},{7,23},{8,24},{9,... | collective-permute-start | bytes 98312 | tf_op jit(solution)/shard_map/ppermute | solution.py:377
  26.2 3.6 %collective-permute-start.11 = (f32[32,256]{1,0:T(8,128)S(1)}, f32[32,256]{1,0:T(8,128)S(1)}, u32[]{:S(2)}, u32[]{:S(2)}) collective-permute-start(f32[32,256]{1,0:T(8,128)S(1)} %get-tuple-element.54), channel_id=1, source_target_pairs={{0,1},{1,0},{2,3},{3,2},{4,5},{5,4},{6,7},{7,6},{8,9},{9,8},{10,11... | collective-permute-start | bytes 98312 | tf_op jit(solution)/shard_map/ppermute | solution.py:377

commit v6 on v5

--- a/solution.py
+++ b/solution.py
@@ -27,6 +27,7 @@
 MAXB = 8
 SIDE = CG + REACH
 ALL = CG + 2 * REACH
+MARGINS = (3 * REACH + 2 * 8, 2 * REACH + 8)
 
 
 def pairings():
@@ -221,19 +222,24 @@
     send_rows(jnp.concatenate(edges, axis=1), send_even, send_odd)
 
 
-def per_tile(left, own, right):
+def per_tile(left, own, right, margin):
     return (
-        jnp.concatenate([left, own[:REACH]], axis=0),
+        jnp.concatenate([left[CG - margin :], own[:REACH]], axis=0),
         jnp.concatenate([own, left[CG - REACH :], right[:REACH]], axis=0),
-        jnp.concatenate([right, own[CG - REACH :]], axis=0),
-    )
-
-
-def inner_sums(doses, px, py, wy_high, wy_low, wx, inner):
+        jnp.concatenate([right[:margin], own[CG - REACH :]], axis=0),
+    )
+
+
+def weights_along(wx, margin):
+    left, own, right = wx
+    return left[CG - margin :, :], own[...], jnp.concatenate([right[:margin, :], right[CG:, :]], axis=0)
+
+
+def inner_sums(doses, px, py, wy_high, wy_low, wx, inner, margin):
     coarse = [stacked_dot(across.astype(F32) * dose, down, NT) for dose, across, down in zip(doses, px, py)]
-    for k, columns in enumerate(per_tile(*coarse)):
+    for k, (columns, along) in enumerate(zip(per_tile(*coarse, margin), weights_along(wx, margin))):
         across = weighted(columns, wy_high[k, :CG, :], wy_low[k, :CG, :])
-        inner[k] = jnp.sum(across * wx[k][...], axis=0, keepdims=True)
+        inner[k] = jnp.sum(across * along, axis=0, keepdims=True)
 
 
 def late_kernel(own, left, right, px_left, px, px_right, py, py_left, py_right, wy_high, wy_low, wx_left, wx, wx_right, inner):
@@ -260,6 +266,7 @@
         wy_low,
         (wx_left, wx, wx_right),
         inner,
+        MARGINS[0],
     )
 
 
@@ -272,6 +279,7 @@
         wy_low,
         (wx_left, wx, wx_right),
         inner,
+        MARGINS[1],
     )
 
 
@@ -303,13 +311,13 @@
     return jnp.where(live, dose * TARGET_LEVEL / jnp.where(live, exposure, 1.0), 0.0), jnp.where(live, exposure, 0.0)
 
 
-def new_doses(got_even, got_odd, doses, sens, forward, inner, wy_high, wy_low, wx):
+def new_doses(got_even, got_odd, doses, sens, forward, inner, wy_high, wy_low, wx, margin):
     outer = outer_rows(got_even[...], got_odd[...])
     outer_t = [jnp.transpose(outer[:, k * CG : (k + 1) * CG]) for k in range(3)]
     result = []
-    for k, columns in enumerate(per_tile(*outer_t)):
+    for k, (columns, along) in enumerate(zip(per_tile(*outer_t, margin), weights_along(wx, margin))):
         across = weighted(columns, wy_high[k, CG:, :], wy_low[k, CG:, :])
-        background = inner[k] + jnp.sum(across * wx[k][...], axis=0, keepdims=True)
+        background = inner[k] + jnp.sum(across * along, axis=0, keepdims=True)
         result.append(exposed(doses[k], sens[k], forward[k], background)[0])
     return result
 
@@ -320,7 +328,7 @@
 ):
     told_left, told_right = sides(told_even[...], told_odd[...])
     forward, sens = zip((told_left[0], told_left[1]), (told[0], told[1]), (told_right[0], told_right[1]))
-    doses = new_doses(got_even, got_odd, (left[4], own[4], right[4]), sens, forward, inner, wy_high, wy_low, (wx_left, wx, wx_right))
+    doses = new_doses(got_even, got_odd, (left[4], own[4], right[4]), sens, forward, inner, wy_high, wy_low, (wx_left, wx, wx_right), MARGINS[0])
     for k in range(3):
         sens_out[k] = sens[k]
         doses_out[k] = doses[k]
@@ -336,7 +344,7 @@
     before = [doses[k] for k in range(3)]
     factors = [sens[k] for k in range(3)]
     forward = (told_left[0], told[0], told_right[0])
-    after = new_doses(got_even, got_odd, before, factors, forward, inner, wy_high, wy_low, (wx_left, wx, wx_right))
+    after = new_doses(got_even, got_odd, before, factors, forward, inner, wy_high, wy_low, (wx_left, wx, wx_right), MARGINS[1])
     for k in range(3):
         doses_out[k] = after[k]
     last_strips(after, (px_left, px, px_right), (py_left, py, py_right), send_even, send_odd)

time: 31.1 us -> 30.9 us (level)
  transfers between devices with their start and end apart: 12 -> 12, of which waited for: 3 -> 3; matrix products, arithmetic and copies ran while one was open for 0% -> 0% of each run, Pallas kernels for 27% -> 26%
where the time goes in v6:
time: 30.9 us; the launch traced here: 30.7 us
  Pallas kernels  13 us (42%)
  starting transfers between devices  13 us (42%)
  waiting for transfers between devices  4.07 us (13%)
  between operations  0.72 us (2%)
    ppermute x12, starting transfers between devices, send(): return lax.ppermute(value, AXES, table)  13 us
    ppermute x12, waiting for transfers between devices, send(): return lax.ppermute(value, AXES, table)  4.07 us
    pallas_call x1, Pallas kernels, body(): call(early_kernel, (cover, cover, shape(SLOTS, SLOTS), shape(2, 1, SLOTS)...  3.84 us
    pallas_call x1, Pallas kernels, body(): call(late_kernel, (cover, cover, weights, weights, shape(SIDE, SLOTS), sh...  2.14 us
    pallas_call x1, Pallas kernels, body(): call(first_update_kernel, (rows, rows, shape(1, 1, SLOTS), strip, strip))  1.28 us
    pallas_call x1, Pallas kernels, body(): inner = call(inner_kernel, rows)(doses3, *covers, *weighing)  1.17 us
    pallas_call x1, Pallas kernels, body(): call(final_kernel, (row, row))  1.09 us
    pallas_call x1, Pallas kernels, body(): call(last_inner_kernel, (row, row))  0.96 us
  transfers between devices with their start and end apart: 12, of which 3 were waited for; matrix products, arithmetic and copies ran while one was open for 0% of the time, Pallas kernels for 26%

profile of v6, /device:TPU:97, one launch (start us, length us, event | category | flops | bytes accessed | tf_op | source)
XLA Modules:
  0.0 30.7 jit_solution(8654502498293842314)
XLA Ops:
  0.6 0.9 %shard_map.68.tile.own = f32[5,1,1024]{2,1,0:T(1,128)S(1)} custom-call(s32[4,1,1024]{2,1,0:T(1,128)} %boxes_in.1, s32[1,16]{1,0:T(1,128)} %counts_in.1, s32[1,16]{1,0:T(1,128)} %tails_in.1, f32[1,1024]{1,0:T(1,128)} %doses_in.1), custom_call_target="tpu_custom_call" | custom-call | tf_op jit(solution)/shard_map/pallas_call | solution.py:397
  1.5 2.4 %collective-permute-start.1 = (f32[5,1,1024]{2,1,0:T(1,128)S(1)}, f32[5,1,1024]{2,1,0:T(1,128)S(1)}, u32[]{:S(2)}, u32[]{:S(2)}) collective-permute-start(f32[5,1,1024]{2,1,0:T(1,128)S(1)} %shard_map.68.tile.own), channel_id=1, source_target_pairs={{0,16},{1,2},{2,1},{3,4},{4,3},{5,6},{6,5},{7,8},{8,7},{9,10},{10,... | collective-permute-start | bytes 61448 | tf_op jit(solution)/shard_map/ppermute | solution.py:385
  3.9 0.1 collective-permute-start
  4.0 3.8 %shard_map.69 = (bf16[128,1024]{1,0:T(8,128)(2,1)S(1)}, bf16[128,1024]{1,0:T(8,128)(2,1)S(1)}, f32[1024,1024]{1,0:T(8,128)S(1)}, f32[2,1,1024]{2,1,0:T(1,128)S(1)}) custom-call(f32[5,1,1024]{2,1,0:T(1,128)S(1)} %shard_map.68.tile.own, f32[512,512]{1,0:T(8,128)} %gain_in.1), custom_call_target="tpu_custom_call" | custom-call | tf_op jit(solution)/shard_map/pallas_call | solution.py:411
  7.9 0.0 collective-permute-done.1.got_odd
  7.9 0.0 collective-permute-done.got_even
  7.9 0.6 %shard_map.70 = (f32[5,1,1024]{2,1,0:T(1,128)S(1)}, f32[5,1,1024]{2,1,0:T(1,128)S(1)}, bf16[128,1024]{1,0:T(8,128)(2,1)S(1)}, bf16[128,1024]{1,0:T(8,128)(2,1)S(...) custom-call(f32[5,1,1024]{2,1,0:T(1,128)S(1)} %shard_map.68.tile.own, f32[5,1,1024]{2,1,0:T(1,128)S(1)} %collective-permute-done.got_even, ...), custom_call_target="tpu_custom_call" | custom-call | tf_op jit(solution)/shard_map/pallas_call | solution.py:424
  8.5 1.3 %collective-permute-start.2 = (f32[32,384]{1,0:T(8,128)S(1)}, f32[32,384]{1,0:T(8,128)S(1)}, u32[]{:S(2)}, u32[]{:S(2)}) collective-permute-start(f32[32,384]{1,0:T(8,128)S(1)} %get-tuple-element.32), channel_id=1, source_target_pairs={{0,16},{1,17},{2,18},{3,19},{4,20},{5,21},{6,22},{7,23},{8,24},{9,... | collective-permute-start | bytes 147464 | tf_op jit(solution)/shard_map/ppermute | solution.py:385
  9.8 1.3 %collective-permute-start.3 = (f32[32,384]{1,0:T(8,128)S(1)}, f32[32,384]{1,0:T(8,128)S(1)}, u32[]{:S(2)}, u32[]{:S(2)}) collective-permute-start(f32[32,384]{1,0:T(8,128)S(1)} %get-tuple-element.33), channel_id=1, source_target_pairs={{0,1},{1,0},{2,3},{3,2},{4,5},{5,4},{6,7},{7,6},{8,9},{9,8},{10,11... | collective-permute-start | bytes 147464 | tf_op jit(solution)/shard_map/ppermute | solution.py:385
  11.1 1.4 %collective-permute-start.5 = (f32[2,1,1024]{2,1,0:T(1,128)S(1)}, f32[2,1,1024]{2,1,0:T(1,128)S(1)}, u32[]{:S(2)}, u32[]{:S(2)}) collective-permute-start(f32[2,1,1024]{2,1,0:T(1,128)S(1)} %get-tuple-element.34.told), channel_id=1, source_target_pairs={{0,16},{1,2},{2,1},{3,4},{4,3},{5,6},{6,5},{7,8},{8,7},{9,10},{10,... | collective-permute-start | bytes 24584 | tf_op jit(solution)/shard_map/ppermute | solution.py:385
  12.5 0.0 collective-permute-start.4
  12.5 2.1 %shard_map.71 = (bf16[128,1024]{1,0:T(8,128)(2,1)S(1)}, bf16[128,1024]{1,0:T(8,128)(2,1)S(1)}, bf16[3,192,1024]{2,1,0:T(8,128)(2,1)S(1)}, bf16[3,192,1024]{2,1,0...) custom-call(f32[5,1,1024]{2,1,0:T(1,128)S(1)} %shard_map.68.tile.own, ...), custom_call_target="tpu_custom_call" | custom-call | tf_op jit(solution)/shard_map/pallas_call | solution.py:430
  14.6 1.1 %collective-permute-done.5.told_odd = f32[2,1,1024]{2,1,0:T(1,128)S(1)} collective-permute-done((f32[2,1,1024]{2,1,0:T(1,128)S(1)}, f32[2,1,1024]{2,1,0:T(1,128)S(1)}, u32[]{:S(2)}, u32[]{:S(2)}) %collective-permute-start.5) | collective-permute-done | bytes 8224 | tf_op jit(solution)/shard_map/ppermute | solution.py:385
  15.7 0.0 collective-permute-done.4.told_even
  15.7 0.0 collective-permute-done.2.got_even
  15.7 0.0 collective-permute-done.3.got_odd
  15.7 1.3 %shard_map.72 = (f32[3,1,1024]{2,1,0:T(1,128)S(1)}, f32[3,1,1024]{2,1,0:T(1,128)S(1)}, f32[1,1,1024]{2,1,0:T(1,128)S(1)}, f32[32,384]{1,0:T(8,128)S(1)}, f32[32,384]{1,0:T(8,128)S(1)}) custom-call(f32[32,384]{1,0:T(8,128)S(1)} %collective-permute-done.2.got_even, f32[32,384]{1,0:T(8,128)S(1)} %collective-permute-done.3.got_odd, ...), custom_call_target="tpu_custom_call" | custom-call | tf_op jit(solution)/shard_map/pallas_call | solution.py:435
  17.0 1.7 %collective-permute-start.6 = (f32[32,384]{1,0:T(8,128)S(1)}, f32[32,384]{1,0:T(8,128)S(1)}, u32[]{:S(2)}, u32[]{:S(2)}) collective-permute-start(f32[32,384]{1,0:T(8,128)S(1)} %get-tuple-element.48), channel_id=1, source_target_pairs={{0,16},{1,17},{2,18},{3,19},{4,20},{5,21},{6,22},{7,23},{8,24},{9,... | collective-permute-start | bytes 147464 | tf_op jit(solution)/shard_map/ppermute | solution.py:385
  18.7 0.1 collective-permute-start.7
  18.8 1.8 %collective-permute-start.9 = (f32[1,1,1024]{2,1,0:T(1,128)S(1)}, f32[1,1,1024]{2,1,0:T(1,128)S(1)}, u32[]{:S(2)}, u32[]{:S(2)}) collective-permute-start(f32[1,1,1024]{2,1,0:T(1,128)S(1)} %get-tuple-element.50.told), channel_id=1, source_target_pairs={{0,16},{1,2},{2,1},{3,4},{4,3},{5,6},{6,5},{7,8},{8,7},{9,10},{10,... | collective-permute-start | bytes 12296 | tf_op jit(solution)/shard_map/ppermute | solution.py:385
  20.6 0.0 collective-permute-start.8
  20.6 1.2 %shard_map.73.inner = f32[3,1,1024]{2,1,0:T(1,128)S(1)} custom-call(f32[3,1,1024]{2,1,0:T(1,128)S(1)} %get-tuple-element.51.doses, bf16[128,1024]{1,0:T(8,128)(2,1)S(1)} %get-tuple-element.37.px_left, bf16[128,1024]{1,0:T(8,128)(2,1)S(1)} %get-tuple-element.30.px, bf16[128,1024]{1,0:T(8,128)(2,1)S(1)} %get-tuple-element.38.px_right, ...), custom_call_target="tpu_custom_call" | custom-call | tf_op jit(solution)/shard_map/pallas_call | solution.py:442
  21.8 1.6 %collective-permute-done.9.told_odd = f32[1,1,1024]{2,1,0:T(1,128)S(1)} collective-permute-done((f32[1,1,1024]{2,1,0:T(1,128)S(1)}, f32[1,1,1024]{2,1,0:T(1,128)S(1)}, u32[]{:S(2)}, u32[]{:S(2)}) %collective-permute-start.9) | collective-permute-done | bytes 4128 | tf_op jit(solution)/shard_map/ppermute | solution.py:385
  23.4 0.0 collective-permute-done.8.told_even
  23.4 0.0 collective-permute-done.6.got_even
  23.4 0.0 collective-permute-done.7.got_odd
  23.4 1.0 %shard_map.74 = (f32[3,1,1024]{2,1,0:T(1,128)S(1)}, f32[32,256]{1,0:T(8,128)S(1)}, f32[32,256]{1,0:T(8,128)S(1)}) custom-call(f32[32,384]{1,0:T(8,128)S(1)} %collective-permute-done.6.got_even, f32[32,384]{1,0:T(8,128)S(1)} %collective-permute-done.7.got_odd, f32[1,1,1024]{2,1,0:T(1,128)S(1)} %get-tuple-element.50.told, ...), custom_call_target="tpu_custom_call" | custom-call | tf_op jit(solution)/shard_map/pallas_call | solution.py:443
  24.4 1.6 %collective-permute-start.10 = (f32[32,256]{1,0:T(8,128)S(1)}, f32[32,256]{1,0:T(8,128)S(1)}, u32[]{:S(2)}, u32[]{:S(2)}) collective-permute-start(f32[32,256]{1,0:T(8,128)S(1)} %get-tuple-element.53), channel_id=1, source_target_pairs={{0,16},{1,17},{2,18},{3,19},{4,20},{5,21},{6,22},{7,23},{8,24},{9,... | collective-permute-start | bytes 98312 | tf_op jit(solution)/shard_map/ppermute | solution.py:385
  26.0 1.3 %collective-permute-start.11 = (f32[32,256]{1,0:T(8,128)S(1)}, f32[32,256]{1,0:T(8,128)S(1)}, u32[]{:S(2)}, u32[]{:S(2)}) collective-permute-start(f32[32,256]{1,0:T(8,128)S(1)} %get-tuple-element.54), channel_id=1, source_target_pairs={{0,1},{1,0},{2,3},{3,2},{4,5},{5,4},{6,7},{7,6},{8,9},{9,8},{10,11... | collective-permute-start | bytes 98312 | tf_op jit(solution)/shard_map/ppermute | solution.py:385
  27.3 1.0 %shard_map.75 = (f32[1,1024]{1,0:T(1,128)S(1)}, f32[1,1024]{1,0:T(1,128)S(1)}) custom-call(f32[3,1,1024]{2,1,0:T(1,128)S(1)} %get-tuple-element.55.doses, bf16[128,1024]{1,0:T(8,128)(2,1)S(1)} %get-tuple-element.37.px_left, bf16[128,1024]{1,0:T(8,128)(2,1)S(1)} %get-tuple-element.30.px, bf16[128,1024]{1,0:T(8,128)(2,1)S(1)} %get-tuple-element.38.px_right, ...), custom_call_target="tpu_custom_call" | custom-call | tf_op jit(solution)/shard_map/pallas_call | solution.py:448
  28.3 0.0 collective-permute-done.10.got_even
  28.3 1.3 %collective-permute-done.11.got_odd = f32[32,256]{1,0:T(8,128)S(1)} collective-permute-done((f32[32,256]{1,0:T(8,128)S(1)}, f32[32,256]{1,0:T(8,128)S(1)}, u32[]{:S(2)}, u32[]{:S(2)}) %collective-permute-start.11) | collective-permute-done | bytes 32800 | tf_op jit(solution)/shard_map/ppermute | solution.py:385
  29.6 1.1 %shard_map.76 = (f32[1,1024]{1,0:T(1,128)}, f32[1,1024]{1,0:T(1,128)}) custom-call(f32[32,256]{1,0:T(8,128)S(1)} %collective-permute-done.10.got_even, f32[32,256]{1,0:T(8,128)S(1)} %collective-permute-done.11.got_odd, f32[3,1,1024]{2,1,0:T(1,128)S(1)} %get-tuple-element.55.doses, f32[3,1,1024]{2,1,0:T(1,128)S(1)} %get-tuple-element.52.sens, ...), custom_call_target="tpu_custom_call" | custom-call | tf_op jit(solution)/shard_map/pallas_call | solution.py:449
Async XLA Ops:
  1.5 6.4 %collective-permute-start.1 = (f32[5,1,1024]{2,1,0:T(1,128)S(1)}, f32[5,1,1024]{2,1,0:T(1,128)S(1)}, u32[]{:S(2)}, u32[]{:S(2)}) collective-permute-start(f32[5,1,1024]{2,1,0:T(1,128)S(1)} %shard_map.68.tile.own), channel_id=1, source_target_pairs={{0,16},{1,2},{2,1},{3,4},{4,3},{5,6},{6,5},{7,8},{8,7},{9,10},{10,... | collective-permute-start | bytes 61448 | tf_op jit(solution)/shard_map/ppermute | solution.py:385
  3.9 4.0 %collective-permute-start = (f32[5,1,1024]{2,1,0:T(1,128)S(1)}, f32[5,1,1024]{2,1,0:T(1,128)S(1)}, u32[]{:S(2)}, u32[]{:S(2)}) collective-permute-start(f32[5,1,1024]{2,1,0:T(1,128)S(1)} %shard_map.68.tile.own), channel_id=1, source_target_pairs={{0,1},{1,0},{2,3},{3,2},{4,5},{5,4},{6,7},{7,6},{8,9},{9,8},{10,11... | collective-permute-start | bytes 61448 | tf_op jit(solution)/shard_map/ppermute | solution.py:385
  8.5 7.2 %collective-permute-start.2 = (f32[32,384]{1,0:T(8,128)S(1)}, f32[32,384]{1,0:T(8,128)S(1)}, u32[]{:S(2)}, u32[]{:S(2)}) collective-permute-start(f32[32,384]{1,0:T(8,128)S(1)} %get-tuple-element.32), channel_id=1, source_target_pairs={{0,16},{1,17},{2,18},{3,19},{4,20},{5,21},{6,22},{7,23},{8,24},{9,... | collective-permute-start | bytes 147464 | tf_op jit(solution)/shard_map/ppermute | solution.py:385
  9.8 5.9 %collective-permute-start.3 = (f32[32,384]{1,0:T(8,128)S(1)}, f32[32,384]{1,0:T(8,128)S(1)}, u32[]{:S(2)}, u32[]{:S(2)}) collective-permute-start(f32[32,384]{1,0:T(8,128)S(1)} %get-tuple-element.33), channel_id=1, source_target_pairs={{0,1},{1,0},{2,3},{3,2},{4,5},{5,4},{6,7},{7,6},{8,9},{9,8},{10,11... | collective-permute-start | bytes 147464 | tf_op jit(solution)/shard_map/ppermute | solution.py:385
  11.1 4.6 %collective-permute-start.5 = (f32[2,1,1024]{2,1,0:T(1,128)S(1)}, f32[2,1,1024]{2,1,0:T(1,128)S(1)}, u32[]{:S(2)}, u32[]{:S(2)}) collective-permute-start(f32[2,1,1024]{2,1,0:T(1,128)S(1)} %get-tuple-element.34.told), channel_id=1, source_target_pairs={{0,16},{1,2},{2,1},{3,4},{4,3},{5,6},{6,5},{7,8},{8,7},{9,10},{10,... | collective-permute-start | bytes 24584 | tf_op jit(solution)/shard_map/ppermute | solution.py:385
  12.5 3.2 %collective-permute-start.4 = (f32[2,1,1024]{2,1,0:T(1,128)S(1)}, f32[2,1,1024]{2,1,0:T(1,128)S(1)}, u32[]{:S(2)}, u32[]{:S(2)}) collective-permute-start(f32[2,1,1024]{2,1,0:T(1,128)S(1)} %get-tuple-element.34.told), channel_id=1, source_target_pairs={{0,1},{1,0},{2,3},{3,2},{4,5},{5,4},{6,7},{7,6},{8,9},{9,8},{10,11... | collective-permute-start | bytes 24584 | tf_op jit(solution)/shard_map/ppermute | solution.py:385
  17.0 6.4 %collective-permute-start.6 = (f32[32,384]{1,0:T(8,128)S(1)}, f32[32,384]{1,0:T(8,128)S(1)}, u32[]{:S(2)}, u32[]{:S(2)}) collective-permute-start(f32[32,384]{1,0:T(8,128)S(1)} %get-tuple-element.48), channel_id=1, source_target_pairs={{0,16},{1,17},{2,18},{3,19},{4,20},{5,21},{6,22},{7,23},{8,24},{9,... | collective-permute-start | bytes 147464 | tf_op jit(solution)/shard_map/ppermute | solution.py:385
  18.7 4.7 %collective-permute-start.7 = (f32[32,384]{1,0:T(8,128)S(1)}, f32[32,384]{1,0:T(8,128)S(1)}, u32[]{:S(2)}, u32[]{:S(2)}) collective-permute-start(f32[32,384]{1,0:T(8,128)S(1)} %get-tuple-element.49), channel_id=1, source_target_pairs={{0,1},{1,0},{2,3},{3,2},{4,5},{5,4},{6,7},{7,6},{8,9},{9,8},{10,11... | collective-permute-start | bytes 147464 | tf_op jit(solution)/shard_map/ppermute | solution.py:385
  18.8 4.6 %collective-permute-start.9 = (f32[1,1,1024]{2,1,0:T(1,128)S(1)}, f32[1,1,1024]{2,1,0:T(1,128)S(1)}, u32[]{:S(2)}, u32[]{:S(2)}) collective-permute-start(f32[1,1,1024]{2,1,0:T(1,128)S(1)} %get-tuple-element.50.told), channel_id=1, source_target_pairs={{0,16},{1,2},{2,1},{3,4},{4,3},{5,6},{6,5},{7,8},{8,7},{9,10},{10,... | collective-permute-start | bytes 12296 | tf_op jit(solution)/shard_map/ppermute | solution.py:385
  20.6 2.8 %collective-permute-start.8 = (f32[1,1,1024]{2,1,0:T(1,128)S(1)}, f32[1,1,1024]{2,1,0:T(1,128)S(1)}, u32[]{:S(2)}, u32[]{:S(2)}) collective-permute-start(f32[1,1,1024]{2,1,0:T(1,128)S(1)} %get-tuple-element.50.told), channel_id=1, source_target_pairs={{0,1},{1,0},{2,3},{3,2},{4,5},{5,4},{6,7},{7,6},{8,9},{9,8},{10,11... | collective-permute-start | bytes 12296 | tf_op jit(solution)/shard_map/ppermute | solution.py:385
  24.4 3.9 %collective-permute-start.10 = (f32[32,256]{1,0:T(8,128)S(1)}, f32[32,256]{1,0:T(8,128)S(1)}, u32[]{:S(2)}, u32[]{:S(2)}) collective-permute-start(f32[32,256]{1,0:T(8,128)S(1)} %get-tuple-element.53), channel_id=1, source_target_pairs={{0,16},{1,17},{2,18},{3,19},{4,20},{5,21},{6,22},{7,23},{8,24},{9,... | collective-permute-start | bytes 98312 | tf_op jit(solution)/shard_map/ppermute | solution.py:385
  26.0 3.6 %collective-permute-start.11 = (f32[32,256]{1,0:T(8,128)S(1)}, f32[32,256]{1,0:T(8,128)S(1)}, u32[]{:S(2)}, u32[]{:S(2)}) collective-permute-start(f32[32,256]{1,0:T(8,128)S(1)} %get-tuple-element.54), channel_id=1, source_target_pairs={{0,1},{1,0},{2,3},{3,2},{4,5},{5,4},{6,7},{7,6},{8,9},{9,8},{10,11... | collective-permute-start | bytes 98312 | tf_op jit(solution)/shard_map/ppermute | solution.py:385

commit v7 on v6

--- a/solution.py
+++ b/solution.py
@@ -350,12 +350,35 @@
     last_strips(after, (px_left, px, px_right), (py_left, py, py_right), send_even, send_odd)
 
 
-def final_kernel(got_even, got_odd, doses, sens, inner, forward, wy_high, wy_low, wx, dose_out, exposure_out):
+def last_result(got_even, got_odd, doses, sens, inner, forward, wy_high, wy_low, wx, results):
+    dose_out, exposure_out, dose, exposure, sent = results
     outer = outer_rows(got_even[...], got_odd[...])
     columns = jnp.concatenate([jnp.transpose(outer[:, :CG]), jnp.transpose(outer[:, CG:])[: 2 * REACH]], axis=0)
     across = weighted(columns, wy_high[1, CG:, :], wy_low[1, CG:, :])
     background = inner[...] + jnp.sum(across * wx[...], axis=0, keepdims=True)
-    dose_out[...], exposure_out[...] = exposed(doses[1], sens[1], forward[...], background)
+    dose[...], exposure[...] = exposed(doses[1], sens[1], forward[...], background)
+    copies = [pltpu.make_async_copy(dose, dose_out, sent.at[0]), pltpu.make_async_copy(exposure, exposure_out, sent.at[1])]
+    for copy in copies:
+        copy.start()
+    for copy in copies:
+        copy.wait()
+
+
+def at_window_edge():
+    row = lax.axis_index("row")
+    return (row == 0) | (row == NTR - 1)
+
+
+def edge_kernel(got_even, doses, sens, inner, forward, wy_high, wy_low, wx, *results):
+    @pl.when(at_window_edge())
+    def _():
+        last_result(got_even, got_even, doses, sens, inner, forward, wy_high, wy_low, wx, results)
+
+
+def final_kernel(got_even, got_odd, doses, sens, inner, forward, wy_high, wy_low, wx, edge_dose, edge_exposure, *results):
+    @pl.when(jnp.logical_not(at_window_edge()))
+    def _():
+        last_result(got_even, got_odd, doses, sens, inner, forward, wy_high, wy_low, wx, results)
 
 
 def shape(*dims, dtype=F32):
@@ -366,8 +389,9 @@
 VMEM = pl.BlockSpec(memory_space=pltpu.VMEM)
 
 
-def call(kernel, outs, vmem=24, ins=None, scratch=()):
-    extra = {} if ins is None else {"in_specs": ins}
+def call(kernel, outs, vmem=24, ins=None, scratch=(), **extra):
+    if ins is not None:
+        extra["in_specs"] = ins
     return pl.pallas_call(
         kernel,
         out_shape=outs,
@@ -446,7 +470,15 @@
     got_odd = send(strip_odd, row_odd)
     got_even = send(strip_even, row_even)
     inner, forward = call(last_inner_kernel, (row, row))(doses3, *covers, wy_high, wy_low, wx, pairs)
-    return call(final_kernel, (row, row))(got_even, got_odd, doses3, sens, inner, forward, wy_high, wy_low, wx)
+    results = {
+        "out_specs": (HBM, HBM),
+        "scratch": (pltpu.VMEM((1, SLOTS), F32), pltpu.VMEM((1, SLOTS), F32), pltpu.SemaphoreType.DMA((2,))),
+    }
+    common = (doses3, sens, inner, forward, wy_high, wy_low, wx)
+    edge = call(edge_kernel, (row, row), **results)(got_even, *common)
+    return call(final_kernel, (row, row), ins=[VMEM] * 9 + [HBM] * 2, input_output_aliases={9: 0, 10: 1}, **results)(
+        got_even, got_odd, *common, *edge
+    )
 
 
 def solution(mesh):

time: 30.9 us -> 31.1 us (level)
    pallas_call x1 -> x2, Pallas kernels: 1.09 us -> 1.13 us  [the longest x1 1.1 us: body(): call(final_kernel, (row, row), ins=[VMEM] * 9 + [HBM] * 2, input_output_a...]
where the time goes in v7:
time: 31.1 us; the launch traced here: 30.9 us
  Pallas kernels  13 us (42%)
  starting transfers between devices  13 us (42%)
  waiting for transfers between devices  4.03 us (13%)
  between operations  0.89 us (3%)
    ppermute x12, starting transfers between devices, send(): return lax.ppermute(value, AXES, table)  13 us
    ppermute x12, waiting for transfers between devices, send(): return lax.ppermute(value, AXES, table)  4.03 us
    pallas_call x1, Pallas kernels, body(): call(early_kernel, (cover, cover, shape(SLOTS, SLOTS), shape(2, 1, SLOTS)...  3.84 us
    pallas_call x1, Pallas kernels, body(): call(late_kernel, (cover, cover, weights, weights, shape(SIDE, SLOTS), sh...  2.14 us
    pallas_call x1, Pallas kernels, body(): call(first_update_kernel, (rows, rows, shape(1, 1, SLOTS), strip, strip))  1.28 us
    pallas_call x1, Pallas kernels, body(): inner = call(inner_kernel, rows)(doses3, *covers, *weighing)  1.17 us
    pallas_call x1, Pallas kernels, body(): call(final_kernel, (row, row), ins=[VMEM] * 9 + [HBM] * 2, input_output_a...  1.1 us
    pallas_call x1, Pallas kernels, body(): call(last_inner_kernel, (row, row))  0.96 us
  transfers between devices with their start and end apart: 12, of which 3 were waited for; matrix products, arithmetic and copies ran while one was open for 0% of the time, Pallas kernels for 26%

profile of v7, /device:TPU:97, one launch (start us, length us, event | category | flops | bytes accessed | tf_op | source)
XLA Modules:
  0.0 30.9 jit_solution(8931341350273946914)
XLA Ops:
  0.6 0.9 %shard_map.68.tile.own = f32[5,1,1024]{2,1,0:T(1,128)S(1)} custom-call(s32[4,1,1024]{2,1,0:T(1,128)} %boxes_in.1, s32[1,16]{1,0:T(1,128)} %counts_in.1, s32[1,16]{1,0:T(1,128)} %tails_in.1, f32[1,1024]{1,0:T(1,128)} %doses_in.1), custom_call_target="tpu_custom_call" | custom-call | tf_op jit(solution)/shard_map/pallas_call | solution.py:421
  1.5 2.4 %collective-permute-start.1 = (f32[5,1,1024]{2,1,0:T(1,128)S(1)}, f32[5,1,1024]{2,1,0:T(1,128)S(1)}, u32[]{:S(2)}, u32[]{:S(2)}) collective-permute-start(f32[5,1,1024]{2,1,0:T(1,128)S(1)} %shard_map.68.tile.own), channel_id=1, source_target_pairs={{0,16},{1,2},{2,1},{3,4},{4,3},{5,6},{6,5},{7,8},{8,7},{9,10},{10,... | collective-permute-start | bytes 61448 | tf_op jit(solution)/shard_map/ppermute | solution.py:409
  3.9 0.1 collective-permute-start
  4.0 3.8 %shard_map.69 = (bf16[128,1024]{1,0:T(8,128)(2,1)S(1)}, bf16[128,1024]{1,0:T(8,128)(2,1)S(1)}, f32[1024,1024]{1,0:T(8,128)S(1)}, f32[2,1,1024]{2,1,0:T(1,128)S(1)}) custom-call(f32[5,1,1024]{2,1,0:T(1,128)S(1)} %shard_map.68.tile.own, f32[512,512]{1,0:T(8,128)} %gain_in.1), custom_call_target="tpu_custom_call" | custom-call | tf_op jit(solution)/shard_map/pallas_call | solution.py:435
  7.9 0.0 collective-permute-done.1.got_odd
  7.9 0.0 collective-permute-done.got_even
  7.9 0.6 %shard_map.70 = (f32[5,1,1024]{2,1,0:T(1,128)S(1)}, f32[5,1,1024]{2,1,0:T(1,128)S(1)}, bf16[128,1024]{1,0:T(8,128)(2,1)S(1)}, bf16[128,1024]{1,0:T(8,128)(2,1)S(...) custom-call(f32[5,1,1024]{2,1,0:T(1,128)S(1)} %shard_map.68.tile.own, f32[5,1,1024]{2,1,0:T(1,128)S(1)} %collective-permute-done.got_even, ...), custom_call_target="tpu_custom_call" | custom-call | tf_op jit(solution)/shard_map/pallas_call | solution.py:448
  8.5 1.3 %collective-permute-start.2 = (f32[32,384]{1,0:T(8,128)S(1)}, f32[32,384]{1,0:T(8,128)S(1)}, u32[]{:S(2)}, u32[]{:S(2)}) collective-permute-start(f32[32,384]{1,0:T(8,128)S(1)} %get-tuple-element.34), channel_id=1, source_target_pairs={{0,16},{1,17},{2,18},{3,19},{4,20},{5,21},{6,22},{7,23},{8,24},{9,... | collective-permute-start | bytes 147464 | tf_op jit(solution)/shard_map/ppermute | solution.py:409
  9.8 1.3 %collective-permute-start.3 = (f32[32,384]{1,0:T(8,128)S(1)}, f32[32,384]{1,0:T(8,128)S(1)}, u32[]{:S(2)}, u32[]{:S(2)}) collective-permute-start(f32[32,384]{1,0:T(8,128)S(1)} %get-tuple-element.35), channel_id=1, source_target_pairs={{0,1},{1,0},{2,3},{3,2},{4,5},{5,4},{6,7},{7,6},{8,9},{9,8},{10,11... | collective-permute-start | bytes 147464 | tf_op jit(solution)/shard_map/ppermute | solution.py:409
  11.1 1.4 %collective-permute-start.5 = (f32[2,1,1024]{2,1,0:T(1,128)S(1)}, f32[2,1,1024]{2,1,0:T(1,128)S(1)}, u32[]{:S(2)}, u32[]{:S(2)}) collective-permute-start(f32[2,1,1024]{2,1,0:T(1,128)S(1)} %get-tuple-element.36.told), channel_id=1, source_target_pairs={{0,16},{1,2},{2,1},{3,4},{4,3},{5,6},{6,5},{7,8},{8,7},{9,10},{10,... | collective-permute-start | bytes 24584 | tf_op jit(solution)/shard_map/ppermute | solution.py:409
  12.5 0.0 collective-permute-start.4
  12.5 2.1 %shard_map.71 = (bf16[128,1024]{1,0:T(8,128)(2,1)S(1)}, bf16[128,1024]{1,0:T(8,128)(2,1)S(1)}, bf16[3,192,1024]{2,1,0:T(8,128)(2,1)S(1)}, bf16[3,192,1024]{2,1,0...) custom-call(f32[5,1,1024]{2,1,0:T(1,128)S(1)} %shard_map.68.tile.own, ...), custom_call_target="tpu_custom_call" | custom-call | tf_op jit(solution)/shard_map/pallas_call | solution.py:454
  14.6 1.1 %collective-permute-done.5.told_odd = f32[2,1,1024]{2,1,0:T(1,128)S(1)} collective-permute-done((f32[2,1,1024]{2,1,0:T(1,128)S(1)}, f32[2,1,1024]{2,1,0:T(1,128)S(1)}, u32[]{:S(2)}, u32[]{:S(2)}) %collective-permute-start.5) | collective-permute-done | bytes 8224 | tf_op jit(solution)/shard_map/ppermute | solution.py:409
  15.7 0.0 collective-permute-done.4.told_even
  15.7 0.0 collective-permute-done.2.got_even
  15.7 0.0 collective-permute-done.3.got_odd
  15.7 1.3 %shard_map.72 = (f32[3,1,1024]{2,1,0:T(1,128)S(1)}, f32[3,1,1024]{2,1,0:T(1,128)S(1)}, f32[1,1,1024]{2,1,0:T(1,128)S(1)}, f32[32,384]{1,0:T(8,128)S(1)}, f32[32,384]{1,0:T(8,128)S(1)}) custom-call(f32[32,384]{1,0:T(8,128)S(1)} %collective-permute-done.2.got_even, f32[32,384]{1,0:T(8,128)S(1)} %collective-permute-done.3.got_odd, ...), custom_call_target="tpu_custom_call" | custom-call | tf_op jit(solution)/shard_map/pallas_call | solution.py:459
  17.0 1.7 %collective-permute-start.6 = (f32[32,384]{1,0:T(8,128)S(1)}, f32[32,384]{1,0:T(8,128)S(1)}, u32[]{:S(2)}, u32[]{:S(2)}) collective-permute-start(f32[32,384]{1,0:T(8,128)S(1)} %get-tuple-element.50), channel_id=1, source_target_pairs={{0,16},{1,17},{2,18},{3,19},{4,20},{5,21},{6,22},{7,23},{8,24},{9,... | collective-permute-start | bytes 147464 | tf_op jit(solution)/shard_map/ppermute | solution.py:409
  18.7 0.1 collective-permute-start.7
  18.8 1.8 %collective-permute-start.9 = (f32[1,1,1024]{2,1,0:T(1,128)S(1)}, f32[1,1,1024]{2,1,0:T(1,128)S(1)}, u32[]{:S(2)}, u32[]{:S(2)}) collective-permute-start(f32[1,1,1024]{2,1,0:T(1,128)S(1)} %get-tuple-element.52.told), channel_id=1, source_target_pairs={{0,16},{1,2},{2,1},{3,4},{4,3},{5,6},{6,5},{7,8},{8,7},{9,10},{10,... | collective-permute-start | bytes 12296 | tf_op jit(solution)/shard_map/ppermute | solution.py:409
  20.6 0.0 collective-permute-start.8
  20.6 1.2 %shard_map.73.inner = f32[3,1,1024]{2,1,0:T(1,128)S(1)} custom-call(f32[3,1,1024]{2,1,0:T(1,128)S(1)} %get-tuple-element.53.doses, bf16[128,1024]{1,0:T(8,128)(2,1)S(1)} %get-tuple-element.39.px_left, bf16[128,1024]{1,0:T(8,128)(2,1)S(1)} %get-tuple-element.32.px, bf16[128,1024]{1,0:T(8,128)(2,1)S(1)} %get-tuple-element.40.px_right, ...), custom_call_target="tpu_custom_call" | custom-call | tf_op jit(solution)/shard_map/pallas_call | solution.py:466
  21.8 1.6 %collective-permute-done.9.told_odd = f32[1,1,1024]{2,1,0:T(1,128)S(1)} collective-permute-done((f32[1,1,1024]{2,1,0:T(1,128)S(1)}, f32[1,1,1024]{2,1,0:T(1,128)S(1)}, u32[]{:S(2)}, u32[]{:S(2)}) %collective-permute-start.9) | collective-permute-done | bytes 4128 | tf_op jit(solution)/shard_map/ppermute | solution.py:409
  23.4 0.0 collective-permute-done.8.told_even
  23.4 0.0 collective-permute-done.6.got_even
  23.4 0.0 collective-permute-done.7.got_odd
  23.4 1.0 %shard_map.74 = (f32[3,1,1024]{2,1,0:T(1,128)S(1)}, f32[32,256]{1,0:T(8,128)S(1)}, f32[32,256]{1,0:T(8,128)S(1)}) custom-call(f32[32,384]{1,0:T(8,128)S(1)} %collective-permute-done.6.got_even, f32[32,384]{1,0:T(8,128)S(1)} %collective-permute-done.7.got_odd, f32[1,1,1024]{2,1,0:T(1,128)S(1)} %get-tuple-element.52.told, ...), custom_call_target="tpu_custom_call" | custom-call | tf_op jit(solution)/shard_map/pallas_call | solution.py:467
  24.4 1.6 %collective-permute-start.10 = (f32[32,256]{1,0:T(8,128)S(1)}, f32[32,256]{1,0:T(8,128)S(1)}, u32[]{:S(2)}, u32[]{:S(2)}) collective-permute-start(f32[32,256]{1,0:T(8,128)S(1)} %get-tuple-element.55), channel_id=1, source_target_pairs={{0,16},{1,17},{2,18},{3,19},{4,20},{5,21},{6,22},{7,23},{8,24},{9,... | collective-permute-start | bytes 98312 | tf_op jit(solution)/shard_map/ppermute | solution.py:409
  26.0 1.3 %collective-permute-start.11 = (f32[32,256]{1,0:T(8,128)S(1)}, f32[32,256]{1,0:T(8,128)S(1)}, u32[]{:S(2)}, u32[]{:S(2)}) collective-permute-start(f32[32,256]{1,0:T(8,128)S(1)} %get-tuple-element.56), channel_id=1, source_target_pairs={{0,1},{1,0},{2,3},{3,2},{4,5},{5,4},{6,7},{7,6},{8,9},{9,8},{10,11... | collective-permute-start | bytes 98312 | tf_op jit(solution)/shard_map/ppermute | solution.py:409
  27.3 1.0 %shard_map.75 = (f32[1,1024]{1,0:T(1,128)S(1)}, f32[1,1024]{1,0:T(1,128)S(1)}) custom-call(f32[3,1,1024]{2,1,0:T(1,128)S(1)} %get-tuple-element.57.doses, bf16[128,1024]{1,0:T(8,128)(2,1)S(1)} %get-tuple-element.39.px_left, bf16[128,1024]{1,0:T(8,128)(2,1)S(1)} %get-tuple-element.32.px, bf16[128,1024]{1,0:T(8,128)(2,1)S(1)} %get-tuple-element.40.px_right, ...), custom_call_target="tpu_custom_call" | custom-call | tf_op jit(solution)/shard_map/pallas_call | solution.py:472
  28.3 0.0 collective-permute-done.10.got_even
  28.4 1.3 %collective-permute-done.11.got_odd = f32[32,256]{1,0:T(8,128)S(1)} collective-permute-done((f32[32,256]{1,0:T(8,128)S(1)}, f32[32,256]{1,0:T(8,128)S(1)}, u32[]{:S(2)}, u32[]{:S(2)}) %collective-permute-start.11) | collective-permute-done | bytes 32800 | tf_op jit(solution)/shard_map/ppermute | solution.py:409
  29.6 1.1 %shard_map.77 = (f32[1,1024]{1,0:T(1,128)}, f32[1,1024]{1,0:T(1,128)}) custom-call(f32[32,256]{1,0:T(8,128)S(1)} %collective-permute-done.10.got_even, f32[32,256]{1,0:T(8,128)S(1)} %collective-permute-done.11.got_odd, f32[3,1,1024]{2,1,0:T(1,128)S(1)} %get-tuple-element.57.doses, ...), custom_call_target="tpu_custom_call", output_to_operand_aliasing={{0}: (9, {}), {1}: (10, {})} | custom-call | tf_op jit(solution)/shard_map/pallas_call | solution.py:479
  (1 shorter events, 0.0 us)
Async XLA Ops:
  1.5 6.4 %collective-permute-start.1 = (f32[5,1,1024]{2,1,0:T(1,128)S(1)}, f32[5,1,1024]{2,1,0:T(1,128)S(1)}, u32[]{:S(2)}, u32[]{:S(2)}) collective-permute-start(f32[5,1,1024]{2,1,0:T(1,128)S(1)} %shard_map.68.tile.own), channel_id=1, source_target_pairs={{0,16},{1,2},{2,1},{3,4},{4,3},{5,6},{6,5},{7,8},{8,7},{9,10},{10,... | collective-permute-start | bytes 61448 | tf_op jit(solution)/shard_map/ppermute | solution.py:409
  3.9 4.0 %collective-permute-start = (f32[5,1,1024]{2,1,0:T(1,128)S(1)}, f32[5,1,1024]{2,1,0:T(1,128)S(1)}, u32[]{:S(2)}, u32[]{:S(2)}) collective-permute-start(f32[5,1,1024]{2,1,0:T(1,128)S(1)} %shard_map.68.tile.own), channel_id=1, source_target_pairs={{0,1},{1,0},{2,3},{3,2},{4,5},{5,4},{6,7},{7,6},{8,9},{9,8},{10,11... | collective-permute-start | bytes 61448 | tf_op jit(solution)/shard_map/ppermute | solution.py:409
  8.5 7.2 %collective-permute-start.2 = (f32[32,384]{1,0:T(8,128)S(1)}, f32[32,384]{1,0:T(8,128)S(1)}, u32[]{:S(2)}, u32[]{:S(2)}) collective-permute-start(f32[32,384]{1,0:T(8,128)S(1)} %get-tuple-element.34), channel_id=1, source_target_pairs={{0,16},{1,17},{2,18},{3,19},{4,20},{5,21},{6,22},{7,23},{8,24},{9,... | collective-permute-start | bytes 147464 | tf_op jit(solution)/shard_map/ppermute | solution.py:409
  9.8 5.9 %collective-permute-start.3 = (f32[32,384]{1,0:T(8,128)S(1)}, f32[32,384]{1,0:T(8,128)S(1)}, u32[]{:S(2)}, u32[]{:S(2)}) collective-permute-start(f32[32,384]{1,0:T(8,128)S(1)} %get-tuple-element.35), channel_id=1, source_target_pairs={{0,1},{1,0},{2,3},{3,2},{4,5},{5,4},{6,7},{7,6},{8,9},{9,8},{10,11... | collective-permute-start | bytes 147464 | tf_op jit(solution)/shard_map/ppermute | solution.py:409
  11.1 4.6 %collective-permute-start.5 = (f32[2,1,1024]{2,1,0:T(1,128)S(1)}, f32[2,1,1024]{2,1,0:T(1,128)S(1)}, u32[]{:S(2)}, u32[]{:S(2)}) collective-permute-start(f32[2,1,1024]{2,1,0:T(1,128)S(1)} %get-tuple-element.36.told), channel_id=1, source_target_pairs={{0,16},{1,2},{2,1},{3,4},{4,3},{5,6},{6,5},{7,8},{8,7},{9,10},{10,... | collective-permute-start | bytes 24584 | tf_op jit(solution)/shard_map/ppermute | solution.py:409
  12.5 3.2 %collective-permute-start.4 = (f32[2,1,1024]{2,1,0:T(1,128)S(1)}, f32[2,1,1024]{2,1,0:T(1,128)S(1)}, u32[]{:S(2)}, u32[]{:S(2)}) collective-permute-start(f32[2,1,1024]{2,1,0:T(1,128)S(1)} %get-tuple-element.36.told), channel_id=1, source_target_pairs={{0,1},{1,0},{2,3},{3,2},{4,5},{5,4},{6,7},{7,6},{8,9},{9,8},{10,11... | collective-permute-start | bytes 24584 | tf_op jit(solution)/shard_map/ppermute | solution.py:409
  17.0 6.4 %collective-permute-start.6 = (f32[32,384]{1,0:T(8,128)S(1)}, f32[32,384]{1,0:T(8,128)S(1)}, u32[]{:S(2)}, u32[]{:S(2)}) collective-permute-start(f32[32,384]{1,0:T(8,128)S(1)} %get-tuple-element.50), channel_id=1, source_target_pairs={{0,16},{1,17},{2,18},{3,19},{4,20},{5,21},{6,22},{7,23},{8,24},{9,... | collective-permute-start | bytes 147464 | tf_op jit(solution)/shard_map/ppermute | solution.py:409
  18.7 4.7 %collective-permute-start.7 = (f32[32,384]{1,0:T(8,128)S(1)}, f32[32,384]{1,0:T(8,128)S(1)}, u32[]{:S(2)}, u32[]{:S(2)}) collective-permute-start(f32[32,384]{1,0:T(8,128)S(1)} %get-tuple-element.51), channel_id=1, source_target_pairs={{0,1},{1,0},{2,3},{3,2},{4,5},{5,4},{6,7},{7,6},{8,9},{9,8},{10,11... | collective-permute-start | bytes 147464 | tf_op jit(solution)/shard_map/ppermute | solution.py:409
  18.8 4.6 %collective-permute-start.9 = (f32[1,1,1024]{2,1,0:T(1,128)S(1)}, f32[1,1,1024]{2,1,0:T(1,128)S(1)}, u32[]{:S(2)}, u32[]{:S(2)}) collective-permute-start(f32[1,1,1024]{2,1,0:T(1,128)S(1)} %get-tuple-element.52.told), channel_id=1, source_target_pairs={{0,16},{1,2},{2,1},{3,4},{4,3},{5,6},{6,5},{7,8},{8,7},{9,10},{10,... | collective-permute-start | bytes 12296 | tf_op jit(solution)/shard_map/ppermute | solution.py:409
  20.6 2.8 %collective-permute-start.8 = (f32[1,1,1024]{2,1,0:T(1,128)S(1)}, f32[1,1,1024]{2,1,0:T(1,128)S(1)}, u32[]{:S(2)}, u32[]{:S(2)}) collective-permute-start(f32[1,1,1024]{2,1,0:T(1,128)S(1)} %get-tuple-element.52.told), channel_id=1, source_target_pairs={{0,1},{1,0},{2,3},{3,2},{4,5},{5,4},{6,7},{7,6},{8,9},{9,8},{10,11... | collective-permute-start | bytes 12296 | tf_op jit(solution)/shard_map/ppermute | solution.py:409
  24.4 3.9 %collective-permute-start.10 = (f32[32,256]{1,0:T(8,128)S(1)}, f32[32,256]{1,0:T(8,128)S(1)}, u32[]{:S(2)}, u32[]{:S(2)}) collective-permute-start(f32[32,256]{1,0:T(8,128)S(1)} %get-tuple-element.55), channel_id=1, source_target_pairs={{0,16},{1,17},{2,18},{3,19},{4,20},{5,21},{6,22},{7,23},{8,24},{9,... | collective-permute-start | bytes 98312 | tf_op jit(solution)/shard_map/ppermute | solution.py:409
  26.0 3.6 %collective-permute-start.11 = (f32[32,256]{1,0:T(8,128)S(1)}, f32[32,256]{1,0:T(8,128)S(1)}, u32[]{:S(2)}, u32[]{:S(2)}) collective-permute-start(f32[32,256]{1,0:T(8,128)S(1)} %get-tuple-element.56), channel_id=1, source_target_pairs={{0,1},{1,0},{2,3},{3,2},{4,5},{5,4},{6,7},{7,6},{8,9},{9,8},{10,11... | collective-permute-start | bytes 98312 | tf_op jit(solution)/shard_map/ppermute | solution.py:409

commit v8 on v7

--- a/solution.py
+++ b/solution.py
@@ -26,6 +26,7 @@
 NT = (((1,), (1,)), ((), ()))
 MAXB = 8
 SIDE = CG + REACH
+PER_CELL = 1.0 / CELL**2
 ALL = CG + 2 * REACH
 MARGINS = (3 * REACH + 2 * 8, 2 * REACH + 8)
 
@@ -70,7 +71,7 @@
 def overlap(low_edge, high_edge, cells):
     begin = cells * CELL
     covered = jnp.minimum(high_edge, begin + CELL) - jnp.maximum(low_edge, begin)
-    return jnp.maximum(covered, 0.0) * (1.0 / CELL)
+    return jnp.maximum(covered, 0.0)
 
 
 def gauss(cells, places):
@@ -153,42 +154,55 @@
 def early_kernel(tile, gain_in, px_out, py_out, pairs, told, gain, gain_parts, picked, chosen_x, arrived):
     copy = pltpu.make_async_copy(gain_in, gain, arrived)
     copy.start()
-    boxes = boxes_of(tile)
-    pixel_x = (boxes[0] + boxes[2]) // 2
-    pixel_y = (boxes[1] + boxes[3]) // 2
-    for at in range(0, TILE, 16):
-        chosen_x[at : at + 16, :] = jnp.where(iota((16, SLOTS), 0) + at == pixel_x, 1.0, 0.0).astype(BF16)
     inverse = 1.0 / FORWARD_RANGE
     box = [tile[k] for k in range(4)]
+    pixel_x = jnp.floor((box[0] + box[2]) * 0.5)
+    pixel_y = jnp.floor((box[1] + box[3]) * 0.5)
     centre_x = jnp.broadcast_to((box[0] + box[2]) * (0.5 * inverse), (8, SLOTS))
     centre_y = jnp.broadcast_to((box[1] + box[3]) * (0.5 * inverse), (8, SLOTS))
-    columns = jnp.concatenate([b * inverse for b in box] + [tile[4], jnp.zeros((3, SLOTS), F32)], axis=0)
+    columns = jnp.concatenate([b * inverse for b in box] + [tile[4] * 0.25, jnp.zeros((3, SLOTS), F32)], axis=0)
     total = jnp.zeros((8, SLOTS), F32)
+    dot_at = (3, 4, 5, 6)
+
+    def find(part):
+        lanes = slice(part * 256, part * 256 + 256)
+        here = jnp.broadcast_to(pixel_y[:, lanes], (8, 256))
+        found = jnp.zeros((8, 256), F32)
+        for row in range(0, TILE, 8):
+            found += jnp.where((iota((8, 256), 0) + row).astype(F32) == here, picked[part, row : row + 8, :], 0.0)
+        told[1, :, lanes] = jnp.sum(found, axis=0, keepdims=True)
+
     for block in range(MAXB):
         at = block * BLK
-        if block == 3:
+        if block == dot_at[0]:
             copy.wait()
-            high, low = two_parts(gain[...])
-            gain_parts[...] = jnp.concatenate([high, low], axis=1)
-        if block >= 3 and block < 7:
-            lanes = slice((block - 3) * 256, (block - 2) * 256)
-            chosen = chosen_x[:, lanes]
-            picked[...] = jnp.dot(gain_parts[...], jnp.concatenate([chosen, chosen], axis=0), preferred_element_type=F32)
+            for first in range(0, TILE, 64):
+                high, low = two_parts(gain[first : first + 64, :])
+                gain_parts[first : first + 64, :] = jnp.concatenate([high, low], axis=1)
+        for part in range(4):
+            if block == dot_at[part]:
+                chosen = chosen_x[:, part * 256 : part * 256 + 256]
+                picked[part] = jnp.dot(gain_parts[...], jnp.concatenate([chosen, chosen], axis=0), preferred_element_type=F32)
         side = jnp.transpose(columns[:, at : at + BLK])
         for down in range(0, BLK, 8):
-            low_x, low_y, high_x, high_y, dose = [side[down : down + 8, k : k + 1] for k in range(5)]
+            rows = slice(down, down + 8)
+            low_x, low_y, high_x, high_y, dose = [side[rows, k : k + 1] for k in range(5)]
             along_x = lax.erf(centre_x - low_x) - lax.erf(centre_x - high_x)
             along_y = lax.erf(centre_y - low_y) - lax.erf(centre_y - high_y)
-            values = (0.25 * along_x) * along_y
+            values = along_x * along_y
             pairs[at + down : at + down + 8, :] = values
             total += dose * values
-        if block >= 3 and block < 7:
-            found = jnp.zeros((8, 256), F32)
-            for row in range(0, TILE, 8):
-                found += jnp.where(iota((8, 256), 0) + row == pixel_y[:, lanes], picked[row : row + 8, :], 0.0)
-            told[1, :, lanes] = jnp.sum(found, axis=0, keepdims=True)
-        if block < 3:
-            for first in range(block * 48, min(block * 48 + 48, CG), 16):
+        if block < dot_at[0]:
+            share = TILE // dot_at[0] // 16 * 16 + 16
+            for first in range(block * share, min(block * share + share, TILE), 16):
+                chosen_x[first : first + 16, :] = jnp.where(cells_from(first, 16) == pixel_x, 1.0, 0.0).astype(BF16)
+        for part in range(4):
+            if block == min(dot_at[part] + 1, MAXB - 1):
+                find(part)
+        if block >= dot_at[0]:
+            share = 32
+            begin = (block - dot_at[0]) * share
+            for first in range(begin, min(begin + share, CG), 16):
                 px_out[first : first + 16, :] = overlap(box[0], box[2], cells_from(first, 16)).astype(BF16)
                 py_out[first : first + 16, :] = overlap(box[1], box[3], cells_from(first, 16)).astype(BF16)
     told[0] = jnp.sum(total, axis=0, keepdims=True)
@@ -199,24 +213,24 @@
     left_out[...] = left
     right_out[...] = right
     edge_cells = jnp.concatenate([cells_from(0, REACH), cells_from(CG - REACH, REACH)], axis=0)
-    edges = [stacked_dot(edge_part(py) * own[4], px[...], NT)]
+    edges = [stacked_dot(edge_part(py) * (own[4] * PER_CELL), px[...], NT)]
     for tile, px_out in ((left, px_left), (right, px_right)):
         across = overlap(tile[0], tile[2], cells_from(0, CG)).astype(BF16)
         px_out[...] = across
-        edges.append(stacked_dot(overlap(tile[1], tile[3], edge_cells) * tile[4], across, NT))
+        edges.append(stacked_dot(overlap(tile[1], tile[3], edge_cells) * (tile[4] * PER_CELL), across, NT))
     send_rows(jnp.concatenate([edges[1], edges[0], edges[2]], axis=1), send_even, send_odd)
 
 
 def strips(doses, px, py, send_even, send_odd):
-    edges = [stacked_dot(edge_part(down) * dose, across[...], NT) for dose, across, down in zip(doses, px, py)]
+    edges = [stacked_dot(edge_part(down) * (dose * PER_CELL), across[...], NT) for dose, across, down in zip(doses, px, py)]
     send_rows(jnp.concatenate(edges, axis=1), send_even, send_odd)
 
 
 def last_strips(doses, px, py, send_even, send_odd):
     edges = [
-        stacked_dot(edge_part(py[1]) * doses[1], px[1][...], NT),
-        stacked_dot(edge_part(py[0]) * doses[0], px[0][CG - REACH :, :], NT),
-        stacked_dot(edge_part(py[2]) * doses[2], px[2][:REACH, :], NT),
+        stacked_dot(edge_part(py[1]) * (doses[1] * PER_CELL), px[1][...], NT),
+        stacked_dot(edge_part(py[0]) * (doses[0] * PER_CELL), px[0][CG - REACH :, :], NT),
+        stacked_dot(edge_part(py[2]) * (doses[2] * PER_CELL), px[2][:REACH, :], NT),
         jnp.zeros((2 * REACH, 2 * CG - ALL), F32),
     ]
     send_rows(jnp.concatenate(edges, axis=1), send_even, send_odd)
@@ -236,7 +250,7 @@
 
 
 def inner_sums(doses, px, py, wy_high, wy_low, wx, inner, margin):
-    coarse = [stacked_dot(across.astype(F32) * dose, down, NT) for dose, across, down in zip(doses, px, py)]
+    coarse = [stacked_dot(across.astype(F32) * (dose * PER_CELL), down, NT) for dose, across, down in zip(doses, px, py)]
     for k, (columns, along) in enumerate(zip(per_tile(*coarse, margin), weights_along(wx, margin))):
         across = weighted(columns, wy_high[k, :CG, :], wy_low[k, :CG, :])
         inner[k] = jnp.sum(across * along, axis=0, keepdims=True)
@@ -286,9 +300,9 @@
 def last_inner_kernel(doses, px_left, px, px_right, py_left, py, py_right, wy_high, wy_low, wx, pairs, inner, forward):
     coarse = jnp.concatenate(
         [
-            stacked_dot(px[...].astype(F32) * doses[1], py[...], NT),
-            stacked_dot(px_left[CG - REACH :, :].astype(F32) * doses[0], py_left[...], NT),
-            stacked_dot(px_right[:REACH, :].astype(F32) * doses[2], py_right[...], NT),
+            stacked_dot(px[...].astype(F32) * (doses[1] * PER_CELL), py[...], NT),
+            stacked_dot(px_left[CG - REACH :, :].astype(F32) * (doses[0] * PER_CELL), py_left[...], NT),
+            stacked_dot(px_right[:REACH, :].astype(F32) * (doses[2] * PER_CELL), py_right[...], NT),
         ],
         axis=0,
     )
@@ -298,7 +312,7 @@
 
 
 def pair_sum(dose, pairs):
-    columns = as_columns(dose)
+    columns = as_columns(dose * 0.25)
     total = jnp.zeros((8, SLOTS), F32)
     for k in range(MAXB):
         total += folded_sum(columns[:, k : k + 1] * pairs[k * BLK : (k + 1) * BLK, :])
@@ -439,7 +453,7 @@
         scratch=(
             pltpu.VMEM((TILE, TILE), F32),
             pltpu.VMEM((TILE, 2 * TILE), BF16),
-            pltpu.VMEM((TILE, 256), F32),
+            pltpu.VMEM((4, TILE, 256), F32),
             pltpu.VMEM((TILE, SLOTS), BF16),
             pltpu.SemaphoreType.DMA,
         ),

time: 31.1 us -> 30.8 us (level)
  no operation moved by 1% of the time
where the time goes in v8:
time: 30.8 us; the launch traced here: 30.6 us
  starting transfers between devices  13.1 us (43%)
  Pallas kernels  12.8 us (42%)
  waiting for transfers between devices  3.88 us (13%)
  between operations  0.73 us (2%)
    ppermute x12, starting transfers between devices, send(): return lax.ppermute(value, AXES, table)  13.1 us
    ppermute x12, waiting for transfers between devices, send(): return lax.ppermute(value, AXES, table)  3.88 us
    pallas_call x1, Pallas kernels, body(): call(early_kernel, (cover, cover, shape(SLOTS, SLOTS), shape(2, 1, SLOTS)...  3.71 us
    pallas_call x1, Pallas kernels, body(): call(late_kernel, (cover, cover, weights, weights, shape(SIDE, SLOTS), sh...  2.13 us
    pallas_call x1, Pallas kernels, body(): call(first_update_kernel, (rows, rows, shape(1, 1, SLOTS), strip, strip))  1.27 us
    pallas_call x1, Pallas kernels, body(): inner = call(inner_kernel, rows)(doses3, *covers, *weighing)  1.18 us
    pallas_call x1, Pallas kernels, body(): call(final_kernel, (row, row), ins=[VMEM] * 9 + [HBM] * 2, input_output_a...  1.1 us
    pallas_call x1, Pallas kernels, body(): call(last_inner_kernel, (row, row))  0.99 us
  transfers between devices with their start and end apart: 12, of which 3 were waited for; matrix products, arithmetic and copies ran while one was open for 0% of the time, Pallas kernels for 26%

profile of v8, /device:TPU:97, one launch (start us, length us, event | category | flops | bytes accessed | tf_op | source)
XLA Modules:
  0.0 30.6 jit_solution(16602450677443708959)
XLA Ops:
  0.6 0.9 %shard_map.68.tile.own = f32[5,1,1024]{2,1,0:T(1,128)S(1)} custom-call(s32[4,1,1024]{2,1,0:T(1,128)} %boxes_in.1, s32[1,16]{1,0:T(1,128)} %counts_in.1, s32[1,16]{1,0:T(1,128)} %tails_in.1, f32[1,1024]{1,0:T(1,128)} %doses_in.1), custom_call_target="tpu_custom_call" | custom-call | tf_op jit(solution)/shard_map/pallas_call | solution.py:435
  1.5 2.4 %collective-permute-start.1 = (f32[5,1,1024]{2,1,0:T(1,128)S(1)}, f32[5,1,1024]{2,1,0:T(1,128)S(1)}, u32[]{:S(2)}, u32[]{:S(2)}) collective-permute-start(f32[5,1,1024]{2,1,0:T(1,128)S(1)} %shard_map.68.tile.own), channel_id=1, source_target_pairs={{0,16},{1,2},{2,1},{3,4},{4,3},{5,6},{6,5},{7,8},{8,7},{9,10},{10,... | collective-permute-start | bytes 61448 | tf_op jit(solution)/shard_map/ppermute | solution.py:423
  3.9 0.1 collective-permute-start
  4.0 3.7 %shard_map.69 = (bf16[128,1024]{1,0:T(8,128)(2,1)S(1)}, bf16[128,1024]{1,0:T(8,128)(2,1)S(1)}, f32[1024,1024]{1,0:T(8,128)S(1)}, f32[2,1,1024]{2,1,0:T(1,128)S(1)}) custom-call(f32[5,1,1024]{2,1,0:T(1,128)S(1)} %shard_map.68.tile.own, f32[512,512]{1,0:T(8,128)} %gain_in.1), custom_call_target="tpu_custom_call" | custom-call | tf_op jit(solution)/shard_map/pallas_call | solution.py:449
  7.7 0.0 collective-permute-done.1.got_odd
  7.7 0.0 collective-permute-done.got_even
  7.7 0.6 %shard_map.70 = (f32[5,1,1024]{2,1,0:T(1,128)S(1)}, f32[5,1,1024]{2,1,0:T(1,128)S(1)}, bf16[128,1024]{1,0:T(8,128)(2,1)S(1)}, bf16[128,1024]{1,0:T(8,128)(2,1)S(...) custom-call(f32[5,1,1024]{2,1,0:T(1,128)S(1)} %shard_map.68.tile.own, f32[5,1,1024]{2,1,0:T(1,128)S(1)} %collective-permute-done.got_even, ...), custom_call_target="tpu_custom_call" | custom-call | tf_op jit(solution)/shard_map/pallas_call | solution.py:462
  8.4 1.3 %collective-permute-start.2 = (f32[32,384]{1,0:T(8,128)S(1)}, f32[32,384]{1,0:T(8,128)S(1)}, u32[]{:S(2)}, u32[]{:S(2)}) collective-permute-start(f32[32,384]{1,0:T(8,128)S(1)} %get-tuple-element.34), channel_id=1, source_target_pairs={{0,16},{1,17},{2,18},{3,19},{4,20},{5,21},{6,22},{7,23},{8,24},{9,... | collective-permute-start | bytes 147464 | tf_op jit(solution)/shard_map/ppermute | solution.py:423
  9.7 1.3 %collective-permute-start.3 = (f32[32,384]{1,0:T(8,128)S(1)}, f32[32,384]{1,0:T(8,128)S(1)}, u32[]{:S(2)}, u32[]{:S(2)}) collective-permute-start(f32[32,384]{1,0:T(8,128)S(1)} %get-tuple-element.35), channel_id=1, source_target_pairs={{0,1},{1,0},{2,3},{3,2},{4,5},{5,4},{6,7},{7,6},{8,9},{9,8},{10,11... | collective-permute-start | bytes 147464 | tf_op jit(solution)/shard_map/ppermute | solution.py:423
  10.9 1.5 %collective-permute-start.5 = (f32[2,1,1024]{2,1,0:T(1,128)S(1)}, f32[2,1,1024]{2,1,0:T(1,128)S(1)}, u32[]{:S(2)}, u32[]{:S(2)}) collective-permute-start(f32[2,1,1024]{2,1,0:T(1,128)S(1)} %get-tuple-element.36.told), channel_id=1, source_target_pairs={{0,16},{1,2},{2,1},{3,4},{4,3},{5,6},{6,5},{7,8},{8,7},{9,10},{10,... | collective-permute-start | bytes 24584 | tf_op jit(solution)/shard_map/ppermute | solution.py:423
  12.4 0.0 collective-permute-start.4
  12.4 2.1 %shard_map.71 = (bf16[128,1024]{1,0:T(8,128)(2,1)S(1)}, bf16[128,1024]{1,0:T(8,128)(2,1)S(1)}, bf16[3,192,1024]{2,1,0:T(8,128)(2,1)S(1)}, bf16[3,192,1024]{2,1,0...) custom-call(f32[5,1,1024]{2,1,0:T(1,128)S(1)} %shard_map.68.tile.own, ...), custom_call_target="tpu_custom_call" | custom-call | tf_op jit(solution)/shard_map/pallas_call | solution.py:468
  14.6 1.0 %collective-permute-done.5.told_odd = f32[2,1,1024]{2,1,0:T(1,128)S(1)} collective-permute-done((f32[2,1,1024]{2,1,0:T(1,128)S(1)}, f32[2,1,1024]{2,1,0:T(1,128)S(1)}, u32[]{:S(2)}, u32[]{:S(2)}) %collective-permute-start.5) | collective-permute-done | bytes 8224 | tf_op jit(solution)/shard_map/ppermute | solution.py:423
  15.6 0.0 collective-permute-done.4.told_even
  15.6 0.0 collective-permute-done.2.got_even
  15.6 0.0 collective-permute-done.3.got_odd
  15.6 1.3 %shard_map.72 = (f32[3,1,1024]{2,1,0:T(1,128)S(1)}, f32[3,1,1024]{2,1,0:T(1,128)S(1)}, f32[1,1,1024]{2,1,0:T(1,128)S(1)}, f32[32,384]{1,0:T(8,128)S(1)}, f32[32,384]{1,0:T(8,128)S(1)}) custom-call(f32[32,384]{1,0:T(8,128)S(1)} %collective-permute-done.2.got_even, f32[32,384]{1,0:T(8,128)S(1)} %collective-permute-done.3.got_odd, ...), custom_call_target="tpu_custom_call" | custom-call | tf_op jit(solution)/shard_map/pallas_call | solution.py:473
  16.9 1.7 %collective-permute-start.6 = (f32[32,384]{1,0:T(8,128)S(1)}, f32[32,384]{1,0:T(8,128)S(1)}, u32[]{:S(2)}, u32[]{:S(2)}) collective-permute-start(f32[32,384]{1,0:T(8,128)S(1)} %get-tuple-element.50), channel_id=1, source_target_pairs={{0,16},{1,17},{2,18},{3,19},{4,20},{5,21},{6,22},{7,23},{8,24},{9,... | collective-permute-start | bytes 147464 | tf_op jit(solution)/shard_map/ppermute | solution.py:423
  18.5 0.1 collective-permute-start.7
  18.7 1.8 %collective-permute-start.9 = (f32[1,1,1024]{2,1,0:T(1,128)S(1)}, f32[1,1,1024]{2,1,0:T(1,128)S(1)}, u32[]{:S(2)}, u32[]{:S(2)}) collective-permute-start(f32[1,1,1024]{2,1,0:T(1,128)S(1)} %get-tuple-element.52.told), channel_id=1, source_target_pairs={{0,16},{1,2},{2,1},{3,4},{4,3},{5,6},{6,5},{7,8},{8,7},{9,10},{10,... | collective-permute-start | bytes 12296 | tf_op jit(solution)/shard_map/ppermute | solution.py:423
  20.4 0.0 collective-permute-start.8
  20.4 1.2 %shard_map.73.inner = f32[3,1,1024]{2,1,0:T(1,128)S(1)} custom-call(f32[3,1,1024]{2,1,0:T(1,128)S(1)} %get-tuple-element.53.doses, bf16[128,1024]{1,0:T(8,128)(2,1)S(1)} %get-tuple-element.39.px_left, bf16[128,1024]{1,0:T(8,128)(2,1)S(1)} %get-tuple-element.32.px, bf16[128,1024]{1,0:T(8,128)(2,1)S(1)} %get-tuple-element.40.px_right, ...), custom_call_target="tpu_custom_call" | custom-call | tf_op jit(solution)/shard_map/pallas_call | solution.py:480
  21.6 1.6 %collective-permute-done.9.told_odd = f32[1,1,1024]{2,1,0:T(1,128)S(1)} collective-permute-done((f32[1,1,1024]{2,1,0:T(1,128)S(1)}, f32[1,1,1024]{2,1,0:T(1,128)S(1)}, u32[]{:S(2)}, u32[]{:S(2)}) %collective-permute-start.9) | collective-permute-done | bytes 4128 | tf_op jit(solution)/shard_map/ppermute | solution.py:423
  23.2 0.0 collective-permute-done.8.told_even
  23.2 0.0 collective-permute-done.6.got_even
  23.2 0.0 collective-permute-done.7.got_odd
  23.2 1.0 %shard_map.74 = (f32[3,1,1024]{2,1,0:T(1,128)S(1)}, f32[32,256]{1,0:T(8,128)S(1)}, f32[32,256]{1,0:T(8,128)S(1)}) custom-call(f32[32,384]{1,0:T(8,128)S(1)} %collective-permute-done.6.got_even, f32[32,384]{1,0:T(8,128)S(1)} %collective-permute-done.7.got_odd, f32[1,1,1024]{2,1,0:T(1,128)S(1)} %get-tuple-element.52.told, ...), custom_call_target="tpu_custom_call" | custom-call | tf_op jit(solution)/shard_map/pallas_call | solution.py:481
  24.2 1.6 %collective-permute-start.10 = (f32[32,256]{1,0:T(8,128)S(1)}, f32[32,256]{1,0:T(8,128)S(1)}, u32[]{:S(2)}, u32[]{:S(2)}) collective-permute-start(f32[32,256]{1,0:T(8,128)S(1)} %get-tuple-element.55), channel_id=1, source_target_pairs={{0,16},{1,17},{2,18},{3,19},{4,20},{5,21},{6,22},{7,23},{8,24},{9,... | collective-permute-start | bytes 98312 | tf_op jit(solution)/shard_map/ppermute | solution.py:423
  25.9 1.3 %collective-permute-start.11 = (f32[32,256]{1,0:T(8,128)S(1)}, f32[32,256]{1,0:T(8,128)S(1)}, u32[]{:S(2)}, u32[]{:S(2)}) collective-permute-start(f32[32,256]{1,0:T(8,128)S(1)} %get-tuple-element.56), channel_id=1, source_target_pairs={{0,1},{1,0},{2,3},{3,2},{4,5},{5,4},{6,7},{7,6},{8,9},{9,8},{10,11... | collective-permute-start | bytes 98312 | tf_op jit(solution)/shard_map/ppermute | solution.py:423
  27.2 1.0 %shard_map.75 = (f32[1,1024]{1,0:T(1,128)S(1)}, f32[1,1024]{1,0:T(1,128)S(1)}) custom-call(f32[3,1,1024]{2,1,0:T(1,128)S(1)} %get-tuple-element.57.doses, bf16[128,1024]{1,0:T(8,128)(2,1)S(1)} %get-tuple-element.39.px_left, bf16[128,1024]{1,0:T(8,128)(2,1)S(1)} %get-tuple-element.32.px, bf16[128,1024]{1,0:T(8,128)(2,1)S(1)} %get-tuple-element.40.px_right, ...), custom_call_target="tpu_custom_call" | custom-call | tf_op jit(solution)/shard_map/pallas_call | solution.py:486
  28.2 0.0 collective-permute-done.10.got_even
  28.2 1.3 %collective-permute-done.11.got_odd = f32[32,256]{1,0:T(8,128)S(1)} collective-permute-done((f32[32,256]{1,0:T(8,128)S(1)}, f32[32,256]{1,0:T(8,128)S(1)}, u32[]{:S(2)}, u32[]{:S(2)}) %collective-permute-start.11) | collective-permute-done | bytes 32800 | tf_op jit(solution)/shard_map/ppermute | solution.py:423
  29.5 1.1 %shard_map.77 = (f32[1,1024]{1,0:T(1,128)}, f32[1,1024]{1,0:T(1,128)}) custom-call(f32[32,256]{1,0:T(8,128)S(1)} %collective-permute-done.10.got_even, f32[32,256]{1,0:T(8,128)S(1)} %collective-permute-done.11.got_odd, f32[3,1,1024]{2,1,0:T(1,128)S(1)} %get-tuple-element.57.doses, ...), custom_call_target="tpu_custom_call", output_to_operand_aliasing={{0}: (9, {}), {1}: (10, {})} | custom-call | tf_op jit(solution)/shard_map/pallas_call | solution.py:493
  (1 shorter events, 0.0 us)
Async XLA Ops:
  1.5 6.2 %collective-permute-start.1 = (f32[5,1,1024]{2,1,0:T(1,128)S(1)}, f32[5,1,1024]{2,1,0:T(1,128)S(1)}, u32[]{:S(2)}, u32[]{:S(2)}) collective-permute-start(f32[5,1,1024]{2,1,0:T(1,128)S(1)} %shard_map.68.tile.own), channel_id=1, source_target_pairs={{0,16},{1,2},{2,1},{3,4},{4,3},{5,6},{6,5},{7,8},{8,7},{9,10},{10,... | collective-permute-start | bytes 61448 | tf_op jit(solution)/shard_map/ppermute | solution.py:423
  3.9 3.8 %collective-permute-start = (f32[5,1,1024]{2,1,0:T(1,128)S(1)}, f32[5,1,1024]{2,1,0:T(1,128)S(1)}, u32[]{:S(2)}, u32[]{:S(2)}) collective-permute-start(f32[5,1,1024]{2,1,0:T(1,128)S(1)} %shard_map.68.tile.own), channel_id=1, source_target_pairs={{0,1},{1,0},{2,3},{3,2},{4,5},{5,4},{6,7},{7,6},{8,9},{9,8},{10,11... | collective-permute-start | bytes 61448 | tf_op jit(solution)/shard_map/ppermute | solution.py:423
  8.4 7.2 %collective-permute-start.2 = (f32[32,384]{1,0:T(8,128)S(1)}, f32[32,384]{1,0:T(8,128)S(1)}, u32[]{:S(2)}, u32[]{:S(2)}) collective-permute-start(f32[32,384]{1,0:T(8,128)S(1)} %get-tuple-element.34), channel_id=1, source_target_pairs={{0,16},{1,17},{2,18},{3,19},{4,20},{5,21},{6,22},{7,23},{8,24},{9,... | collective-permute-start | bytes 147464 | tf_op jit(solution)/shard_map/ppermute | solution.py:423
  9.7 5.9 %collective-permute-start.3 = (f32[32,384]{1,0:T(8,128)S(1)}, f32[32,384]{1,0:T(8,128)S(1)}, u32[]{:S(2)}, u32[]{:S(2)}) collective-permute-start(f32[32,384]{1,0:T(8,128)S(1)} %get-tuple-element.35), channel_id=1, source_target_pairs={{0,1},{1,0},{2,3},{3,2},{4,5},{5,4},{6,7},{7,6},{8,9},{9,8},{10,11... | collective-permute-start | bytes 147464 | tf_op jit(solution)/shard_map/ppermute | solution.py:423
  10.9 4.6 %collective-permute-start.5 = (f32[2,1,1024]{2,1,0:T(1,128)S(1)}, f32[2,1,1024]{2,1,0:T(1,128)S(1)}, u32[]{:S(2)}, u32[]{:S(2)}) collective-permute-start(f32[2,1,1024]{2,1,0:T(1,128)S(1)} %get-tuple-element.36.told), channel_id=1, source_target_pairs={{0,16},{1,2},{2,1},{3,4},{4,3},{5,6},{6,5},{7,8},{8,7},{9,10},{10,... | collective-permute-start | bytes 24584 | tf_op jit(solution)/shard_map/ppermute | solution.py:423
  12.4 3.1 %collective-permute-start.4 = (f32[2,1,1024]{2,1,0:T(1,128)S(1)}, f32[2,1,1024]{2,1,0:T(1,128)S(1)}, u32[]{:S(2)}, u32[]{:S(2)}) collective-permute-start(f32[2,1,1024]{2,1,0:T(1,128)S(1)} %get-tuple-element.36.told), channel_id=1, source_target_pairs={{0,1},{1,0},{2,3},{3,2},{4,5},{5,4},{6,7},{7,6},{8,9},{9,8},{10,11... | collective-permute-start | bytes 24584 | tf_op jit(solution)/shard_map/ppermute | solution.py:423
  16.9 6.4 %collective-permute-start.6 = (f32[32,384]{1,0:T(8,128)S(1)}, f32[32,384]{1,0:T(8,128)S(1)}, u32[]{:S(2)}, u32[]{:S(2)}) collective-permute-start(f32[32,384]{1,0:T(8,128)S(1)} %get-tuple-element.50), channel_id=1, source_target_pairs={{0,16},{1,17},{2,18},{3,19},{4,20},{5,21},{6,22},{7,23},{8,24},{9,... | collective-permute-start | bytes 147464 | tf_op jit(solution)/shard_map/ppermute | solution.py:423
  18.5 4.7 %collective-permute-start.7 = (f32[32,384]{1,0:T(8,128)S(1)}, f32[32,384]{1,0:T(8,128)S(1)}, u32[]{:S(2)}, u32[]{:S(2)}) collective-permute-start(f32[32,384]{1,0:T(8,128)S(1)} %get-tuple-element.51), channel_id=1, source_target_pairs={{0,1},{1,0},{2,3},{3,2},{4,5},{5,4},{6,7},{7,6},{8,9},{9,8},{10,11... | collective-permute-start | bytes 147464 | tf_op jit(solution)/shard_map/ppermute | solution.py:423
  18.7 4.6 %collective-permute-start.9 = (f32[1,1,1024]{2,1,0:T(1,128)S(1)}, f32[1,1,1024]{2,1,0:T(1,128)S(1)}, u32[]{:S(2)}, u32[]{:S(2)}) collective-permute-start(f32[1,1,1024]{2,1,0:T(1,128)S(1)} %get-tuple-element.52.told), channel_id=1, source_target_pairs={{0,16},{1,2},{2,1},{3,4},{4,3},{5,6},{6,5},{7,8},{8,7},{9,10},{10,... | collective-permute-start | bytes 12296 | tf_op jit(solution)/shard_map/ppermute | solution.py:423
  20.4 2.8 %collective-permute-start.8 = (f32[1,1,1024]{2,1,0:T(1,128)S(1)}, f32[1,1,1024]{2,1,0:T(1,128)S(1)}, u32[]{:S(2)}, u32[]{:S(2)}) collective-permute-start(f32[1,1,1024]{2,1,0:T(1,128)S(1)} %get-tuple-element.52.told), channel_id=1, source_target_pairs={{0,1},{1,0},{2,3},{3,2},{4,5},{5,4},{6,7},{7,6},{8,9},{9,8},{10,11... | collective-permute-start | bytes 12296 | tf_op jit(solution)/shard_map/ppermute | solution.py:423
  24.2 3.9 %collective-permute-start.10 = (f32[32,256]{1,0:T(8,128)S(1)}, f32[32,256]{1,0:T(8,128)S(1)}, u32[]{:S(2)}, u32[]{:S(2)}) collective-permute-start(f32[32,256]{1,0:T(8,128)S(1)} %get-tuple-element.55), channel_id=1, source_target_pairs={{0,16},{1,17},{2,18},{3,19},{4,20},{5,21},{6,22},{7,23},{8,24},{9,... | collective-permute-start | bytes 98312 | tf_op jit(solution)/shard_map/ppermute | solution.py:423
  25.9 3.6 %collective-permute-start.11 = (f32[32,256]{1,0:T(8,128)S(1)}, f32[32,256]{1,0:T(8,128)S(1)}, u32[]{:S(2)}, u32[]{:S(2)}) collective-permute-start(f32[32,256]{1,0:T(8,128)S(1)} %get-tuple-element.56), channel_id=1, source_target_pairs={{0,1},{1,0},{2,3},{3,2},{4,5},{5,4},{6,7},{7,6},{8,9},{9,8},{10,11... | collective-permute-start | bytes 98312 | tf_op jit(solution)/shard_map/ppermute | solution.py:423

commit v9 on v8

--- a/solution.py
+++ b/solution.py
@@ -162,7 +162,7 @@
     centre_y = jnp.broadcast_to((box[1] + box[3]) * (0.5 * inverse), (8, SLOTS))
     columns = jnp.concatenate([b * inverse for b in box] + [tile[4] * 0.25, jnp.zeros((3, SLOTS), F32)], axis=0)
     total = jnp.zeros((8, SLOTS), F32)
-    dot_at = (3, 4, 5, 6)
+    dot_at = (4, 5, 6, 7)
 
     def find(part):
         lanes = slice(part * 256, part * 256 + 256)
@@ -231,9 +231,16 @@
         stacked_dot(edge_part(py[1]) * (doses[1] * PER_CELL), px[1][...], NT),
         stacked_dot(edge_part(py[0]) * (doses[0] * PER_CELL), px[0][CG - REACH :, :], NT),
         stacked_dot(edge_part(py[2]) * (doses[2] * PER_CELL), px[2][:REACH, :], NT),
-        jnp.zeros((2 * REACH, 2 * CG - ALL), F32),
     ]
-    send_rows(jnp.concatenate(edges, axis=1), send_even, send_odd)
+    beside = jnp.concatenate(edges[1:], axis=1)
+    half = REACH // 2
+    folded = [
+        jnp.concatenate([edges[0][at : at + REACH], jnp.concatenate([beside[at : at + half], beside[at + half : at + REACH]], axis=1)], axis=0)
+        for at in (0, REACH)
+    ]
+    even = is_even("row")
+    send_even[...] = jnp.where(even, folded[1], folded[0])
+    send_odd[...] = jnp.where(even, folded[0], folded[1])
 
 
 def per_tile(left, own, right, margin):
@@ -367,7 +374,10 @@
 def last_result(got_even, got_odd, doses, sens, inner, forward, wy_high, wy_low, wx, results):
     dose_out, exposure_out, dose, exposure, sent = results
     outer = outer_rows(got_even[...], got_odd[...])
-    columns = jnp.concatenate([jnp.transpose(outer[:, :CG]), jnp.transpose(outer[:, CG:])[: 2 * REACH]], axis=0)
+    each = REACH + REACH // 2
+    middle = jnp.concatenate([outer[:REACH], outer[each : each + REACH]], axis=0)
+    ends = [outer[at + REACH : at + each, side : side + 2 * REACH] for at in (0, each) for side in (0, 2 * REACH)]
+    columns = jnp.concatenate([jnp.transpose(middle), jnp.transpose(jnp.concatenate(ends, axis=0))], axis=0)
     across = weighted(columns, wy_high[1, CG:, :], wy_low[1, CG:, :])
     background = inner[...] + jnp.sum(across * wx[...], axis=0, keepdims=True)
     dose[...], exposure[...] = exposed(doses[1], sens[1], forward[...], background)
@@ -431,7 +441,7 @@
     tile = shape(5, 1, SLOTS)
     weights = shape(3, ALL, SLOTS, dtype=BF16)
     strip = shape(REACH, 3 * CG)
-    short = shape(REACH, 2 * CG)
+    short = shape(REACH + REACH // 2, CG)
     own = call(
         start_kernel,
         tile,

time: 30.8 us -> 30.7 us (level)
  no operation moved by 1% of the time
where the time goes in v9:
time: 30.7 us; the launch traced here: 30.5 us
  Pallas kernels  13 us (42%)
  starting transfers between devices  13 us (42%)
  waiting for transfers between devices  3.82 us (12%)
  between operations  0.73 us (2%)
    ppermute x12, starting transfers between devices, send(): return lax.ppermute(value, AXES, table)  13 us
    ppermute x12, waiting for transfers between devices, send(): return lax.ppermute(value, AXES, table)  3.82 us
    pallas_call x1, Pallas kernels, body(): call(early_kernel, (cover, cover, shape(SLOTS, SLOTS), shape(2, 1, SLOTS)...  3.75 us
    pallas_call x1, Pallas kernels, body(): call(late_kernel, (cover, cover, weights, weights, shape(SIDE, SLOTS), sh...  2.13 us
    pallas_call x1, Pallas kernels, body(): call(first_update_kernel, (rows, rows, shape(1, 1, SLOTS), strip, strip))  1.27 us
    pallas_call x1, Pallas kernels, body(): inner = call(inner_kernel, rows)(doses3, *covers, *weighing)  1.18 us
    pallas_call x1, Pallas kernels, body(): call(final_kernel, (row, row), ins=[VMEM] * 9 + [HBM] * 2, input_output_a...  1.12 us
    pallas_call x1, Pallas kernels, body(): call(update_kernel, (rows, short, short))  1.02 us
  transfers between devices with their start and end apart: 12, of which 3 were waited for; matrix products, arithmetic and copies ran while one was open for 0% of the time, Pallas kernels for 26%

profile of v9, /device:TPU:97, one launch (start us, length us, event | category | flops | bytes accessed | tf_op | source)
XLA Modules:
  0.0 30.5 jit_solution(9439511531805142792)
XLA Ops:
  0.6 0.9 %shard_map.68.tile.own = f32[5,1,1024]{2,1,0:T(1,128)S(1)} custom-call(s32[4,1,1024]{2,1,0:T(1,128)} %boxes_in.1, s32[1,16]{1,0:T(1,128)} %counts_in.1, s32[1,16]{1,0:T(1,128)} %tails_in.1, f32[1,1024]{1,0:T(1,128)} %doses_in.1), custom_call_target="tpu_custom_call" | custom-call | tf_op jit(solution)/shard_map/pallas_call | solution.py:445
  1.5 2.4 %collective-permute-start.1 = (f32[5,1,1024]{2,1,0:T(1,128)S(1)}, f32[5,1,1024]{2,1,0:T(1,128)S(1)}, u32[]{:S(2)}, u32[]{:S(2)}) collective-permute-start(f32[5,1,1024]{2,1,0:T(1,128)S(1)} %shard_map.68.tile.own), channel_id=1, source_target_pairs={{0,16},{1,2},{2,1},{3,4},{4,3},{5,6},{6,5},{7,8},{8,7},{9,10},{10,... | collective-permute-start | bytes 61448 | tf_op jit(solution)/shard_map/ppermute | solution.py:433
  3.9 0.1 collective-permute-start
  4.0 3.7 %shard_map.69 = (bf16[128,1024]{1,0:T(8,128)(2,1)S(1)}, bf16[128,1024]{1,0:T(8,128)(2,1)S(1)}, f32[1024,1024]{1,0:T(8,128)S(1)}, f32[2,1,1024]{2,1,0:T(1,128)S(1)}) custom-call(f32[5,1,1024]{2,1,0:T(1,128)S(1)} %shard_map.68.tile.own, f32[512,512]{1,0:T(8,128)} %gain_in.1), custom_call_target="tpu_custom_call" | custom-call | tf_op jit(solution)/shard_map/pallas_call | solution.py:459
  7.8 0.0 collective-permute-done.1.got_odd
  7.8 0.0 collective-permute-done.got_even
  7.8 0.6 %shard_map.70 = (f32[5,1,1024]{2,1,0:T(1,128)S(1)}, f32[5,1,1024]{2,1,0:T(1,128)S(1)}, bf16[128,1024]{1,0:T(8,128)(2,1)S(1)}, bf16[128,1024]{1,0:T(8,128)(2,1)S(...) custom-call(f32[5,1,1024]{2,1,0:T(1,128)S(1)} %shard_map.68.tile.own, f32[5,1,1024]{2,1,0:T(1,128)S(1)} %collective-permute-done.got_even, ...), custom_call_target="tpu_custom_call" | custom-call | tf_op jit(solution)/shard_map/pallas_call | solution.py:472
  8.4 1.3 %collective-permute-start.2 = (f32[32,384]{1,0:T(8,128)S(1)}, f32[32,384]{1,0:T(8,128)S(1)}, u32[]{:S(2)}, u32[]{:S(2)}) collective-permute-start(f32[32,384]{1,0:T(8,128)S(1)} %get-tuple-element.34), channel_id=1, source_target_pairs={{0,16},{1,17},{2,18},{3,19},{4,20},{5,21},{6,22},{7,23},{8,24},{9,... | collective-permute-start | bytes 147464 | tf_op jit(solution)/shard_map/ppermute | solution.py:433
  9.7 1.3 %collective-permute-start.3 = (f32[32,384]{1,0:T(8,128)S(1)}, f32[32,384]{1,0:T(8,128)S(1)}, u32[]{:S(2)}, u32[]{:S(2)}) collective-permute-start(f32[32,384]{1,0:T(8,128)S(1)} %get-tuple-element.35), channel_id=1, source_target_pairs={{0,1},{1,0},{2,3},{3,2},{4,5},{5,4},{6,7},{7,6},{8,9},{9,8},{10,11... | collective-permute-start | bytes 147464 | tf_op jit(solution)/shard_map/ppermute | solution.py:433
  11.0 1.5 %collective-permute-start.5 = (f32[2,1,1024]{2,1,0:T(1,128)S(1)}, f32[2,1,1024]{2,1,0:T(1,128)S(1)}, u32[]{:S(2)}, u32[]{:S(2)}) collective-permute-start(f32[2,1,1024]{2,1,0:T(1,128)S(1)} %get-tuple-element.36.told), channel_id=1, source_target_pairs={{0,16},{1,2},{2,1},{3,4},{4,3},{5,6},{6,5},{7,8},{8,7},{9,10},{10,... | collective-permute-start | bytes 24584 | tf_op jit(solution)/shard_map/ppermute | solution.py:433
  12.4 0.0 collective-permute-start.4
  12.4 2.1 %shard_map.71 = (bf16[128,1024]{1,0:T(8,128)(2,1)S(1)}, bf16[128,1024]{1,0:T(8,128)(2,1)S(1)}, bf16[3,192,1024]{2,1,0:T(8,128)(2,1)S(1)}, bf16[3,192,1024]{2,1,0...) custom-call(f32[5,1,1024]{2,1,0:T(1,128)S(1)} %shard_map.68.tile.own, ...), custom_call_target="tpu_custom_call" | custom-call | tf_op jit(solution)/shard_map/pallas_call | solution.py:478
  14.6 1.0 %collective-permute-done.5.told_odd = f32[2,1,1024]{2,1,0:T(1,128)S(1)} collective-permute-done((f32[2,1,1024]{2,1,0:T(1,128)S(1)}, f32[2,1,1024]{2,1,0:T(1,128)S(1)}, u32[]{:S(2)}, u32[]{:S(2)}) %collective-permute-start.5) | collective-permute-done | bytes 8224 | tf_op jit(solution)/shard_map/ppermute | solution.py:433
  15.6 0.0 collective-permute-done.4.told_even
  15.6 0.0 collective-permute-done.2.got_even
  15.6 0.0 collective-permute-done.3.got_odd
  15.6 1.3 %shard_map.72 = (f32[3,1,1024]{2,1,0:T(1,128)S(1)}, f32[3,1,1024]{2,1,0:T(1,128)S(1)}, f32[1,1,1024]{2,1,0:T(1,128)S(1)}, f32[32,384]{1,0:T(8,128)S(1)}, f32[32,384]{1,0:T(8,128)S(1)}) custom-call(f32[32,384]{1,0:T(8,128)S(1)} %collective-permute-done.2.got_even, f32[32,384]{1,0:T(8,128)S(1)} %collective-permute-done.3.got_odd, ...), custom_call_target="tpu_custom_call" | custom-call | tf_op jit(solution)/shard_map/pallas_call | solution.py:483
  16.9 1.7 %collective-permute-start.6 = (f32[32,384]{1,0:T(8,128)S(1)}, f32[32,384]{1,0:T(8,128)S(1)}, u32[]{:S(2)}, u32[]{:S(2)}) collective-permute-start(f32[32,384]{1,0:T(8,128)S(1)} %get-tuple-element.50), channel_id=1, source_target_pairs={{0,16},{1,17},{2,18},{3,19},{4,20},{5,21},{6,22},{7,23},{8,24},{9,... | collective-permute-start | bytes 147464 | tf_op jit(solution)/shard_map/ppermute | solution.py:433
  18.6 0.1 collective-permute-start.7
  18.7 1.8 %collective-permute-start.9 = (f32[1,1,1024]{2,1,0:T(1,128)S(1)}, f32[1,1,1024]{2,1,0:T(1,128)S(1)}, u32[]{:S(2)}, u32[]{:S(2)}) collective-permute-start(f32[1,1,1024]{2,1,0:T(1,128)S(1)} %get-tuple-element.52.told), channel_id=1, source_target_pairs={{0,16},{1,2},{2,1},{3,4},{4,3},{5,6},{6,5},{7,8},{8,7},{9,10},{10,... | collective-permute-start | bytes 12296 | tf_op jit(solution)/shard_map/ppermute | solution.py:433
  20.5 0.0 collective-permute-start.8
  20.5 1.2 %shard_map.73.inner = f32[3,1,1024]{2,1,0:T(1,128)S(1)} custom-call(f32[3,1,1024]{2,1,0:T(1,128)S(1)} %get-tuple-element.53.doses, bf16[128,1024]{1,0:T(8,128)(2,1)S(1)} %get-tuple-element.39.px_left, bf16[128,1024]{1,0:T(8,128)(2,1)S(1)} %get-tuple-element.32.px, bf16[128,1024]{1,0:T(8,128)(2,1)S(1)} %get-tuple-element.40.px_right, ...), custom_call_target="tpu_custom_call" | custom-call | tf_op jit(solution)/shard_map/pallas_call | solution.py:490
  21.6 1.6 %collective-permute-done.9.told_odd = f32[1,1,1024]{2,1,0:T(1,128)S(1)} collective-permute-done((f32[1,1,1024]{2,1,0:T(1,128)S(1)}, f32[1,1,1024]{2,1,0:T(1,128)S(1)}, u32[]{:S(2)}, u32[]{:S(2)}) %collective-permute-start.9) | collective-permute-done | bytes 4128 | tf_op jit(solution)/shard_map/ppermute | solution.py:433
  23.3 0.0 collective-permute-done.8.told_even
  23.3 0.0 collective-permute-done.6.got_even
  23.3 0.0 collective-permute-done.7.got_odd
  23.3 1.0 %shard_map.74 = (f32[3,1,1024]{2,1,0:T(1,128)S(1)}, f32[48,128]{1,0:T(8,128)S(1)}, f32[48,128]{1,0:T(8,128)S(1)}) custom-call(f32[32,384]{1,0:T(8,128)S(1)} %collective-permute-done.6.got_even, f32[32,384]{1,0:T(8,128)S(1)} %collective-permute-done.7.got_odd, f32[1,1,1024]{2,1,0:T(1,128)S(1)} %get-tuple-element.52.told, ...), custom_call_target="tpu_custom_call" | custom-call | tf_op jit(solution)/shard_map/pallas_call | solution.py:491
  24.3 1.6 %collective-permute-start.10 = (f32[48,128]{1,0:T(8,128)S(1)}, f32[48,128]{1,0:T(8,128)S(1)}, u32[]{:S(2)}, u32[]{:S(2)}) collective-permute-start(f32[48,128]{1,0:T(8,128)S(1)} %get-tuple-element.55), channel_id=1, source_target_pairs={{0,16},{1,17},{2,18},{3,19},{4,20},{5,21},{6,22},{7,23},{8,24},{9,... | collective-permute-start | bytes 73736 | tf_op jit(solution)/shard_map/ppermute | solution.py:433
  25.9 1.3 %collective-permute-start.11 = (f32[48,128]{1,0:T(8,128)S(1)}, f32[48,128]{1,0:T(8,128)S(1)}, u32[]{:S(2)}, u32[]{:S(2)}) collective-permute-start(f32[48,128]{1,0:T(8,128)S(1)} %get-tuple-element.56), channel_id=1, source_target_pairs={{0,1},{1,0},{2,3},{3,2},{4,5},{5,4},{6,7},{7,6},{8,9},{9,8},{10,11... | collective-permute-start | bytes 73736 | tf_op jit(solution)/shard_map/ppermute | solution.py:433
  27.2 1.0 %shard_map.75 = (f32[1,1024]{1,0:T(1,128)S(1)}, f32[1,1024]{1,0:T(1,128)S(1)}) custom-call(f32[3,1,1024]{2,1,0:T(1,128)S(1)} %get-tuple-element.57.doses, bf16[128,1024]{1,0:T(8,128)(2,1)S(1)} %get-tuple-element.39.px_left, bf16[128,1024]{1,0:T(8,128)(2,1)S(1)} %get-tuple-element.32.px, bf16[128,1024]{1,0:T(8,128)(2,1)S(1)} %get-tuple-element.40.px_right, ...), custom_call_target="tpu_custom_call" | custom-call | tf_op jit(solution)/shard_map/pallas_call | solution.py:496
  28.2 0.0 collective-permute-done.10.got_even
  28.2 1.2 %collective-permute-done.11.got_odd = f32[48,128]{1,0:T(8,128)S(1)} collective-permute-done((f32[48,128]{1,0:T(8,128)S(1)}, f32[48,128]{1,0:T(8,128)S(1)}, u32[]{:S(2)}, u32[]{:S(2)}) %collective-permute-start.11) | collective-permute-done | bytes 24608 | tf_op jit(solution)/shard_map/ppermute | solution.py:433
  29.4 1.1 %shard_map.77 = (f32[1,1024]{1,0:T(1,128)}, f32[1,1024]{1,0:T(1,128)}) custom-call(f32[48,128]{1,0:T(8,128)S(1)} %collective-permute-done.10.got_even, f32[48,128]{1,0:T(8,128)S(1)} %collective-permute-done.11.got_odd, f32[3,1,1024]{2,1,0:T(1,128)S(1)} %get-tuple-element.57.doses, ...), custom_call_target="tpu_custom_call", output_to_operand_aliasing={{0}: (9, {}), {1}: (10, {})} | custom-call | tf_op jit(solution)/shard_map/pallas_call | solution.py:503
  (1 shorter events, 0.0 us)
Async XLA Ops:
  1.5 6.3 %collective-permute-start.1 = (f32[5,1,1024]{2,1,0:T(1,128)S(1)}, f32[5,1,1024]{2,1,0:T(1,128)S(1)}, u32[]{:S(2)}, u32[]{:S(2)}) collective-permute-start(f32[5,1,1024]{2,1,0:T(1,128)S(1)} %shard_map.68.tile.own), channel_id=1, source_target_pairs={{0,16},{1,2},{2,1},{3,4},{4,3},{5,6},{6,5},{7,8},{8,7},{9,10},{10,... | collective-permute-start | bytes 61448 | tf_op jit(solution)/shard_map/ppermute | solution.py:433
  3.9 3.9 %collective-permute-start = (f32[5,1,1024]{2,1,0:T(1,128)S(1)}, f32[5,1,1024]{2,1,0:T(1,128)S(1)}, u32[]{:S(2)}, u32[]{:S(2)}) collective-permute-start(f32[5,1,1024]{2,1,0:T(1,128)S(1)} %shard_map.68.tile.own), channel_id=1, source_target_pairs={{0,1},{1,0},{2,3},{3,2},{4,5},{5,4},{6,7},{7,6},{8,9},{9,8},{10,11... | collective-permute-start | bytes 61448 | tf_op jit(solution)/shard_map/ppermute | solution.py:433
  8.4 7.2 %collective-permute-start.2 = (f32[32,384]{1,0:T(8,128)S(1)}, f32[32,384]{1,0:T(8,128)S(1)}, u32[]{:S(2)}, u32[]{:S(2)}) collective-permute-start(f32[32,384]{1,0:T(8,128)S(1)} %get-tuple-element.34), channel_id=1, source_target_pairs={{0,16},{1,17},{2,18},{3,19},{4,20},{5,21},{6,22},{7,23},{8,24},{9,... | collective-permute-start | bytes 147464 | tf_op jit(solution)/shard_map/ppermute | solution.py:433
  9.7 5.9 %collective-permute-start.3 = (f32[32,384]{1,0:T(8,128)S(1)}, f32[32,384]{1,0:T(8,128)S(1)}, u32[]{:S(2)}, u32[]{:S(2)}) collective-permute-start(f32[32,384]{1,0:T(8,128)S(1)} %get-tuple-element.35), channel_id=1, source_target_pairs={{0,1},{1,0},{2,3},{3,2},{4,5},{5,4},{6,7},{7,6},{8,9},{9,8},{10,11... | collective-permute-start | bytes 147464 | tf_op jit(solution)/shard_map/ppermute | solution.py:433
  11.0 4.6 %collective-permute-start.5 = (f32[2,1,1024]{2,1,0:T(1,128)S(1)}, f32[2,1,1024]{2,1,0:T(1,128)S(1)}, u32[]{:S(2)}, u32[]{:S(2)}) collective-permute-start(f32[2,1,1024]{2,1,0:T(1,128)S(1)} %get-tuple-element.36.told), channel_id=1, source_target_pairs={{0,16},{1,2},{2,1},{3,4},{4,3},{5,6},{6,5},{7,8},{8,7},{9,10},{10,... | collective-permute-start | bytes 24584 | tf_op jit(solution)/shard_map/ppermute | solution.py:433
  12.4 3.2 %collective-permute-start.4 = (f32[2,1,1024]{2,1,0:T(1,128)S(1)}, f32[2,1,1024]{2,1,0:T(1,128)S(1)}, u32[]{:S(2)}, u32[]{:S(2)}) collective-permute-start(f32[2,1,1024]{2,1,0:T(1,128)S(1)} %get-tuple-element.36.told), channel_id=1, source_target_pairs={{0,1},{1,0},{2,3},{3,2},{4,5},{5,4},{6,7},{7,6},{8,9},{9,8},{10,11... | collective-permute-start | bytes 24584 | tf_op jit(solution)/shard_map/ppermute | solution.py:433
  16.9 6.4 %collective-permute-start.6 = (f32[32,384]{1,0:T(8,128)S(1)}, f32[32,384]{1,0:T(8,128)S(1)}, u32[]{:S(2)}, u32[]{:S(2)}) collective-permute-start(f32[32,384]{1,0:T(8,128)S(1)} %get-tuple-element.50), channel_id=1, source_target_pairs={{0,16},{1,17},{2,18},{3,19},{4,20},{5,21},{6,22},{7,23},{8,24},{9,... | collective-permute-start | bytes 147464 | tf_op jit(solution)/shard_map/ppermute | solution.py:433
  18.6 4.7 %collective-permute-start.7 = (f32[32,384]{1,0:T(8,128)S(1)}, f32[32,384]{1,0:T(8,128)S(1)}, u32[]{:S(2)}, u32[]{:S(2)}) collective-permute-start(f32[32,384]{1,0:T(8,128)S(1)} %get-tuple-element.51), channel_id=1, source_target_pairs={{0,1},{1,0},{2,3},{3,2},{4,5},{5,4},{6,7},{7,6},{8,9},{9,8},{10,11... | collective-permute-start | bytes 147464 | tf_op jit(solution)/shard_map/ppermute | solution.py:433
  18.7 4.6 %collective-permute-start.9 = (f32[1,1,1024]{2,1,0:T(1,128)S(1)}, f32[1,1,1024]{2,1,0:T(1,128)S(1)}, u32[]{:S(2)}, u32[]{:S(2)}) collective-permute-start(f32[1,1,1024]{2,1,0:T(1,128)S(1)} %get-tuple-element.52.told), channel_id=1, source_target_pairs={{0,16},{1,2},{2,1},{3,4},{4,3},{5,6},{6,5},{7,8},{8,7},{9,10},{10,... | collective-permute-start | bytes 12296 | tf_op jit(solution)/shard_map/ppermute | solution.py:433
  20.5 2.8 %collective-permute-start.8 = (f32[1,1,1024]{2,1,0:T(1,128)S(1)}, f32[1,1,1024]{2,1,0:T(1,128)S(1)}, u32[]{:S(2)}, u32[]{:S(2)}) collective-permute-start(f32[1,1,1024]{2,1,0:T(1,128)S(1)} %get-tuple-element.52.told), channel_id=1, source_target_pairs={{0,1},{1,0},{2,3},{3,2},{4,5},{5,4},{6,7},{7,6},{8,9},{9,8},{10,11... | collective-permute-start | bytes 12296 | tf_op jit(solution)/shard_map/ppermute | solution.py:433
  24.3 3.9 %collective-permute-start.10 = (f32[48,128]{1,0:T(8,128)S(1)}, f32[48,128]{1,0:T(8,128)S(1)}, u32[]{:S(2)}, u32[]{:S(2)}) collective-permute-start(f32[48,128]{1,0:T(8,128)S(1)} %get-tuple-element.55), channel_id=1, source_target_pairs={{0,16},{1,17},{2,18},{3,19},{4,20},{5,21},{6,22},{7,23},{8,24},{9,... | collective-permute-start | bytes 73736 | tf_op jit(solution)/shard_map/ppermute | solution.py:433
  25.9 3.5 %collective-permute-start.11 = (f32[48,128]{1,0:T(8,128)S(1)}, f32[48,128]{1,0:T(8,128)S(1)}, u32[]{:S(2)}, u32[]{:S(2)}) collective-permute-start(f32[48,128]{1,0:T(8,128)S(1)} %get-tuple-element.56), channel_id=1, source_target_pairs={{0,1},{1,0},{2,3},{3,2},{4,5},{5,4},{6,7},{7,6},{8,9},{9,8},{10,11... | collective-permute-start | bytes 73736 | tf_op jit(solution)/shard_map/ppermute | solution.py:433
